TPU v7x, 32 devices: a whole 2x2x4 slice. The times are simulated.
32 devices in a mesh: mem: 2 (over y), gx: 4 (over x, core), gy: 4 (over z).
Axes of the slice: x: 2, y: 2, z: 4, core: 2. Of those that a mesh axis runs over, the one named last changes fastest.
Arguments:
- alpha: float32 [128, 2, 8, 16, 512], P('mem', None, None, 'gy', 'gx'), may hold values from -6 to 6
- static_control: float32 [2, 8, 16, 512], P(None, None, 'gy', 'gx'), may hold values from -6 to 6
- perturbations: bfloat16 [128, 2, 8, 16, 512], P('mem', None, None, 'gy', 'gx'), may hold values from -6 to 6
- sigma: float32 [2, 8, 16, 512], P(None, None, 'gy', 'gx'), may hold values from 0.5 to 2
- obs_coef: float32 [2, 8, 16384], P(None, None, ('gx', 'gy')), may hold values from -1.5 to 1.5
- interp_weights: float32 [4, 16384], P(None, ('gx', 'gy')), may hold values from 0.1 to 0.9
- obs_values: float32 [16384], P(('gx', 'gy')), may hold values from -6 to 6
- obs_weights: float32 [16384], P(('gx', 'gy')), may hold values from 0.5 to 4
- obs_tile: int32 [16384, 1], P(('gx', 'gy')), may hold values from 0 to 15; in each aligned block of 1024 rows (0 to 1023, 1024 to 2047, ...) at most 128 rows name the same one
- obs_cell: int32 [16384], P(('gx', 'gy')), may hold values from 0 to 2047
Outputs:
- alpha_out: float32 [128, 2, 8, 16, 512], P('mem', None, None, 'gy', 'gx')
- static_out: float32 [2, 8, 16, 512], P(None, None, 'gy', 'gx')
- increment: float32 [2, 8, 16, 512], P(None, None, 'gy', 'gx')
Inputs may be any that keep to these rules, and one draw needn't show every extreme that they name: `obs_tile`: within the rows of one device no tile is named more than 128 times; in some devices' rows a tile is named exactly 128 times.
All inputs are finite; a program needn't handle non-finite values.
Results may differ from a plain program's by a relative error of at most 0.0003.
Values sent between devices are 32-bit elements; how exact they have to be, the bound alone decides.
No kernel may reach another device: no remote copies, remote signals or barrier semaphores. Data moves between devices by JAX's collectives and lax.ppermute only.
A program may use at most 128 MiB of HBM per device.

v0:
```python
import functools
import math

import jax
import jax.numpy as jnp
import numpy as np
from jax import lax
from jax.experimental import pallas as pl
from jax.experimental.pallas import tpu as pltpu
from jax.sharding import PartitionSpec as P


F32, BF16 = jnp.float32, jnp.bfloat16

ens_share = 0.8660254037844386
static_share = 0.5
descent = 0.2
PASS = 20.0**4
LANES = 128
EDGE = 16
SLOT = 2 * EDGE
SLOTS = LANES // SLOT
VMEM_CAP = 28 * 2**20


def four_passes(inside):
    count = len(inside)
    step = np.zeros((count, count))
    for i in range(count):
        for j in range(count):
            if inside[i] and inside[j]:
                step[i, j] = 2.0 if i == j else (9.0 if abs(i - j) == 1 else 0.0)
    return np.linalg.matrix_power(step, 4)


def lat_table(lat, parts):
    rows = []
    for part in range(parts):
        placed = part * lat + np.arange(-4, lat + 4)
        full = four_passes((placed >= 0) & (placed < lat * parts))
        rows.append(full[:, 4 : 4 + lat])
    return np.stack(rows).astype(np.float32)


def lon_table(lon, parts):
    kinds = []
    order = np.concatenate(
        [EDGE + np.arange(lon), np.tile(np.concatenate([np.arange(EDGE), EDGE + lon + np.arange(EDGE)]), SLOTS)]
    )
    for part in (0, 1, parts - 1) if parts > 2 else range(parts):
        placed = part * lon + np.arange(-EDGE, lon + EDGE)
        full = four_passes((placed >= 0) & (placed < lon * parts))
        kinds.append(full[np.ix_(order, order)])
    return np.stack(kinds)


def split(value):
    high = value.astype(BF16)
    return high, (value - high.astype(F32)).astype(BF16)


def dot(a, b, dims=(((1,), (0,)), ((), ()))):
    return lax.dot_general(a, b, dims, preferred_element_type=F32)


def dot3(high, low, weights_high, weights_low):
    return dot(high, weights_high) + dot(low, weights_high) + dot(high, weights_low)


def lane_of(shape):
    return lax.broadcasted_iota(jnp.int32, shape, len(shape) - 1)


def vmem():
    return pl.BlockSpec(memory_space=pltpu.VMEM)


def smem():
    return pl.BlockSpec(memory_space=pltpu.SMEM)


def call(body, out_shape, flops=0, nbytes=0, **kw):
    return pl.pallas_call(
        body,
        out_shape=out_shape,
        cost_estimate=pl.CostEstimate(flops=int(flops), bytes_accessed=int(nbytes), transcendentals=0),
        compiler_params=pltpu.CompilerParams(vmem_limit_bytes=VMEM_CAP),
        **kw,
    )


def slot_of(shape):
    return lane_of(shape) // SLOT


def repeat_slots(x):
    x = x + pltpu.roll(x, 2 * SLOT, 1)
    return x + pltpu.roll(x, SLOT, 1)


def edges(pieces):
    total = None
    for j, piece in enumerate(pieces):
        moved = pltpu.roll(piece, (EDGE + SLOT * j) % LANES, 1)
        total = moved if total is None else jnp.where(slot_of(moved.shape) == j, moved, total)
    return total


def beside(from_left, from_right):
    return jnp.where(lane_of(from_left.shape) % SLOT < EDGE, from_left, from_right)


def narrow(x):
    half = x.shape[0] // 2
    return jnp.where(slot_of((half, LANES)) < SLOTS // 2, x[:half], x[half:])


def widen(x):
    other = pltpu.roll(x, LANES // 2, 1)
    low = slot_of(x.shape) < SLOTS // 2
    return jnp.concatenate([jnp.where(low, x, other), jnp.where(low, other, x)], 0)


def pick_slots(wide, rows):
    total = wide[:rows]
    slot = slot_of(total.shape)
    for j in range(1, SLOTS):
        total = jnp.where(slot == j, wide[j * rows : (j + 1) * rows], total)
    return total


def near(l12, l4):
    return abs(l12 - 4 - l4) <= 4


def forward_rows(lat_ref, z_of, p_of, lats, which=None):
    z = [z_of(l) for l in range(lats)]
    out = []
    for l12 in range(lats + 8) if which is None else which:
        total = None
        for l in range(lats):
            if near(l12, l):
                term = lat_ref[l12 * lats + l] * z[l]
                total = term if total is None else total + term
        out.append(p_of(l12) * total)
    return out


def adjoint_rows(lat_ref, p_of, g_of, lats):
    out = [None] * lats
    for l12 in range(lats + 8):
        q = p_of(l12) * g_of(l12)
        for l in range(lats):
            if near(l12, l):
                term = lat_ref[l12 * lats + l] * q
                out[l] = term if out[l] is None else out[l] + term
    return out


def p_getter(p_refs, lats):
    above, own, below = p_refs

    def get(l12, rows):
        if l12 < 4:
            return above[l12, rows, :]
        if l12 < 4 + lats:
            return own[l12 - 4, rows, :]
        return below[l12 - 4 - lats, rows, :]

    return get


def put_split(high_ref, low_ref, rows, columns, value):
    high, low = split(value)
    high_ref[rows, columns] = high
    low_ref[rows, columns] = low


def put_side(high_ref, low_ref, first, rows, group, value, slots):
    for j in range(slots):
        at = slice(first + j * group + rows[0], first + j * group + rows[1])
        part = jnp.where(slot_of(value.shape) == j, value, 0.0)
        put_split(high_ref, low_ref, at, slice(LANES, 2 * LANES), part)


def prepare_body(channels, x_ref, t_ref, a_ref, ax_ref, ta_ref, tx_ref):
    lats, rows, _ = a_ref.shape
    part = rows // SLOTS
    for l in range(lats):
        x = x_ref[pl.ds(l, rows, stride=lats), :]
        a_ref[l] = x
        ax_ref[l] = edges([x[j * part : (j + 1) * part] for j in range(SLOTS)])

    @pl.when(pl.program_id(0) == 0)
    def _():
        for l in range(lats):
            t = t_ref[pl.ds(l, channels, stride=lats), :]
            ta_ref[l] = t
            tx_ref[l] = edges([t])


def prepare(x, t, lats, channels, step_rows):
    lon = x.shape[1]
    rows = x.shape[0] // lats
    sds = lambda *shape: jax.ShapeDtypeStruct(shape, F32)
    block = lambda n: pl.BlockSpec((lats, n, lon), lambda i: (0, i, 0))
    fixed = pl.BlockSpec((lats, channels, lon), lambda i: (0, 0, 0))
    return call(
        functools.partial(prepare_body, channels),
        (sds(lats, rows, lon), sds(lats, rows // SLOTS, lon), sds(lats, channels, lon), sds(lats, channels, lon)),
        grid=(rows // step_rows,),
        in_specs=[
            pl.BlockSpec((step_rows * lats, lon), lambda i: (i, 0)),
            pl.BlockSpec(t.shape, lambda i: (0, 0)),
        ],
        out_specs=(block(step_rows), block(step_rows // SLOTS), fixed, fixed),
        flops=x.size * 4,
        nbytes=x.size * 9,
    )(x, t)


def filter_rows(main, side, high_ref, low_ref, weights, lats, count, slots):
    group = count // slots
    for l in range(lats):
        put_split(high_ref, low_ref, slice(l * count, (l + 1) * count), slice(0, LANES), main[l])
        put_side(high_ref, low_ref, l * count, (0, group), group, side[l], slots)
    return dot3(high_ref[: lats * count, :], low_ref[: lats * count, :], *weights)


def first_own_body(
    channels, n_mem, lat_ref, am, al, ar, po, tm, tl, tr, tpo, bh, bl, z_out, zt_out, e_ref, x_ref, xt_ref, hi, lo, acc
):
    step = pl.program_id(0)
    lats, rows, _ = am.shape
    members = rows // channels
    weights = bh[...], bl[...]
    part = rows // SLOTS
    own = range(4, 4 + lats)

    @pl.when(step == 0)
    def _():
        side = [beside(tl[l], tr[l]) for l in range(lats)]
        z = filter_rows([tm[l] for l in range(lats)], side, hi, lo, weights, lats, channels, 1)
        for l in range(lats):
            zt_out[l] = z[l * channels : (l + 1) * channels]
        out = forward_rows(lat_ref, lambda l: zt_out[l], lambda l12: tpo[l12 - 4], lats, own)
        for l, value in enumerate(out):
            acc[l] = value * (1.0 / n_mem)
            xt_ref[l] = edges([tpo[l]])

    side = [beside(al[l], ar[l]) for l in range(lats)]
    z = filter_rows([am[l] for l in range(lats)], side, hi, lo, weights, lats, rows, SLOTS)
    for l in range(lats):
        z_out[l] = z[l * rows : (l + 1) * rows]
        x_ref[l] = edges([po[l, j * part : (j + 1) * part, :] for j in range(SLOTS)])

    def one(k, sums):
        sel = pl.ds(pl.multiple_of(k * channels, channels), channels)
        out = forward_rows(lat_ref, lambda l: z_out[l, sel, :], lambda l12: po[l12 - 4, sel, :], lats, own)
        return tuple(a + b for a, b in zip(sums, out))

    sums = lax.fori_loop(0, members, one, tuple(acc[l] for l in range(lats)), unroll=2)
    for l, value in enumerate(sums):
        acc[l] = value

    @pl.when(step == pl.num_programs(0) - 1)
    def _():
        e_ref[...] = acc[...]


def first_own(lat_w, a, a_sides, t, t_sides, p_own, lon_h, lon_l, channels, n_mem, step_rows):
    lats, rows, lon = a.shape
    part = step_rows // SLOTS
    mb = pl.BlockSpec((lats, step_rows, lon), lambda i: (0, i, 0))
    sb = pl.BlockSpec((lats, part, lon), lambda i: (0, i, 0))
    fb = pl.BlockSpec((lats, channels, lon), lambda i: (0, 0, 0))
    tb = pl.BlockSpec((lats, channels, lon), lambda i: (0, rows // channels, 0))
    wb = pl.BlockSpec((2 * lon, lon), lambda i: (0, 0))
    sds = lambda *shape: jax.ShapeDtypeStruct(shape, F32)
    fixed = sds(lats, channels, lon)
    return call(
        functools.partial(first_own_body, channels, n_mem),
        (sds(lats, rows, lon), fixed, fixed, sds(lats, rows // SLOTS, lon), fixed),
        grid=(rows // step_rows,),
        in_specs=[smem(), mb, sb, sb, mb, fb, fb, fb, tb, wb, wb],
        out_specs=(mb, fb, fb, sb, fb),
        scratch_shapes=[pltpu.VMEM((lats * step_rows, 2 * lon), BF16)] * 2 + [pltpu.VMEM((lats, channels, lon), F32)],
        flops=lats * rows * lon * 100,
        nbytes=a.size * 16,
    )(lat_w, a, *a_sides, p_own, t, *t_sides, p_own, lon_h, lon_l)


def first_rest_body(
    channels, n_mem, lat_ref, start, z_in, zt, pu, pd, tpu_, tpd, e_in, eo_ref, ea_ref, eb_ref, ec_ref, x_ref, xt_ref, acc
):
    step = pl.program_id(0)
    lats, rows, lon = z_in.shape
    members = rows // channels
    part = rows // SLOTS
    halo = list(range(4)) + list(range(4 + lats, 8 + lats))

    def get(above, below, l12, sel):
        return above[l12, sel, :] if l12 < 4 else below[l12 - 4 - lats, sel, :]

    @pl.when(step == 0)
    def _():
        out = forward_rows(lat_ref, lambda l: zt[l], lambda l12: get(tpu_, tpd, l12, slice(None)), lats, halo)
        acc[4 : 4 + lats] = e_in[...]
        acc[8 + lats] = jnp.zeros((channels, lon), F32)
        for i, (l12, value) in enumerate(zip(halo, out)):
            acc[l12] = value * (1.0 / n_mem)
            xt_ref[i] = edges([get(tpu_, tpd, l12, slice(None))])

    for i, l12 in enumerate(halo):
        x_ref[i] = edges([get(pu, pd, l12, slice(j * part, (j + 1) * part)) for j in range(SLOTS)])

    def one(k, sums):
        sel = pl.ds(pl.multiple_of(k * channels, channels), channels)
        out = forward_rows(lat_ref, lambda l: z_in[l, sel, :], lambda l12: get(pu, pd, l12, sel), lats, halo)
        return tuple(a + b for a, b in zip(sums, out))

    sums = lax.fori_loop(0, members, one, tuple(acc[l12] for l12 in halo), unroll=2)
    for l12, value in zip(halo, sums):
        acc[l12] = value

    @pl.when(step == pl.num_programs(0) - 1)
    def _():
        for ref, first in ((eo_ref, 4), (ea_ref, start[0]), (eb_ref, start[1]), (ec_ref, 0)):
            for r in range(ref.shape[0]):
                ref[r] = acc[first + r]


def first_rest(lat_w, starts, z, zt, p_up, p_down, e_own, channels, n_mem, step_rows):
    lats, rows, lon = z.shape
    part = step_rows // SLOTS
    mb = pl.BlockSpec((lats, step_rows, lon), lambda i: (0, i, 0))
    fb = pl.BlockSpec((lats, channels, lon), lambda i: (0, 0, 0))
    tb = pl.BlockSpec((lats, channels, lon), lambda i: (0, rows // channels, 0))
    whole = lambda *shape: pl.BlockSpec(shape, lambda i: (0,) * len(shape))
    shapes = [(lats + 1, channels, lon)] * 3 + [(1, channels, lon)]
    return call(
        functools.partial(first_rest_body, channels, n_mem),
        [jax.ShapeDtypeStruct(shape, F32) for shape in shapes]
        + [jax.ShapeDtypeStruct((8, rows // SLOTS, lon), F32), jax.ShapeDtypeStruct((8, channels, lon), F32)],
        grid=(rows // step_rows,),
        in_specs=[smem(), smem(), mb, fb, mb, mb, tb, tb, fb],
        out_specs=[whole(*shape) for shape in shapes]
        + [pl.BlockSpec((8, part, lon), lambda i: (0, i, 0)), whole(8, channels, lon)],
        scratch_shapes=[pltpu.VMEM((lats + 9, channels, lon), F32)],
        flops=lats * rows * lon * 60,
        nbytes=z.size * 14,
    )(lat_w, starts, z, zt, p_up, p_down, p_up, p_down, e_own)


ABOVE_A, BELOW_A, ABOVE_B, BELOW_B, TWO_BELOW, TWO_ABOVE, LEFT_A, RIGHT_A, LEFT_B, RIGHT_B = range(10)


def load_g(flag, ga, gb, gc, go, gm_ref, gs_ref, lats, channels):
    above = lambda l: flag[ABOVE_A] * ga[l] + flag[ABOVE_B] * gb[l]
    below = lambda l: flag[BELOW_A] * ga[l] + flag[BELOW_B] * gb[l]
    for l12 in range(lats + 8):
        if l12 < 4:
            value = above(l12)
            if l12 == 0:
                value = value + flag[TWO_ABOVE] * gc[0]
        elif l12 < 4 + lats:
            value = go[l12 - 4]
            if l12 == 4:
                value = value + above(lats)
        else:
            value = below(l12 - 4 - lats)
            if l12 == 4 + lats:
                value = value + go[lats]
        gm_ref[l12] = value[:channels]
        gs_ref[l12] = widen(value[channels:])


def step_body(channels, n_mem, scale, last, *refs):
    lat_ref, flag, start, ga, gb, gc, go = refs[:7]
    am, ax = refs[7], refs[8 : 8 + (2 if not last else 1)]
    refs = refs[8 + len(ax) :]
    p_main, p_sides = refs[:3], refs[3:7]
    tm, tx = refs[7], refs[8 : 8 + len(ax)]
    refs = refs[8 + len(ax) :]
    tp_main, tp_sides = refs[:3], refs[3:7]
    bh, bl = refs[7:9]
    refs = refs[9:]
    if last:
        am_out, tm_out, gm_ref, gs_ref, rh, rl = refs
    else:
        am_out, as_out, tm_out, ts_out, eo_ref, ea_ref, eb_ref, ec_ref = refs[:8]
        gm_ref, gs_ref, rh, rl, zm_ref, zs_ref, acc_m, acc_s = refs[8:]
    step = pl.program_id(0)
    lats, rows, lon = p_main[0].shape
    members = rows // channels
    part = rows // SLOTS
    weights = bh[...], bl[...]
    side_units = part // channels
    unroll = 2 if members % 2 == 0 else 1

    def side_get(sides, l12, sel):
        if 4 <= l12 < 4 + lats:
            return beside(sides[0][l12 - 4, sel, :], sides[1][l12 - 4, sel, :])
        i = l12 if l12 < 4 else l12 - lats
        return beside(sides[2][i, sel, :], sides[3][i, sel, :])

    def adjoint_main(p, k, count):
        sel = pl.ds(pl.multiple_of(k * channels, channels), channels)
        out = adjoint_rows(lat_ref, lambda l12: p(l12, sel), lambda l12: gm_ref[l12], lats)
        for l, value in enumerate(out):
            at = pl.ds(pl.multiple_of(l * count + k * channels, channels), channels)
            put_split(rh, rl, at, slice(0, lon), value)

    def adjoint_side(sides, unit, count, slots):
        sel = slice(unit * channels, (unit + 1) * channels)
        out = adjoint_rows(lat_ref, lambda l12: side_get(sides, l12, sel), lambda l12: gs_ref[l12], lats)
        for l, value in enumerate(out):
            put_side(rh, rl, l * count, (sel.start, sel.stop), count // slots, value, slots)

    def update(main, side, main_put, side_put, count, slots):
        group = count // slots
        grad = dot3(rh[: lats * count, :], rl[: lats * count, :], *weights)
        new_main, new_side = [], []
        for l in range(lats):
            at = slice(l * count, (l + 1) * count)
            new_main.append((1.0 - descent) * main(l) - scale * grad[at, :lon])
            main_put(l, new_main[l])
            if not last:
                found = grad[at, lon:]
                found = pick_slots(found, group) if slots > 1 else found
                new_side.append((1.0 - descent) * side(l) - scale * found)
                side_put(l, new_side[l])
        if not last:
            z = filter_rows(new_main, new_side, rh, rl, weights, lats, count, slots)
            for l in range(lats):
                at = slice(l * count, (l + 1) * count)
                zm_ref[l, :count, :] = z[at, :lon]
                found = z[at, lon:]
                if slots > 1:
                    zs_ref[l, :group, :] = pick_slots(found, group)
                else:
                    zs_ref[l, :group, :] = jnp.where(slot_of(found.shape) == 0, found, 0.0)

    def forward_side(sides, unit, share=None):
        sel = slice(unit * channels, (unit + 1) * channels)
        out = forward_rows(lat_ref, lambda l: zs_ref[l, sel, :], lambda l12: side_get(sides, l12, sel), lats)
        for l12, value in enumerate(out):
            acc_s[l12] += value if share is None else value * share

    def put_rows(ref):
        def put(l, value):
            ref[pl.ds(l, value.shape[0], stride=lats), :] = value

        return put

    def put_lat(ref):
        def put(l, value):
            ref[l] = value

        return put

    p = p_getter(p_main, lats)

    @pl.when(step == 0)
    def _():
        load_g(flag, ga, gb, gc, go, gm_ref, gs_ref, lats, channels)
        tp = p_getter(tp_main, lats)
        adjoint_main(tp, 0, channels)
        adjoint_side(tp_sides, 0, channels, 1)
        if last:
            update(lambda l: tm[l], None, put_rows(tm_out), None, channels, 1)
        else:
            update(
                lambda l: tm[l], lambda l: beside(tx[0][l], tx[1][l]), put_lat(tm_out), put_lat(ts_out), channels, 1
            )
            acc_m[...] = jnp.zeros_like(acc_m)
            acc_s[...] = jnp.zeros_like(acc_s)
            out = forward_rows(lat_ref, lambda l: zm_ref[l, :channels, :], lambda l12: tp(l12, slice(None)), lats)
            for l12, value in enumerate(out):
                acc_m[l12] = value * (1.0 / n_mem)
            forward_side(tp_sides, 0, 1.0 / n_mem)

    lax.fori_loop(0, members, lambda k, c: (adjoint_main(p, k, rows), c)[1], 0, unroll=unroll)
    for unit in range(side_units):
        adjoint_side(p_sides, unit, rows, SLOTS)
    if last:
        update(lambda l: am[l], None, put_rows(am_out), None, rows, SLOTS)
    else:
        update(lambda l: am[l], lambda l: beside(ax[0][l], ax[1][l]), put_lat(am_out), put_lat(as_out), rows, SLOTS)

        def one(k, sums):
            sel = pl.ds(pl.multiple_of(k * channels, channels), channels)
            out = forward_rows(lat_ref, lambda l: zm_ref[l, sel, :], lambda l12: p(l12, sel), lats)
            return tuple(a + b for a, b in zip(sums, out))

        sums = lax.fori_loop(0, members, one, tuple(acc_m[l12] for l12 in range(lats + 8)), unroll=unroll)
        for l12, value in enumerate(sums):
            acc_m[l12] = value
        for unit in range(side_units):
            forward_side(p_sides, unit)

        @pl.when(step == pl.num_programs(0) - 1)
        def _():
            for ref, first in ((eo_ref, 4), (ea_ref, start[0]), (eb_ref, start[1]), (ec_ref, 0)):
                for r in range(ref.shape[0]):
                    ref[r, :channels, :] = acc_m[first + r]
                    ref[r, channels:, :] = narrow(repeat_slots(acc_s[first + r]))


def member_step(
    lat_w, flags, starts, g4, a, a_sides, t, t_sides, p3, x4, xt4, lon_h, lon_l, channels, n_mem, scale, last, step_rows
):
    lats, rows, lon = a.shape
    part = step_rows // SLOTS
    mb = pl.BlockSpec((lats, step_rows, lon), lambda i: (0, i, 0))
    sb = pl.BlockSpec((lats, part, lon), lambda i: (0, i, 0))
    fb = pl.BlockSpec((lats, channels, lon), lambda i: (0, 0, 0))
    tpb = pl.BlockSpec((lats, channels, lon), lambda i: (0, rows // channels, 0))
    xb = pl.BlockSpec((8, part, lon), lambda i: (0, i, 0))
    width = lon if last else 2 * lon
    wb = pl.BlockSpec((2 * lon, width), lambda i: (0, 0))
    whole = lambda shape: pl.BlockSpec(shape, lambda i: (0,) * len(shape))
    sds = lambda *shape: jax.ShapeDtypeStruct(shape, F32)
    half = channels + channels // 2
    scratch = [pltpu.VMEM((lats + 8, channels, lon), F32)] * 2 + [pltpu.VMEM((lats * step_rows, 2 * lon), BF16)] * 2
    if last:
        out_shape = [sds(rows * lats, lon), sds(channels * lats, lon)]
        out_specs = [pl.BlockSpec((step_rows * lats, lon), lambda i: (i, 0)), whole((channels * lats, lon))]
    else:
        out_shape = [sds(lats, rows, lon), sds(lats, rows // SLOTS, lon)] + [sds(lats, channels, lon)] * 2
        out_specs = [mb, sb, fb, fb]
        for count in (lats + 1, lats + 1, lats + 1, 1):
            out_shape.append(sds(count, half, lon))
            out_specs.append(whole((count, half, lon)))
        scratch += [pltpu.VMEM((lats, step_rows, lon), F32), pltpu.VMEM((lats, max(part, channels), lon), F32)]
        scratch += [pltpu.VMEM((lats + 9, channels, lon), F32)] * 2
    return call(
        functools.partial(step_body, channels, n_mem, scale, last),
        out_shape,
        grid=(rows // step_rows,),
        in_specs=[smem()] * 3
        + [whole(g.shape) for g in g4]
        + [mb] + [sb] * len(a_sides)
        + [mb, mb, mb, sb, sb, xb, xb, fb] + [fb] * len(t_sides)
        + [tpb, tpb, tpb] + [whole(x.shape) for x in xt4] + [wb, wb],
        out_specs=out_specs,
        scratch_shapes=scratch,
        flops=lats * rows * lon * 800,
        nbytes=a.size * 40,
    )(lat_w, flags, starts, *g4, a, *a_sides, *p3, *x4, t, *t_sides, *p3, *xt4, lon_h, lon_l)


FIELDS = 24


def route_body(capacity, tile_ref, coef_ref, weight_ref, cell_ref, value_ref, precision_ref, out_ref):
    count = tile_ref.shape[0]
    tile = tile_ref[...]
    named = lane_of((count, LANES)) == tile
    named_bf = jnp.where(named, 1.0, 0.0).astype(BF16)
    before = lax.broadcasted_iota(jnp.int32, (count, count), 0) > lax.broadcasted_iota(jnp.int32, (count, count), 1)
    ranks = dot(jnp.where(before, 1.0, 0.0).astype(BF16), named_bf)
    rank = jnp.sum(jnp.where(named, ranks, 0.0), axis=1, keepdims=True)
    place = tile * capacity + rank.astype(jnp.int32)
    record = jnp.concatenate(
        [
            coef_ref[...],
            weight_ref[...],
            cell_ref[...].astype(F32),
            value_ref[...],
            precision_ref[...],
            jnp.zeros((1, count), F32),
        ],
        0,
    )
    high = record.astype(BF16).astype(F32)
    rest = record - high
    middle = rest.astype(BF16).astype(F32)
    pieces = jnp.concatenate([high, middle, rest - middle], 0).astype(BF16)
    for group in range(out_ref.shape[0]):
        hit = lane_of((count, LANES)) + group * LANES == place
        sent = dot(pieces, jnp.where(hit, 1.0, 0.0).astype(BF16))
        out_ref[group] = sent[:FIELDS] + sent[FIELDS : 2 * FIELDS] + sent[2 * FIELDS :]


def route(tile, coef, weight, cell, value, precision, capacity, slots):
    count = tile.shape[0]
    return call(
        functools.partial(route_body, capacity),
        jax.ShapeDtypeStruct((slots // LANES, FIELDS, LANES), F32),
        in_specs=[vmem()] * 6,
        out_specs=vmem(),
        flops=count * slots * 150,
        nbytes=slots * 200,
    )(tile, coef, weight, cell[None], value[None], precision[None])


def index_body(channels, here_ref, left_ref, right_ref, main_ref, side_ref, record_ref, beside_ref):
    groups = here_ref.shape[0]
    lon = LANES

    def base_of(block):
        cell = block[channels + 4 : channels + 5].astype(jnp.int32)
        return cell >> (2 * lon).bit_length(), (cell & (2 * lon - 1)) >> 1

    def mark(ref, at, index):
        hit = lax.broadcasted_iota(jnp.int32, (ref.shape[0], LANES), 0) == index
        ref[:, at] = jnp.where(hit, 1.0, 0.0).astype(BF16)

    for group in range(groups):
        at = slice(group * LANES, (group + 1) * LANES)
        far = slice((groups + group) * LANES, (groups + group + 1) * LANES)
        block = here_ref[group]
        row, column = base_of(block)
        mark(main_ref, at, row * lon + column)
        record_ref[:, at] = block
        block = left_ref[group]
        row, column = base_of(block)
        mark(side_ref, at, jnp.where(column >= lon - EDGE + 2, row * SLOT + column - (lon - EDGE), -1))
        beside_ref[:, at] = block
        block = right_ref[group]
        row, column = base_of(block)
        mark(side_ref, far, jnp.where(column < EDGE - 2, row * SLOT + EDGE + column, -1))
        beside_ref[:, far] = block


def index(here, left, right, channels, lats, lon):
    slots = here.shape[0] * LANES
    assert lon == 128
    return call(
        functools.partial(index_body, channels),
        (
            jax.ShapeDtypeStruct((lats * lon, slots), BF16),
            jax.ShapeDtypeStruct((lats * SLOT, 2 * slots), BF16),
            jax.ShapeDtypeStruct((FIELDS, slots), F32),
            jax.ShapeDtypeStruct((FIELDS, 2 * slots), F32),
        ),
        in_specs=[vmem()] * 3,
        out_specs=(vmem(),) * 4,
        flops=lats * lon * slots * 4,
        nbytes=lats * lon * slots * 2,
    )(here, left, right)


def stacked_split(value):
    high = value.astype(BF16).astype(F32)
    return jnp.concatenate([high, value - high], 0).astype(BF16)


def obs_body(channels, ens_scale, first, flag, *refs):
    s_refs, refs = refs[: 3 if first else 8], refs[3 if first else 8 :]
    ohm_ref, ohs_ref, record_ref, beside_ref, g_ref, g1_ref, dx_ref = refs
    lats = g_ref.shape[0] - 1
    lon = g_ref.shape[2]
    lane = lane_of((channels, lon))
    slot = lane // SLOT
    main, side, next_main, next_side = [], [], [], []
    for r in range(lats + 1):
        if first:
            s_ref, xa, xb = s_refs
            a = ens_scale * s_ref[r]
            left = flag[LEFT_A] * xa[r] + flag[LEFT_B] * xb[r]
            right = flag[RIGHT_A] * xa[r] + flag[RIGHT_B] * xb[r]
            edge = pltpu.roll(jnp.where(lane < EDGE, right, left), EDGE, 1)
            b = ens_scale * repeat_slots(jnp.where(slot == 0, edge, 0.0))
        else:
            own, other, na, na2, nb, nb2, nc, nc2 = s_refs
            total = own[r] + other[r]
            total = total + (flag[ABOVE_A] + flag[BELOW_A]) * (na[r] + na2[r])
            total = total + (flag[ABOVE_B] + flag[BELOW_B]) * (nb[r] + nb2[r])
            if r == lats:
                total = total + flag[TWO_BELOW] * (nc[0] + nc2[0])
            a = ens_scale * total[:channels]
            b = ens_scale * widen(total[channels:])
        main.append(a)
        side.append(b)
        if r < lats:
            dx_ref[pl.ds(r, channels, stride=lats), :] = a
        next_main.append(jnp.where(lane == lon - 1, pltpu.roll(b, lon - 1 - EDGE, 1), pltpu.roll(a, lon - 1, 1)))

    def next_side(r, at):
        first_own = pltpu.roll(main[r], (EDGE - 1 + SLOT * at) % LANES, 1)
        return jnp.where(lane == EDGE - 1 + SLOT * at, first_own, pltpu.roll(side[r], LANES - 1, 1))

    def join(rows):
        total = rows[0]
        for r in range(1, lats):
            total = jnp.where(slot == r, rows[r], total)
        return total

    x_main = jnp.concatenate(
        [
            jnp.concatenate(rows, 1)
            for rows in (main[:lats], next_main[:lats], main[1:], next_main[1:])
        ],
        0,
    )
    x_side = jnp.concatenate(
        [
            join(side[:lats]),
            join([next_side(r, r) for r in range(lats)]),
            join(side[1:]),
            join([next_side(r + 1, r) for r in range(lats)]),
        ],
        0,
    )

    def handle(x, onehot, record):
        hit = onehot[...]
        weights = record[channels : channels + 4, :]
        found = dot(stacked_split(x), hit)
        found = found[: 4 * channels] + found[4 * channels :]
        mapped = weights[0:1] * found[:channels]
        for corner in range(1, 4):
            mapped += weights[corner : corner + 1] * found[corner * channels : (corner + 1) * channels]
        c = record[:channels, :]
        model = jnp.sum(c * mapped, axis=0, keepdims=True)
        misfit = record[channels + 6 : channels + 7, :] * (model - record[channels + 5 : channels + 6, :])
        spread = c * misfit
        sent = jnp.concatenate([weights[corner : corner + 1] * spread for corner in range(4)], 0)
        back = dot(stacked_split(sent), hit, (((1,), (1,)), ((), ())))
        return back[: 4 * channels] + back[4 * channels :]

    back_main = handle(x_main, ohm_ref, record_ref)
    back_side = handle(x_side, ohs_ref, beside_ref)
    zero = jnp.zeros((channels, lon), F32)
    g_main = [zero] * (lats + 1)
    g_side = [zero] * (lats + 1)
    for r in range(lats):
        for low in range(2):
            here = slice(2 * low * channels, (2 * low + 1) * channels)
            after = slice((2 * low + 1) * channels, (2 * low + 2) * channels)
            own = back_main[here, r * lon : (r + 1) * lon]
            moved = back_main[after, r * lon : (r + 1) * lon]
            edge = jnp.where(slot == r, back_side[here], 0.0)
            edge_moved = jnp.where(slot == r, back_side[after], 0.0)
            into_own = pltpu.roll(edge_moved, (2 * LANES - (EDGE - 1) - SLOT * r) % LANES, 1)
            into_side = pltpu.roll(moved, (EDGE + 1 + SLOT * r) % LANES, 1)
            moved_main = jnp.where(lane == 0, into_own, pltpu.roll(moved, 1, 1))
            moved_side = jnp.where(
                lane == EDGE + SLOT * r, into_side, jnp.where(slot == r, pltpu.roll(edge_moved, 1, 1), 0.0)
            )
            g_main[r + low] = g_main[r + low] + own + moved_main
            g_side[r + low] = g_side[r + low] + edge + moved_side
    for r in range(lats + 1):
        edge = narrow(repeat_slots(g_side[r]))
        g_ref[r, :channels, :] = g_main[r]
        g_ref[r, channels:, :] = edge
        if r == lats:
            g1_ref[0, :channels, :] = g_main[r]
            g1_ref[0, channels:, :] = edge


def observe(flags, sums, records, channels, ens_scale, lats):
    lon = sums[0].shape[2]
    slots = records[0].shape[1]
    half = channels + channels // 2
    return call(
        functools.partial(obs_body, channels, ens_scale, len(sums) == 3),
        (
            jax.ShapeDtypeStruct((lats + 1, half, lon), F32),
            jax.ShapeDtypeStruct((1, half, lon), F32),
            jax.ShapeDtypeStruct((lats * channels, lon), F32),
        ),
        in_specs=[smem()] + [vmem()] * (len(sums) + 4),
        out_specs=(vmem(),) * 3,
        flops=slots * 512 * 128 * 6,
        nbytes=slots * 512 * 4,
    )(flags, *sums, *records)


def shifted(block, axis, distance):
    count = lax.axis_size(axis)
    route = [(i - distance, i) for i in range(count) if 0 <= i - distance < count]
    if not route:
        return jnp.zeros_like(block)
    return lax.ppermute(block, axis, route)


def partner_a(i, count):
    return min(i ^ 1, count - 1)


def partner_b(i, count):
    return (i + 1) % count if i % 2 else (i - 1) % count


def swap(block, axis, partner, other_member=False):
    count = lax.axis_size(axis)
    if not other_member:
        return lax.ppermute(block, axis, [(i, partner(i, count)) for i in range(count)])
    return lax.ppermute(
        block,
        ("mem", axis),
        [(m * count + i, (1 - m) * count + partner(i, count)) for m in range(2) for i in range(count)],
    )


def two_away(block, distance, other_member=False):
    count = lax.axis_size("gy")
    if count == 4:
        return swap(block, "gy", lambda i, n: i ^ 2, other_member)
    block = shifted(block, "gy", distance)
    return swap(block, "gy", lambda i, n: i, True) if other_member else block


def gather_rows(own, to_a, to_b, up1):
    stay = lambda i, n: i
    return (
        own,
        swap(own, "gy", stay, True),
        swap(to_a, "gy", partner_a),
        swap(to_a, "gy", partner_a, True),
        swap(to_b, "gy", partner_b),
        swap(to_b, "gy", partner_b, True),
        two_away(up1, -2),
        two_away(up1, -2, True),
    )


def assimilate(
    alpha,
    static_control,
    perturbations,
    sigma,
    obs_coef,
    interp_weights,
    obs_values,
    obs_weights,
    obs_tile,
    obs_cell,
):
    members, variables, levels, lats, lon = alpha.shape
    channels = variables * levels
    n_mem, n_gx, n_gy = (lax.axis_size(a) for a in ("mem", "gx", "gy"))
    assert n_mem == 2 and n_gx % 2 == 0 and n_gy % 2 == 0
    ens_scale = ens_share / math.sqrt(members * n_mem - 1)
    rows = members * channels
    step_rows = 8 * channels

    def lat_major(x, count):
        return x.reshape(count, lats, lon).transpose(1, 0, 2)

    p_own = jnp.concatenate(
        [
            lat_major(perturbations.astype(F32), rows),
            lat_major(sigma * (static_share / ens_scale), channels),
        ],
        1,
    )
    p_up, p_down = shifted(p_own, "gy", 1), shifted(p_own, "gy", -1)
    p3 = (p_up, p_own, p_down)
    a, a_edges, t, t_edges = prepare(
        alpha.reshape(rows * lats, lon), static_control.reshape(channels * lats, lon), lats, channels, step_rows
    )

    def from_beside(x):
        return shifted(x, "gx", 1), shifted(x, "gx", -1)

    a_sides, t_sides = from_beside(a_edges), from_beside(t_edges)

    x, y = lax.axis_index("gx"), lax.axis_index("gy")
    odd = y % 2 == 1
    odd_x = x % 2 == 1
    flags = jnp.stack(
        [
            odd,
            ~odd,
            ~odd & (y > 0),
            odd & (y < n_gy - 1),
            y < n_gy - 2,
            y >= 2,
            odd_x,
            ~odd_x,
            ~odd_x & (x > 0),
            odd_x & (x < n_gx - 1),
        ]
    ).astype(F32)
    starts = jnp.where(jnp.stack([odd, ~odd]), 0, 4 + lats).astype(jnp.int32)

    obs_rows = obs_tile.shape[0]
    tile_count = n_gx * n_gy
    capacity = 2 * obs_rows // tile_count
    slots = tile_count * capacity
    sent = route(
        obs_tile, obs_coef.reshape(channels, obs_rows), interp_weights, obs_cell, obs_values, obs_weights, capacity, slots
    )
    per_group = LANES // capacity if capacity < LANES else 1
    if per_group > 1:
        sent = sent.reshape(-1, FIELDS, per_group, capacity).transpose(0, 2, 1, 3).reshape(tile_count, FIELDS, capacity)
    arrived = lax.all_to_all(sent, ("gx", "gy"), split_axis=0, concat_axis=0, tiled=True)
    if per_group > 1:
        arrived = arrived.reshape(-1, per_group, FIELDS, capacity).transpose(0, 2, 1, 3).reshape(-1, FIELDS, LANES)
    from_left, from_right = from_beside(arrived)
    records = index(arrived, from_left, from_right, channels, lats, lon)

    lat_w = jnp.asarray(lat_table(lats, n_gy) * (4.0 / PASS / PASS))[y].reshape(-1)
    kind = jnp.where(x == 0, 0, jnp.where(x == n_gx - 1, min(n_gx, 3) - 1, 1))
    table = lon_table(lon, n_gx)
    table_high = table.astype(jnp.bfloat16)
    table_low = (table - table_high.astype(np.float64)).astype(jnp.bfloat16)
    lon_h, lon_l = jnp.asarray(table_high)[kind], jnp.asarray(table_low)[kind]

    z, zt, e_own, x_own, xt_own = first_own(
        lat_w, a, a_sides, t, t_sides, p_own, lon_h[:, :lon], lon_l[:, :lon], channels, n_mem, step_rows
    )
    x_own, xt_own = from_beside(x_own), from_beside(xt_own)
    *e4, x_rest, xt_rest = first_rest(lat_w, starts, z, zt, p_up, p_down, e_own, channels, n_mem, step_rows)
    own, own2, na, na2, nb, nb2, nc, nc2 = gather_rows(*e4)
    s = own + own2 + (na + na2) + (flags[ABOVE_B] + flags[BELOW_B]) * (nb + nb2)
    s = s + jnp.concatenate([jnp.zeros_like(s[:lats]), flags[TWO_BELOW] * (nc + nc2)], 0)
    s, x_rest, xt_rest = lax.optimization_barrier((s, x_rest, xt_rest))
    sums = (s, swap(s, "gx", partner_a), swap(s, "gx", partner_b))
    x_rest, xt_rest = from_beside(x_rest), from_beside(xt_rest)
    x4, xt4 = (*x_own, *x_rest), (*xt_own, *xt_rest)
    g, g_over, _ = observe(flags, sums, records, channels, ens_scale, lats)

    def gather_g(g, g_over):
        return swap(g, "gy", partner_a), swap(g, "gy", partner_b), two_away(g_over, 2), g

    scale = descent * ens_scale
    a, a_side, t, t_side, *e4 = member_step(
        lat_w, flags, starts, gather_g(g, g_over), a, a_sides, t, t_sides, p3, x4, xt4, lon_h, lon_l,
        channels, n_mem, scale, False, step_rows,
    )
    sums = gather_rows(*e4)
    g, g_over, dx = observe(flags, sums, records, channels, ens_scale, lats)
    a, t = member_step(
        lat_w, flags, starts, gather_g(g, g_over), a, (a_side,), t, (t_side,), p3, x4, xt4, lon_h[:, :lon], lon_l[:, :lon],
        channels, n_mem, scale, True, step_rows,
    )
    return (
        a.reshape(alpha.shape),
        t.reshape(static_control.shape),
        dx.reshape(static_control.shape),
    )


def solution(mesh):
    placed = (
        P("mem", None, None, "gy", "gx"),
        P(None, None, "gy", "gx"),
        P("mem", None, None, "gy", "gx"),
        P(None, None, "gy", "gx"),
        P(None, None, ("gx", "gy")),
        P(None, ("gx", "gy")),
        P(("gx", "gy")),
        P(("gx", "gy")),
        P(("gx", "gy"), None),
        P(("gx", "gy")),
    )
    return jax.shard_map(
        assimilate,
        mesh=mesh,
        in_specs=placed,
        out_specs=(
            P("mem", None, None, "gy", "gx"),
            P(None, None, "gy", "gx"),
            P(None, None, "gy", "gx"),
        ),
        check_vma=False,
    )
```

profile of v0, /device:TPU:0, one launch (start us, length us, event | category | flops | bytes accessed | tf_op | source)
XLA Modules:
  0.0 206.5 jit_solution(8336254187332891213)
XLA Ops:
  4.4 6.9 %collective-permute-start.4 = (f32[4,1040,128]{2,1,0:T(8,128)S(1)}, f32[4,1040,128]{2,1,0:T(8,128)}, u32[]{:S(2)}, u32[]{:S(2)}) collective-permute-start(f32[4,1040,128]{2,1,0:T(8,128)S(1)} %pad_maximum_fusion.po.tpo.refs_11_.refs_21_.refs_10_.refs_19_), channel_id=1, source_target_pairs={{0,1},{1,2},{2,3},{4,5},{5,6},{6,7},{8,9},{9,10},{10,11},{12,13},{... | collective-permute-start | bytes 6389768 | tf_op jit(solution)/shard_map/ppermute | solution.py:777
  11.3 3.4 %shard_map.148 = (f32[4,1024,128]{2,1,0:T(8,128)S(1)}, f32[4,256,128]{2,1,0:T(8,128)}, f32[4,16,128]{2,1,0:T(8,128)S(1)}, f32[4,16,128]{2,1,0:T(8,128)}) custom-call(f32[4096,128]{1,0:T(8,128)S(1)} %bitcast.33, f32[64,128]{1,0:T(8,128)S(1)} %bitcast.34), custom_call_target="tpu_custom_call" | custom-call | flops 2097152 | bytes 4718592 | tf_op jit(solution)/shard_map/pallas_call | solution.py:208
  17.4 3.1 %collective-permute-start = (f32[4,256,128]{2,1,0:T(8,128)}, f32[4,256,128]{2,1,0:T(8,128)S(1)}, u32[]{:S(2)}, u32[]{:S(2)}) collective-permute-start(f32[4,256,128]{2,1,0:T(8,128)} %get-tuple-element.41), channel_id=1, source_target_pairs={{0,4},{4,8},{8,12},{1,5},{5,9},{9,13},{2,6},{6,10},{10,14},{3,7},{... | collective-permute-start | bytes 1572872 | tf_op jit(solution)/shard_map/ppermute | solution.py:777
  24.8 5.6 %collective-permute-start.2 = (f32[4,16,128]{2,1,0:T(8,128)}, f32[4,16,128]{2,1,0:T(8,128)}, u32[]{:S(2)}, u32[]{:S(2)}) collective-permute-start(f32[4,16,128]{2,1,0:T(8,128)} %get-tuple-element.43), channel_id=1, source_target_pairs={{0,4},{4,8},{8,12},{1,5},{5,9},{9,13},{2,6},{6,10},{10,14},{3,7},{... | collective-permute-start | bytes 98312 | tf_op jit(solution)/shard_map/ppermute | solution.py:777
  33.7 6.1 %shard_map.149 = (f32[4,1024,128]{2,1,0:T(8,128)S(1)}, f32[4,16,128]{2,1,0:T(8,128)S(1)}, f32[4,16,128]{2,1,0:T(8,128)S(1)}, f32[4,256,128]{2,1,0:T(8,128)S(1)}, f32[4,16,128]{2,1,0:T(8,128)S(1)}) custom-call(f32[48]{0:T(128)S(1)} %reshape_squeeze.3.lat_ref.refs_0_, f32[4,1024,128]{2,1,0:T(8,128)S(1)} %copy-done.1, ...), custom_call_target="tpu_custom_call" | custom-call | flops 52428800 | bytes 8388608 | tf_op jit(solution)/shard_map/pallas_call | solution.py:281
  41.3 13.2 %collective-permute-done.5.pd.tpd.refs_12_.refs_22_.refs_11_.refs_20_ = f32[4,1040,128]{2,1,0:T(8,128)} collective-permute-done((f32[4,1040,128]{2,1,0:T(8,128)S(1)}, f32[4,1040,128]{2,1,0:T(8,128)}, u32[]{:S(2)}, u32[]{:S(2)}) %collective-permute-start.5) | collective-permute-done | bytes 2129952 | tf_op jit(solution)/shard_map/ppermute | solution.py:777
  55.6 7.3 %shard_map.150 = (f32[5,16,128]{2,1,0:T(8,128)S(1)}, f32[5,16,128]{2,1,0:T(8,128)S(1)}, f32[5,16,128]{2,1,0:T(8,128)S(1)}, f32[1,16,128]{2,1,0:T(8,128)S(1)}, f3...) custom-call(f32[48]{0:T(128)S(1)} %reshape_squeeze.3.lat_ref.refs_0_, s32[2]{0:T(128)S(1)} %add_select_fusion.start.refs_2_, ...), custom_call_target="tpu_custom_call" | custom-call | flops 31457280 | bytes 7340032 | tf_op jit(solution)/shard_map/pallas_call | solution.py:341
  62.9 5.1 %collective-permute-start.12 = (f32[1,16,128]{2,1,0:T(8,128)S(1)}, f32[1,16,128]{2,1,0:T(8,128)S(1)}, u32[]{:S(2)}, u32[]{:S(2)}) collective-permute-start(f32[1,16,128]{2,1,0:T(8,128)S(1)} %get-tuple-element.50), channel_id=1, source_target_pairs={{0,18},{1,19},{2,16},{3,17},{16,2},{17,3},{18,0},{19,1},{4,22},{5,... | collective-permute-start | bytes 24584 | tf_op jit(solution)/shard_map/ppermute | solution.py:792
  72.5 5.2 %collective-permute-start.10 = (f32[5,16,128]{2,1,0:T(8,128)S(1)}, f32[5,16,128]{2,1,0:T(8,128)S(1)}, u32[]{:S(2)}, u32[]{:S(2)}) collective-permute-start(f32[5,16,128]{2,1,0:T(8,128)S(1)} %get-tuple-element.49), channel_id=1, source_target_pairs={{0,19},{1,18},{2,17},{3,16},{16,3},{17,2},{18,1},{19,0},{4,23},{5,... | collective-permute-start | bytes 122888 | tf_op jit(solution)/shard_map/ppermute | solution.py:792
  84.8 4.0 %collective-permute-start.22 = (f32[8,256,128]{2,1,0:T(8,128)}, f32[8,256,128]{2,1,0:T(8,128)}, u32[]{:S(2)}, u32[]{:S(2)}) collective-permute-start(f32[8,256,128]{2,1,0:T(8,128)} %get-tuple-element.61), channel_id=1, source_target_pairs={{0,4},{4,8},{8,12},{1,5},{5,9},{9,13},{2,6},{6,10},{10,14},{3,7},{... | collective-permute-start | bytes 3145736 | tf_op jit(solution)/shard_map/ppermute | solution.py:777
  95.2 3.4 %shard_map.151 = f32[16,24,128]{2,1,0:T(8,128)S(1)} custom-call(s32[1024,1]{1,0:T(8,128)S(1)} %copy-done.10, f32[16,1024]{1,0:T(8,128)S(1)} %bitcast.35, f32[4,1024]{1,0:T(4,128)S(1)} %copy-done.25, s32[1,1024]{1,0:T(1,128)S(1)} %bitcast.36, f32[1,1024]{1,0:T(1,128)S(1)} %bitcast.37, f32[1,1024]{1,0:T(1,128)S(1)} %bitcast.38), custom_call_target="tpu_custom_call" | custom-call | flops 314572800 | bytes 409600 | tf_op jit(solution)/shard_map/pallas_call | solution.py:588
  99.3 4.2 %all-to-all-start = ((f32[16,24,128]{2,1,0:T(8,128)}), f32[16,24,128]{2,1,0:T(8,128)}, u32[]{:S(2)}, u32[]{:S(2)}) async-start(f32[16,24,128]{2,1,0:T(8,128)} %copy-done.11), calls=%async_computation | async-start | bytes 393216 | tf_op jit(solution)/shard_map/all_to_all | solution.py:891
  104.8 6.7 %all-to-all-done.here_ref = f32[16,24,128]{2,1,0:T(8,128)} async-done(((f32[16,24,128]{2,1,0:T(8,128)}), f32[16,24,128]{2,1,0:T(8,128)}, u32[]{:S(2)}, u32[]{:S(2)}) %all-to-all-start) | async-done | bytes 196640 | tf_op jit(solution)/shard_map/all_to_all | solution.py:891
  112.9 3.0 %collective-permute-start.24 = (f32[4,16,128]{2,1,0:T(8,128)}, f32[4,16,128]{2,1,0:T(8,128)S(1)}, u32[]{:S(2)}, u32[]{:S(2)}) collective-permute-start(f32[4,16,128]{2,1,0:T(8,128)} %copy-done.24), channel_id=1, source_target_pairs={{0,4},{4,8},{8,12},{1,5},{5,9},{9,13},{2,6},{6,10},{10,14},{3,7},{... | collective-permute-start | bytes 98312 | tf_op jit(solution)/shard_map/ppermute | solution.py:777
  117.6 4.0 %collective-permute-start.20 = (f32[4,256,128]{2,1,0:T(8,128)}, f32[4,256,128]{2,1,0:T(8,128)S(1)}, u32[]{:S(2)}, u32[]{:S(2)}) collective-permute-start(f32[4,256,128]{2,1,0:T(8,128)} %copy-done.20), channel_id=1, source_target_pairs={{0,4},{4,8},{8,12},{1,5},{5,9},{9,13},{2,6},{6,10},{10,14},{3,7},{... | collective-permute-start | bytes 1572872 | tf_op jit(solution)/shard_map/ppermute | solution.py:777
  121.6 3.6 %collective-permute-start.15 = (f32[16,24,128]{2,1,0:T(8,128)}, f32[16,24,128]{2,1,0:T(8,128)S(1)}, u32[]{:S(2)}, u32[]{:S(2)}) collective-permute-start(f32[16,24,128]{2,1,0:T(8,128)} %all-to-all-done.here_ref), channel_id=1, source_target_pairs={{0,4},{4,8},{8,12},{1,5},{5,9},{9,13},{2,6},{6,10},{10,14},{3,7},{... | collective-permute-start | bytes 589832 | tf_op jit(solution)/shard_map/ppermute | solution.py:777
  126.5 3.4 %collective-permute-done.14.refs_2_ = f32[5,16,128]{2,1,0:T(8,128)S(1)} collective-permute-done((f32[5,16,128]{2,1,0:T(8,128)S(1)}, f32[5,16,128]{2,1,0:T(8,128)S(1)}, u32[]{:S(2)}, u32[]{:S(2)}) %collective-permute-start.14) | collective-permute-done | bytes 40992 | tf_op jit(solution)/shard_map/ppermute | solution.py:791
  129.9 6.4 %collective-permute-start.13 = (f32[5,16,128]{2,1,0:T(8,128)S(1)}, f32[5,16,128]{2,1,0:T(8,128)S(1)}, u32[]{:S(2)}, u32[]{:S(2)}) collective-permute-start(f32[5,16,128]{2,1,0:T(8,128)S(1)} %pad_add_fusion.refs_0_), channel_id=1, source_target_pairs={{0,4},{4,0},{8,12},{12,8},{1,5},{5,1},{9,13},{13,9},{2,6},{6,2},{1... | collective-permute-start | bytes 122888 | tf_op jit(solution)/shard_map/ppermute | solution.py:791
  139.5 3.6 %shard_map.153 = (f32[5,24,128]{2,1,0:T(8,128)S(1)}, f32[1,24,128]{2,1,0:T(8,128)S(1)}, f32[64,128]{1,0:T(8,128)}) custom-call(f32[10]{0:T(128)S(1)} %convert_element_type.4.flag.refs_1_, f32[5,16,128]{2,1,0:T(8,128)S(1)} %pad_add_fusion.refs_0_, f32[5,16,128]{2,1,0:T(8,128)S(1)} %collective-permute-done.13.refs_1_, ...), custom_call_target="tpu_custom_call" | custom-call | flops 805306368 | bytes 4194304 | tf_op jit(solution)/shard_map/pallas_call | solution.py:758
  149.7 4.8 %collective-permute-done.18.refs_4_ = f32[5,24,128]{2,1,0:T(8,128)S(1)} collective-permute-done((f32[5,24,128]{2,1,0:T(8,128)S(1)}, f32[5,24,128]{2,1,0:T(8,128)S(1)}, u32[]{:S(2)}, u32[]{:S(2)}) %collective-permute-start.18) | collective-permute-done | bytes 61472 | tf_op jit(solution)/shard_map/ppermute | solution.py:791
  155.4 16.0 %shard_map.154 = (f32[4,1024,128]{2,1,0:T(8,128)S(1)}, f32[4,256,128]{2,1,0:T(8,128)S(1)}, f32[4,16,128]{2,1,0:T(8,128)S(1)}, f32[4,16,128]{2,1,0:T(8,128)S(1)},...) custom-call(f32[48]{0:T(128)S(1)} %reshape_squeeze.3.lat_ref.refs_0_, ...), custom_call_target="tpu_custom_call" | custom-call | flops 419430400 | bytes 20971520 | tf_op jit(solution)/shard_map/pallas_call | solution.py:537
  177.9 3.1 %collective-permute-start.32 = (f32[5,24,128]{2,1,0:T(8,128)S(1)}, f32[5,24,128]{2,1,0:T(8,128)S(1)}, u32[]{:S(2)}, u32[]{:S(2)}) collective-permute-start(f32[5,24,128]{2,1,0:T(8,128)S(1)} %get-tuple-element.66), channel_id=1, source_target_pairs={{0,19},{1,18},{2,17},{3,16},{16,3},{17,2},{18,1},{19,0},{4,23},{5,... | collective-permute-start | bytes 184328 | tf_op jit(solution)/shard_map/ppermute | solution.py:792
  187.0 3.5 %shard_map.155 = (f32[5,24,128]{2,1,0:T(8,128)S(1)}, f32[1,24,128]{2,1,0:T(8,128)S(1)}, f32[64,128]{1,0:T(8,128)}) custom-call(f32[10]{0:T(128)S(1)} %convert_element_type.4.flag.refs_1_, f32[5,24,128]{2,1,0:T(8,128)S(1)} %get-tuple-element.64.refs_0_, f32[5,24,128]{2,1,0:T(8,128)S(1)} %collective-permute-done.28.refs_1_, ...), custom_call_target="tpu_custom_call" | custom-call | flops 805306368 | bytes 4194304 | tf_op jit(solution)/shard_map/pallas_call | solution.py:758
  197.2 9.3 %shard_map.156 = (f32[4096,128]{1,0:T(8,128)}, f32[64,128]{1,0:T(8,128)}) custom-call(f32[48]{0:T(128)S(1)} %reshape_squeeze.3.lat_ref.refs_0_, f32[10]{0:T(128)S(1)} %convert_element_type.4.flag.refs_1_, s32[2]{0:T(128)S(1)} %copy-done.19, f32[5,24,128]{2,1,0:T(8,128)S(1)} %collective-permute-done.35.refs_3_, ...), custom_call_target="tpu_custom_call" | custom-call | flops 419430400 | bytes 20971520 | tf_op jit(solution)/shard_map/pallas_call | solution.py:537
  (137 shorter events, 69.1 us)
Async XLA Ops:
  3.0 51.5 %collective-permute-start.5 = (f32[4,1040,128]{2,1,0:T(8,128)S(1)}, f32[4,1040,128]{2,1,0:T(8,128)}, u32[]{:S(2)}, u32[]{:S(2)}) collective-permute-start(f32[4,1040,128]{2,1,0:T(8,128)S(1)} %pad_maximum_fusion.po.tpo.refs_11_.refs_21_.refs_10_.refs_19_), channel_id=1, source_target_pairs={{1,0},{2,1},{3,2},{5,4},{6,5},{7,6},{9,8},{10,9},{11,10},{13,12},{... | collective-permute-start | bytes 6389768 | tf_op jit(solution)/shard_map/ppermute | solution.py:777
  4.4 51.2 %collective-permute-start.4 = (f32[4,1040,128]{2,1,0:T(8,128)S(1)}, f32[4,1040,128]{2,1,0:T(8,128)}, u32[]{:S(2)}, u32[]{:S(2)}) collective-permute-start(f32[4,1040,128]{2,1,0:T(8,128)S(1)} %pad_maximum_fusion.po.tpo.refs_11_.refs_21_.refs_10_.refs_19_), channel_id=1, source_target_pairs={{0,1},{1,2},{2,3},{4,5},{5,6},{6,7},{8,9},{9,10},{10,11},{12,13},{... | collective-permute-start | bytes 6389768 | tf_op jit(solution)/shard_map/ppermute | solution.py:777
  16.1 14.9 %collective-permute-start.1 = (f32[4,256,128]{2,1,0:T(8,128)}, f32[4,256,128]{2,1,0:T(8,128)S(1)}, u32[]{:S(2)}, u32[]{:S(2)}) collective-permute-start(f32[4,256,128]{2,1,0:T(8,128)} %get-tuple-element.41), channel_id=1, source_target_pairs={{4,0},{8,4},{12,8},{5,1},{9,5},{13,9},{6,2},{10,6},{14,10},{7,3},{... | collective-permute-start | bytes 1572872 | tf_op jit(solution)/shard_map/ppermute | solution.py:777
  17.4 13.6 %collective-permute-start = (f32[4,256,128]{2,1,0:T(8,128)}, f32[4,256,128]{2,1,0:T(8,128)S(1)}, u32[]{:S(2)}, u32[]{:S(2)}) collective-permute-start(f32[4,256,128]{2,1,0:T(8,128)} %get-tuple-element.41), channel_id=1, source_target_pairs={{0,4},{4,8},{8,12},{1,5},{5,9},{9,13},{2,6},{6,10},{10,14},{3,7},{... | collective-permute-start | bytes 1572872 | tf_op jit(solution)/shard_map/ppermute | solution.py:777
  62.9 14.8 %collective-permute-start.12 = (f32[1,16,128]{2,1,0:T(8,128)S(1)}, f32[1,16,128]{2,1,0:T(8,128)S(1)}, u32[]{:S(2)}, u32[]{:S(2)}) collective-permute-start(f32[1,16,128]{2,1,0:T(8,128)S(1)} %get-tuple-element.50), channel_id=1, source_target_pairs={{0,18},{1,19},{2,16},{3,17},{16,2},{17,3},{18,0},{19,1},{4,22},{5,... | collective-permute-start | bytes 24584 | tf_op jit(solution)/shard_map/ppermute | solution.py:792
  67.9 9.8 %collective-permute-start.11 = (f32[1,16,128]{2,1,0:T(8,128)S(1)}, f32[1,16,128]{2,1,0:T(8,128)S(1)}, u32[]{:S(2)}, u32[]{:S(2)}) collective-permute-start(f32[1,16,128]{2,1,0:T(8,128)S(1)} %get-tuple-element.50), channel_id=1, source_target_pairs={{0,2},{1,3},{2,0},{3,1},{4,6},{5,7},{6,4},{7,5},{8,10},{9,11},{10,... | collective-permute-start | bytes 24584 | tf_op jit(solution)/shard_map/ppermute | solution.py:791
  69.7 12.0 %collective-permute-start.8 = (f32[5,16,128]{2,1,0:T(8,128)S(1)}, f32[5,16,128]{2,1,0:T(8,128)S(1)}, u32[]{:S(2)}, u32[]{:S(2)}) collective-permute-start(f32[5,16,128]{2,1,0:T(8,128)S(1)} %get-tuple-element.48), channel_id=1, source_target_pairs={{0,17},{1,16},{2,19},{3,18},{16,1},{17,0},{18,3},{19,2},{4,21},{5,... | collective-permute-start | bytes 122888 | tf_op jit(solution)/shard_map/ppermute | solution.py:792
  72.5 9.3 %collective-permute-start.7 = (f32[5,16,128]{2,1,0:T(8,128)S(1)}, f32[5,16,128]{2,1,0:T(8,128)S(1)}, u32[]{:S(2)}, u32[]{:S(2)}) collective-permute-start(f32[5,16,128]{2,1,0:T(8,128)S(1)} %get-tuple-element.48), channel_id=1, source_target_pairs={{0,1},{1,0},{2,3},{3,2},{4,5},{5,4},{6,7},{7,6},{8,9},{9,8},{10,11... | collective-permute-start | bytes 122888 | tf_op jit(solution)/shard_map/ppermute | solution.py:791
  72.5 9.3 %collective-permute-start.10 = (f32[5,16,128]{2,1,0:T(8,128)S(1)}, f32[5,16,128]{2,1,0:T(8,128)S(1)}, u32[]{:S(2)}, u32[]{:S(2)}) collective-permute-start(f32[5,16,128]{2,1,0:T(8,128)S(1)} %get-tuple-element.49), channel_id=1, source_target_pairs={{0,19},{1,18},{2,17},{3,16},{16,3},{17,2},{18,1},{19,0},{4,23},{5,... | collective-permute-start | bytes 122888 | tf_op jit(solution)/shard_map/ppermute | solution.py:792
  83.5 71.9 %collective-permute-start.23 = (f32[8,256,128]{2,1,0:T(8,128)}, f32[8,256,128]{2,1,0:T(8,128)S(1)}, u32[]{:S(2)}, u32[]{:S(2)}) collective-permute-start(f32[8,256,128]{2,1,0:T(8,128)} %get-tuple-element.61), channel_id=1, source_target_pairs={{4,0},{8,4},{12,8},{5,1},{9,5},{13,9},{6,2},{10,6},{14,10},{7,3},{... | collective-permute-start | bytes 3145736 | tf_op jit(solution)/shard_map/ppermute | solution.py:777
  84.8 70.6 %collective-permute-start.22 = (f32[8,256,128]{2,1,0:T(8,128)}, f32[8,256,128]{2,1,0:T(8,128)}, u32[]{:S(2)}, u32[]{:S(2)}) collective-permute-start(f32[8,256,128]{2,1,0:T(8,128)} %get-tuple-element.61), channel_id=1, source_target_pairs={{0,4},{4,8},{8,12},{1,5},{5,9},{9,13},{2,6},{6,10},{10,14},{3,7},{... | collective-permute-start | bytes 3145736 | tf_op jit(solution)/shard_map/ppermute | solution.py:777
  99.3 12.2 %all-to-all-start = ((f32[16,24,128]{2,1,0:T(8,128)}), f32[16,24,128]{2,1,0:T(8,128)}, u32[]{:S(2)}, u32[]{:S(2)}) async-start(f32[16,24,128]{2,1,0:T(8,128)} %copy-done.11), calls=%async_computation | async-start | bytes 393216 | tf_op jit(solution)/shard_map/all_to_all | solution.py:891
  103.5 12.4 %collective-permute-start.25 = (f32[4,16,128]{2,1,0:T(8,128)}, f32[4,16,128]{2,1,0:T(8,128)}, u32[]{:S(2)}, u32[]{:S(2)}) collective-permute-start(f32[4,16,128]{2,1,0:T(8,128)} %copy-done.24), channel_id=1, source_target_pairs={{4,0},{8,4},{12,8},{5,1},{9,5},{13,9},{6,2},{10,6},{14,10},{7,3},{... | collective-permute-start | bytes 98312 | tf_op jit(solution)/shard_map/ppermute | solution.py:777
  111.6 10.0 %collective-permute-start.16 = (f32[16,24,128]{2,1,0:T(8,128)}, f32[16,24,128]{2,1,0:T(8,128)S(1)}, u32[]{:S(2)}, u32[]{:S(2)}) collective-permute-start(f32[16,24,128]{2,1,0:T(8,128)} %all-to-all-done.here_ref), channel_id=1, source_target_pairs={{4,0},{8,4},{12,8},{5,1},{9,5},{13,9},{6,2},{10,6},{14,10},{7,3},{... | collective-permute-start | bytes 589832 | tf_op jit(solution)/shard_map/ppermute | solution.py:777
  116.0 27.2 %collective-permute-start.21 = (f32[4,256,128]{2,1,0:T(8,128)}, f32[4,256,128]{2,1,0:T(8,128)S(1)}, u32[]{:S(2)}, u32[]{:S(2)}) collective-permute-start(f32[4,256,128]{2,1,0:T(8,128)} %copy-done.20), channel_id=1, source_target_pairs={{4,0},{8,4},{12,8},{5,1},{9,5},{13,9},{6,2},{10,6},{14,10},{7,3},{... | collective-permute-start | bytes 1572872 | tf_op jit(solution)/shard_map/ppermute | solution.py:777
  117.6 26.7 %collective-permute-start.20 = (f32[4,256,128]{2,1,0:T(8,128)}, f32[4,256,128]{2,1,0:T(8,128)S(1)}, u32[]{:S(2)}, u32[]{:S(2)}) collective-permute-start(f32[4,256,128]{2,1,0:T(8,128)} %copy-done.20), channel_id=1, source_target_pairs={{0,4},{4,8},{8,12},{1,5},{5,9},{9,13},{2,6},{6,10},{10,14},{3,7},{... | collective-permute-start | bytes 1572872 | tf_op jit(solution)/shard_map/ppermute | solution.py:777
  129.9 8.3 %collective-permute-start.13 = (f32[5,16,128]{2,1,0:T(8,128)S(1)}, f32[5,16,128]{2,1,0:T(8,128)S(1)}, u32[]{:S(2)}, u32[]{:S(2)}) collective-permute-start(f32[5,16,128]{2,1,0:T(8,128)S(1)} %pad_add_fusion.refs_0_), channel_id=1, source_target_pairs={{0,4},{4,0},{8,12},{12,8},{1,5},{5,1},{9,13},{13,9},{2,6},{6,2},{1... | collective-permute-start | bytes 122888 | tf_op jit(solution)/shard_map/ppermute | solution.py:791
  138.2 11.2 %collective-permute-start.27 = (f32[8,16,128]{2,1,0:T(8,128)}, f32[8,16,128]{2,1,0:T(8,128)S(1)}, u32[]{:S(2)}, u32[]{:S(2)}) collective-permute-start(f32[8,16,128]{2,1,0:T(8,128)} %copy-done.22), channel_id=1, source_target_pairs={{4,0},{8,4},{12,8},{5,1},{9,5},{13,9},{6,2},{10,6},{14,10},{7,3},{... | collective-permute-start | bytes 196616 | tf_op jit(solution)/shard_map/ppermute | solution.py:777
  147.8 6.7 %collective-permute-start.18 = (f32[5,24,128]{2,1,0:T(8,128)S(1)}, f32[5,24,128]{2,1,0:T(8,128)S(1)}, u32[]{:S(2)}, u32[]{:S(2)}) collective-permute-start(f32[5,24,128]{2,1,0:T(8,128)S(1)} %get-tuple-element.58.refs_6_), channel_id=1, source_target_pairs={{0,3},{1,2},{2,1},{3,0},{4,7},{5,6},{6,5},{7,4},{8,11},{9,10},{10,... | collective-permute-start | bytes 184328 | tf_op jit(solution)/shard_map/ppermute | solution.py:791
  171.5 6.4 %collective-permute-start.34 = (f32[1,24,128]{2,1,0:T(8,128)S(1)}, f32[1,24,128]{2,1,0:T(8,128)S(1)}, u32[]{:S(2)}, u32[]{:S(2)}) collective-permute-start(f32[1,24,128]{2,1,0:T(8,128)S(1)} %get-tuple-element.67), channel_id=1, source_target_pairs={{0,18},{1,19},{2,16},{3,17},{16,2},{17,3},{18,0},{19,1},{4,22},{5,... | collective-permute-start | bytes 36872 | tf_op jit(solution)/shard_map/ppermute | solution.py:792
  172.3 8.7 %collective-permute-start.33 = (f32[1,24,128]{2,1,0:T(8,128)S(1)}, f32[1,24,128]{2,1,0:T(8,128)S(1)}, u32[]{:S(2)}, u32[]{:S(2)}) collective-permute-start(f32[1,24,128]{2,1,0:T(8,128)S(1)} %get-tuple-element.67), channel_id=1, source_target_pairs={{0,2},{1,3},{2,0},{3,1},{4,6},{5,7},{6,4},{7,5},{8,10},{9,11},{10,... | collective-permute-start | bytes 36872 | tf_op jit(solution)/shard_map/ppermute | solution.py:791
  174.4 8.3 %collective-permute-start.30 = (f32[5,24,128]{2,1,0:T(8,128)S(1)}, f32[5,24,128]{2,1,0:T(8,128)S(1)}, u32[]{:S(2)}, u32[]{:S(2)}) collective-permute-start(f32[5,24,128]{2,1,0:T(8,128)S(1)} %get-tuple-element.65), channel_id=1, source_target_pairs={{0,17},{1,16},{2,19},{3,18},{16,1},{17,0},{18,3},{19,2},{4,21},{5,... | collective-permute-start | bytes 184328 | tf_op jit(solution)/shard_map/ppermute | solution.py:792
  175.1 7.6 %collective-permute-start.29 = (f32[5,24,128]{2,1,0:T(8,128)S(1)}, f32[5,24,128]{2,1,0:T(8,128)S(1)}, u32[]{:S(2)}, u32[]{:S(2)}) collective-permute-start(f32[5,24,128]{2,1,0:T(8,128)S(1)} %get-tuple-element.65), channel_id=1, source_target_pairs={{0,1},{1,0},{2,3},{3,2},{4,5},{5,4},{6,7},{7,6},{8,9},{9,8},{10,11... | collective-permute-start | bytes 184328 | tf_op jit(solution)/shard_map/ppermute | solution.py:791
  177.9 7.3 %collective-permute-start.32 = (f32[5,24,128]{2,1,0:T(8,128)S(1)}, f32[5,24,128]{2,1,0:T(8,128)S(1)}, u32[]{:S(2)}, u32[]{:S(2)}) collective-permute-start(f32[5,24,128]{2,1,0:T(8,128)S(1)} %get-tuple-element.66), channel_id=1, source_target_pairs={{0,19},{1,18},{2,17},{3,16},{16,3},{17,2},{18,1},{19,0},{4,23},{5,... | collective-permute-start | bytes 184328 | tf_op jit(solution)/shard_map/ppermute | solution.py:792
  (44 other events, 497.4 us)
where the time goes:
time: 208 us; the launch traced here: 206 us
  starting transfers between devices  86.7 us (42%)
  Pallas kernels  54.5 us (26%)
  waiting for transfers between devices  44.9 us (22%)
  local copies, waits for them, and re-layouts  16.5 us (8%)
  between operations  2.34 us (1%)
    ppermute x16, starting transfers between devices, shifted(): return lax.ppermute(block, axis, route)  43.9 us
    pallas_call x2, Pallas kernels, member_step(): call(functools.partial(step_body, channels, n_mem, scale, last), out_shap...  25.3 us
    ppermute x14, starting transfers between devices, swap(): lax.ppermute(block, axis, [(i, partner(i, count)) for i in range(count)])  19.8 us
    ppermute x8, starting transfers between devices, swap(): lax.ppermute(block, ('mem', axis), [(m * count + i, (1 - m) * count + par...  18.8 us
    ppermute x16, waiting for transfers between devices, shifted(): return lax.ppermute(block, axis, route)  17.2 us
    ppermute x14, waiting for transfers between devices, swap(): lax.ppermute(block, axis, [(i, partner(i, count)) for i in range(count)])  15.6 us
    unnamed x59, local copies, waits for them, and re-layouts  12.6 us
    pallas_call x1, Pallas kernels, first_rest(): call(functools.partial(first_rest_body, channels, n_mem), [jax.ShapeDtype...  7.26 us
  transfers between devices with their start and end apart: 39, of which 16 were waited for; matrix products, arithmetic and copies ran while one was open for 2% of the time, Pallas kernels for 9%

commit v1 on v0

--- a/solution.py
+++ b/solution.py
@@ -23,34 +23,36 @@
 VMEM_CAP = 28 * 2**20
 
 
-def four_passes(inside):
+def passes(inside, times=4):
     count = len(inside)
     step = np.zeros((count, count))
     for i in range(count):
         for j in range(count):
             if inside[i] and inside[j]:
                 step[i, j] = 2.0 if i == j else (9.0 if abs(i - j) == 1 else 0.0)
-    return np.linalg.matrix_power(step, 4)
+    return np.linalg.matrix_power(step, times)
 
 
 def lat_table(lat, parts):
     rows = []
     for part in range(parts):
         placed = part * lat + np.arange(-4, lat + 4)
-        full = four_passes((placed >= 0) & (placed < lat * parts))
+        full = passes((placed >= 0) & (placed < lat * parts))
         rows.append(full[:, 4 : 4 + lat])
     return np.stack(rows).astype(np.float32)
 
 
-def lon_table(lon, parts):
+def lon_table(lon, parts, times):
     kinds = []
-    order = np.concatenate(
-        [EDGE + np.arange(lon), np.tile(np.concatenate([np.arange(EDGE), EDGE + lon + np.arange(EDGE)]), SLOTS)]
-    )
+    own, slot = EDGE + np.arange(lon), np.concatenate([np.arange(EDGE), EDGE + lon + np.arange(EDGE)])
+    out = np.concatenate([own, np.tile(slot, SLOTS)])
     for part in (0, 1, parts - 1) if parts > 2 else range(parts):
         placed = part * lon + np.arange(-EDGE, lon + EDGE)
-        full = four_passes((placed >= 0) & (placed < lon * parts))
-        kinds.append(full[np.ix_(order, order)])
+        full = passes((placed >= 0) & (placed < lon * parts), times)[:, out]
+        high = full.astype(jnp.bfloat16)
+        low = (full - high.astype(np.float64)).astype(jnp.bfloat16)
+        none = np.zeros((lon - 3 * SLOT, len(out)), jnp.bfloat16)
+        kinds.append(np.concatenate([high[own], high[own], low[own], high[slot], high[slot], low[slot], none]))
     return np.stack(kinds)
 
 
@@ -61,10 +63,6 @@
 
 def dot(a, b, dims=(((1,), (0,)), ((), ()))):
     return lax.dot_general(a, b, dims, preferred_element_type=F32)
-
-
-def dot3(high, low, weights_high, weights_low):
-    return dot(high, weights_high) + dot(low, weights_high) + dot(high, weights_low)
 
 
 def lane_of(shape):
@@ -106,8 +104,9 @@
     return total
 
 
-def beside(from_left, from_right):
-    return jnp.where(lane_of(from_left.shape) % SLOT < EDGE, from_left, from_right)
+def beside(odd, from_a, from_b):
+    first = jnp.where(lane_of(from_a.shape) % SLOT < EDGE, odd, 1.0 - odd) > 0.5
+    return jnp.where(first, from_a, from_b)
 
 
 def narrow(x):
@@ -170,89 +169,91 @@
     return get
 
 
-def put_split(high_ref, low_ref, rows, columns, value):
+def put_main(ref, rows, value):
     high, low = split(value)
-    high_ref[rows, columns] = high
-    low_ref[rows, columns] = low
-
-
-def put_side(high_ref, low_ref, first, rows, group, value, slots):
+    ref[rows, :LANES] = high
+    ref[rows, LANES : 2 * LANES] = low
+    ref[rows, 2 * LANES : 3 * LANES] = high
+
+
+def put_side(ref, first, group, value, slots):
+    high = value.astype(BF16).astype(F32)
+    low = value - high
+    slot = slot_of(value.shape)
     for j in range(slots):
-        at = slice(first + j * group + rows[0], first + j * group + rows[1])
-        part = jnp.where(slot_of(value.shape) == j, value, 0.0)
-        put_split(high_ref, low_ref, at, slice(LANES, 2 * LANES), part)
-
-
-def prepare_body(channels, x_ref, t_ref, a_ref, ax_ref, ta_ref, tx_ref):
+        there = 0.0
+        for at, piece in enumerate((high, low, high)):
+            there = jnp.where(slot == at, pltpu.roll(piece, (SLOT * (at - j)) % LANES, 1) if at != j else piece, there)
+        ref[pl.ds(first + j * group, value.shape[0]), 3 * LANES :] = there.astype(BF16)
+
+
+def prepare_body(channels, x_ref, t_ref, a_ref, ax_ref, ta_ref):
+    step = pl.program_id(0)
     lats, rows, _ = a_ref.shape
     part = rows // SLOTS
     for l in range(lats):
         x = x_ref[pl.ds(l, rows, stride=lats), :]
         a_ref[l] = x
-        ax_ref[l] = edges([x[j * part : (j + 1) * part] for j in range(SLOTS)])
-
-    @pl.when(pl.program_id(0) == 0)
+        at = pl.ds(pl.multiple_of(step * part, part), part)
+        ax_ref[l, at, :] = edges([x[j * part : (j + 1) * part] for j in range(SLOTS)])
+
+    @pl.when(step == 0)
     def _():
         for l in range(lats):
             t = t_ref[pl.ds(l, channels, stride=lats), :]
             ta_ref[l] = t
-            tx_ref[l] = edges([t])
+            ax_ref[l, pl.ds(pl.num_programs(0) * part, channels), :] = edges([t])
 
 
 def prepare(x, t, lats, channels, step_rows):
     lon = x.shape[1]
     rows = x.shape[0] // lats
     sds = lambda *shape: jax.ShapeDtypeStruct(shape, F32)
-    block = lambda n: pl.BlockSpec((lats, n, lon), lambda i: (0, i, 0))
-    fixed = pl.BlockSpec((lats, channels, lon), lambda i: (0, 0, 0))
+    whole = lambda *shape: pl.BlockSpec(shape, lambda i: (0,) * len(shape))
+    packed = (lats, rows // SLOTS + channels, lon)
     return call(
         functools.partial(prepare_body, channels),
-        (sds(lats, rows, lon), sds(lats, rows // SLOTS, lon), sds(lats, channels, lon), sds(lats, channels, lon)),
+        (sds(lats, rows, lon), sds(*packed), sds(lats, channels, lon)),
         grid=(rows // step_rows,),
         in_specs=[
             pl.BlockSpec((step_rows * lats, lon), lambda i: (i, 0)),
-            pl.BlockSpec(t.shape, lambda i: (0, 0)),
+            whole(*t.shape),
         ],
-        out_specs=(block(step_rows), block(step_rows // SLOTS), fixed, fixed),
+        out_specs=(pl.BlockSpec((lats, step_rows, lon), lambda i: (0, i, 0)), whole(*packed), whole(lats, channels, lon)),
         flops=x.size * 4,
         nbytes=x.size * 9,
     )(x, t)
 
 
-def filter_rows(main, side, high_ref, low_ref, weights, lats, count, slots):
-    group = count // slots
-    for l in range(lats):
-        put_split(high_ref, low_ref, slice(l * count, (l + 1) * count), slice(0, LANES), main[l])
-        put_side(high_ref, low_ref, l * count, (0, group), group, side[l], slots)
-    return dot3(high_ref[: lats * count, :], low_ref[: lats * count, :], *weights)
-
-
-def first_own_body(
-    channels, n_mem, lat_ref, am, al, ar, po, tm, tl, tr, tpo, bh, bl, z_out, zt_out, e_ref, x_ref, xt_ref, hi, lo, acc
-):
+def first_own_body(channels, n_mem, lat_ref, flag, am, aa, ab, po, tm, ta, tb, tpo, w_ref, z_out, zt_out, e_ref, x_ref, h, acc):
     step = pl.program_id(0)
     lats, rows, _ = am.shape
     members = rows // channels
-    weights = bh[...], bl[...]
+    weights = w_ref[...]
     part = rows // SLOTS
     own = range(4, 4 + lats)
 
+    def filtered(main, side, count, slots):
+        for l in range(lats):
+            put_main(h, slice(l * count, (l + 1) * count), main[l])
+            put_side(h, l * count, count // slots, side(l), slots)
+        return dot(h[: lats * count, :], weights)
+
     @pl.when(step == 0)
     def _():
-        side = [beside(tl[l], tr[l]) for l in range(lats)]
-        z = filter_rows([tm[l] for l in range(lats)], side, hi, lo, weights, lats, channels, 1)
+        z = filtered(tm, lambda l: beside(flag[LEFT_A], ta[l], tb[l]), channels, 1)
         for l in range(lats):
             zt_out[l] = z[l * channels : (l + 1) * channels]
         out = forward_rows(lat_ref, lambda l: zt_out[l], lambda l12: tpo[l12 - 4], lats, own)
         for l, value in enumerate(out):
             acc[l] = value * (1.0 / n_mem)
-            xt_ref[l] = edges([tpo[l]])
-
-    side = [beside(al[l], ar[l]) for l in range(lats)]
-    z = filter_rows([am[l] for l in range(lats)], side, hi, lo, weights, lats, rows, SLOTS)
+            x_ref[l, pl.ds(pl.num_programs(0) * part, channels), :] = edges([tpo[l]])
+
+    z = filtered(am, lambda l: beside(flag[LEFT_A], aa[l], ab[l]), rows, SLOTS)
     for l in range(lats):
         z_out[l] = z[l * rows : (l + 1) * rows]
-        x_ref[l] = edges([po[l, j * part : (j + 1) * part, :] for j in range(SLOTS)])
+        at = pl.ds(pl.multiple_of(step * part, part), part)
+        x_ref[l, at, :] = edges([po[l, j * part : (j + 1) * part, :] for j in range(SLOTS)])
 
     def one(k, sums):
         sel = pl.ds(pl.multiple_of(k * channels, channels), channels)
@@ -268,30 +269,32 @@
         e_ref[...] = acc[...]
 
 
-def first_own(lat_w, a, a_sides, t, t_sides, p_own, lon_h, lon_l, channels, n_mem, step_rows):
+def first_own(lat_w, flags, a, a_sides, t, p_own, weights, channels, n_mem, step_rows):
     lats, rows, lon = a.shape
     part = step_rows // SLOTS
     mb = pl.BlockSpec((lats, step_rows, lon), lambda i: (0, i, 0))
     sb = pl.BlockSpec((lats, part, lon), lambda i: (0, i, 0))
     fb = pl.BlockSpec((lats, channels, lon), lambda i: (0, 0, 0))
     tb = pl.BlockSpec((lats, channels, lon), lambda i: (0, rows // channels, 0))
-    wb = pl.BlockSpec((2 * lon, lon), lambda i: (0, 0))
+    tsb = pl.BlockSpec((lats, channels, lon), lambda i: (0, rows // SLOTS // channels, 0))
     sds = lambda *shape: jax.ShapeDtypeStruct(shape, F32)
+    whole = lambda *shape: pl.BlockSpec(shape, lambda i: (0,) * len(shape))
     fixed = sds(lats, channels, lon)
+    packed = (lats, rows // SLOTS + channels, lon)
     return call(
         functools.partial(first_own_body, channels, n_mem),
-        (sds(lats, rows, lon), fixed, fixed, sds(lats, rows // SLOTS, lon), fixed),
+        (sds(lats, rows, lon), fixed, fixed, sds(*packed)),
         grid=(rows // step_rows,),
-        in_specs=[smem(), mb, sb, sb, mb, fb, fb, fb, tb, wb, wb],
-        out_specs=(mb, fb, fb, sb, fb),
-        scratch_shapes=[pltpu.VMEM((lats * step_rows, 2 * lon), BF16)] * 2 + [pltpu.VMEM((lats, channels, lon), F32)],
+        in_specs=[smem(), smem(), mb, sb, sb, mb, fb, tsb, tsb, tb, whole(*weights.shape)],
+        out_specs=(mb, fb, fb, whole(*packed)),
+        scratch_shapes=[pltpu.VMEM((lats * step_rows, 4 * lon), BF16), pltpu.VMEM((lats, channels, lon), F32)],
         flops=lats * rows * lon * 100,
         nbytes=a.size * 16,
-    )(lat_w, a, *a_sides, p_own, t, *t_sides, p_own, lon_h, lon_l)
+    )(lat_w, flags, a, *a_sides, p_own, t, *a_sides, p_own, weights)
 
 
 def first_rest_body(
-    channels, n_mem, lat_ref, start, z_in, zt, pu, pd, tpu_, tpd, e_in, eo_ref, ea_ref, eb_ref, ec_ref, x_ref, xt_ref, acc
+    channels, n_mem, lat_ref, start, z_in, zt, pu, pd, tpu_, tpd, e_in, eo_ref, ea_ref, eb_ref, ec_ref, x_ref, acc
 ):
     step = pl.program_id(0)
     lats, rows, lon = z_in.shape
@@ -309,10 +312,11 @@
         acc[8 + lats] = jnp.zeros((channels, lon), F32)
         for i, (l12, value) in enumerate(zip(halo, out)):
             acc[l12] = value * (1.0 / n_mem)
-            xt_ref[i] = edges([get(tpu_, tpd, l12, slice(None))])
+            x_ref[i, pl.ds(pl.num_programs(0) * part, channels), :] = edges([get(tpu_, tpd, l12, slice(None))])
 
     for i, l12 in enumerate(halo):
-        x_ref[i] = edges([get(pu, pd, l12, slice(j * part, (j + 1) * part)) for j in range(SLOTS)])
+        at = pl.ds(pl.multiple_of(step * part, part), part)
+        x_ref[i, at, :] = edges([get(pu, pd, l12, slice(j * part, (j + 1) * part)) for j in range(SLOTS)])
 
     def one(k, sums):
         sel = pl.ds(pl.multiple_of(k * channels, channels), channels)
@@ -332,20 +336,17 @@
 
 def first_rest(lat_w, starts, z, zt, p_up, p_down, e_own, channels, n_mem, step_rows):
     lats, rows, lon = z.shape
-    part = step_rows // SLOTS
     mb = pl.BlockSpec((lats, step_rows, lon), lambda i: (0, i, 0))
     fb = pl.BlockSpec((lats, channels, lon), lambda i: (0, 0, 0))
     tb = pl.BlockSpec((lats, channels, lon), lambda i: (0, rows // channels, 0))
     whole = lambda *shape: pl.BlockSpec(shape, lambda i: (0,) * len(shape))
-    shapes = [(lats + 1, channels, lon)] * 3 + [(1, channels, lon)]
+    shapes = [(lats + 1, channels, lon)] * 3 + [(1, channels, lon), (8, rows // SLOTS + channels, lon)]
     return call(
         functools.partial(first_rest_body, channels, n_mem),
-        [jax.ShapeDtypeStruct(shape, F32) for shape in shapes]
-        + [jax.ShapeDtypeStruct((8, rows // SLOTS, lon), F32), jax.ShapeDtypeStruct((8, channels, lon), F32)],
+        [jax.ShapeDtypeStruct(shape, F32) for shape in shapes],
         grid=(rows // step_rows,),
         in_specs=[smem(), smem(), mb, fb, mb, mb, tb, tb, fb],
-        out_specs=[whole(*shape) for shape in shapes]
-        + [pl.BlockSpec((8, part, lon), lambda i: (0, i, 0)), whole(8, channels, lon)],
+        out_specs=[whole(*shape) for shape in shapes],
         scratch_shapes=[pltpu.VMEM((lats + 9, channels, lon), F32)],
         flops=lats * rows * lon * 60,
         nbytes=z.size * 14,
@@ -355,91 +356,62 @@
 ABOVE_A, BELOW_A, ABOVE_B, BELOW_B, TWO_BELOW, TWO_ABOVE, LEFT_A, RIGHT_A, LEFT_B, RIGHT_B = range(10)
 
 
-def load_g(flag, ga, gb, gc, go, gm_ref, gs_ref, lats, channels):
-    above = lambda l: flag[ABOVE_A] * ga[l] + flag[ABOVE_B] * gb[l]
-    below = lambda l: flag[BELOW_A] * ga[l] + flag[BELOW_B] * gb[l]
+def load_g(flag, g_refs, gm_ref, gs_ref, lats, channels, before=None):
+    def rows_of(refs, l12):
+        ga, gb, gc, go = refs
+        above = lambda l: flag[ABOVE_A] * ga[l] + flag[ABOVE_B] * gb[l]
+        below = lambda l: flag[BELOW_A] * ga[l] + flag[BELOW_B] * gb[l]
+        if l12 < 4:
+            return above(l12) + flag[TWO_ABOVE] * gc[0] if l12 == 0 else above(l12)
+        if l12 < 4 + lats:
+            return go[l12 - 4] + above(lats) if l12 == 4 else go[l12 - 4]
+        return below(l12 - 4 - lats) + go[lats] if l12 == 4 + lats else below(l12 - 4 - lats)
+
     for l12 in range(lats + 8):
-        if l12 < 4:
-            value = above(l12)
-            if l12 == 0:
-                value = value + flag[TWO_ABOVE] * gc[0]
-        elif l12 < 4 + lats:
-            value = go[l12 - 4]
-            if l12 == 4:
-                value = value + above(lats)
-        else:
-            value = below(l12 - 4 - lats)
-            if l12 == 4 + lats:
-                value = value + go[lats]
+        value = rows_of(g_refs, l12)
+        if before is not None:
+            value = value + (1.0 - descent) * rows_of(before, l12)
         gm_ref[l12] = value[:channels]
         gs_ref[l12] = widen(value[channels:])
 
 
 def step_body(channels, n_mem, scale, last, *refs):
-    lat_ref, flag, start, ga, gb, gc, go = refs[:7]
-    am, ax = refs[7], refs[8 : 8 + (2 if not last else 1)]
-    refs = refs[8 + len(ax) :]
-    p_main, p_sides = refs[:3], refs[3:7]
-    tm, tx = refs[7], refs[8 : 8 + len(ax)]
-    refs = refs[8 + len(ax) :]
-    tp_main, tp_sides = refs[:3], refs[3:7]
-    bh, bl = refs[7:9]
-    refs = refs[9:]
+    lat_ref, flag, start = refs[:3]
+    g_refs, refs = refs[3:7], refs[7:]
+    before = None
     if last:
-        am_out, tm_out, gm_ref, gs_ref, rh, rl = refs
+        before, am, tm, refs = refs[:4], refs[4], refs[5], refs[6:]
+    p_main, p_sides, tp_main, tp_sides, w_ref = refs[:3], refs[3:7], refs[7:10], refs[10:14], refs[14]
+    refs = refs[15:]
+    if last:
+        am_out, tm_out, gm_ref, gs_ref, h = refs
     else:
-        am_out, as_out, tm_out, ts_out, eo_ref, ea_ref, eb_ref, ec_ref = refs[:8]
-        gm_ref, gs_ref, rh, rl, zm_ref, zs_ref, acc_m, acc_s = refs[8:]
+        eo_ref, ea_ref, eb_ref, ec_ref, gm_ref, gs_ref, h, zm_ref, zs_ref, acc_m, acc_s = refs
     step = pl.program_id(0)
     lats, rows, lon = p_main[0].shape
     members = rows // channels
     part = rows // SLOTS
-    weights = bh[...], bl[...]
-    side_units = part // channels
+    weights = w_ref[...]
+    odd = flag[LEFT_A]
     unroll = 2 if members % 2 == 0 else 1
 
     def side_get(sides, l12, sel):
         if 4 <= l12 < 4 + lats:
-            return beside(sides[0][l12 - 4, sel, :], sides[1][l12 - 4, sel, :])
+            return beside(odd, sides[0][l12 - 4, sel, :], sides[1][l12 - 4, sel, :])
         i = l12 if l12 < 4 else l12 - lats
-        return beside(sides[2][i, sel, :], sides[3][i, sel, :])
+        return beside(odd, sides[2][i, sel, :], sides[3][i, sel, :])
 
     def adjoint_main(p, k, count):
         sel = pl.ds(pl.multiple_of(k * channels, channels), channels)
         out = adjoint_rows(lat_ref, lambda l12: p(l12, sel), lambda l12: gm_ref[l12], lats)
         for l, value in enumerate(out):
-            at = pl.ds(pl.multiple_of(l * count + k * channels, channels), channels)
-            put_split(rh, rl, at, slice(0, lon), value)
+            put_main(h, pl.ds(pl.multiple_of(l * count + k * channels, channels), channels), value)
 
     def adjoint_side(sides, unit, count, slots):
         sel = slice(unit * channels, (unit + 1) * channels)
         out = adjoint_rows(lat_ref, lambda l12: side_get(sides, l12, sel), lambda l12: gs_ref[l12], lats)
         for l, value in enumerate(out):
-            put_side(rh, rl, l * count, (sel.start, sel.stop), count // slots, value, slots)
-
-    def update(main, side, main_put, side_put, count, slots):
-        group = count // slots
-        grad = dot3(rh[: lats * count, :], rl[: lats * count, :], *weights)
-        new_main, new_side = [], []
-        for l in range(lats):
-            at = slice(l * count, (l + 1) * count)
-            new_main.append((1.0 - descent) * main(l) - scale * grad[at, :lon])
-            main_put(l, new_main[l])
-            if not last:
-                found = grad[at, lon:]
-                found = pick_slots(found, group) if slots > 1 else found
-                new_side.append((1.0 - descent) * side(l) - scale * found)
-                side_put(l, new_side[l])
-        if not last:
-            z = filter_rows(new_main, new_side, rh, rl, weights, lats, count, slots)
-            for l in range(lats):
-                at = slice(l * count, (l + 1) * count)
-                zm_ref[l, :count, :] = z[at, :lon]
-                found = z[at, lon:]
-                if slots > 1:
-                    zs_ref[l, :group, :] = pick_slots(found, group)
-                else:
-                    zs_ref[l, :group, :] = jnp.where(slot_of(found.shape) == 0, found, 0.0)
+            put_side(h, l * count + unit * channels, count // slots, value, slots)
 
     def forward_side(sides, unit, share=None):
         sel = slice(unit * channels, (unit + 1) * channels)
@@ -447,32 +419,35 @@
         for l12, value in enumerate(out):
             acc_s[l12] += value if share is None else value * share
 
-    def put_rows(ref):
-        def put(l, value):
-            ref[pl.ds(l, value.shape[0], stride=lats), :] = value
-
-        return put
-
-    def put_lat(ref):
-        def put(l, value):
-            ref[l] = value
-
-        return put
+    def filtered(count, slots):
+        found = dot(h[: lats * count, :], weights)
+        for l in range(lats):
+            at = slice(l * count, (l + 1) * count)
+            zm_ref[l, :count, :] = found[at, :lon]
+            side = found[at, lon:]
+            if slots > 1:
+                zs_ref[l, : count // slots, :] = pick_slots(side, count // slots)
+            else:
+                zs_ref[l, :count, :] = jnp.where(slot_of(side.shape) == 0, side, 0.0)
+
+    def finish(source, out_ref, count):
+        found = dot(h[: lats * count, :], weights)
+        for l in range(lats):
+            new = (1.0 - descent) ** 2 * source[l] - scale * found[l * count : (l + 1) * count]
+            out_ref[pl.ds(l, count, stride=lats), :] = new
 
     p = p_getter(p_main, lats)
 
     @pl.when(step == 0)
     def _():
-        load_g(flag, ga, gb, gc, go, gm_ref, gs_ref, lats, channels)
+        load_g(flag, g_refs, gm_ref, gs_ref, lats, channels, before)
         tp = p_getter(tp_main, lats)
         adjoint_main(tp, 0, channels)
         adjoint_side(tp_sides, 0, channels, 1)
         if last:
-            update(lambda l: tm[l], None, put_rows(tm_out), None, channels, 1)
+            finish(tm, tm_out, channels)
         else:
-            update(
-                lambda l: tm[l], lambda l: beside(tx[0][l], tx[1][l]), put_lat(tm_out), put_lat(ts_out), channels, 1
-            )
+            filtered(channels, 1)
             acc_m[...] = jnp.zeros_like(acc_m)
             acc_s[...] = jnp.zeros_like(acc_s)
             out = forward_rows(lat_ref, lambda l: zm_ref[l, :channels, :], lambda l12: tp(l12, slice(None)), lats)
@@ -481,12 +456,12 @@
             forward_side(tp_sides, 0, 1.0 / n_mem)
 
     lax.fori_loop(0, members, lambda k, c: (adjoint_main(p, k, rows), c)[1], 0, unroll=unroll)
-    for unit in range(side_units):
+    for unit in range(part // channels):
         adjoint_side(p_sides, unit, rows, SLOTS)
     if last:
-        update(lambda l: am[l], None, put_rows(am_out), None, rows, SLOTS)
+        finish(am, am_out, rows)
     else:
-        update(lambda l: am[l], lambda l: beside(ax[0][l], ax[1][l]), put_lat(am_out), put_lat(as_out), rows, SLOTS)
+        filtered(rows, SLOTS)
 
         def one(k, sums):
             sel = pl.ds(pl.multiple_of(k * channels, channels), channels)
@@ -496,7 +471,7 @@
         sums = lax.fori_loop(0, members, one, tuple(acc_m[l12] for l12 in range(lats + 8)), unroll=unroll)
         for l12, value in enumerate(sums):
             acc_m[l12] = value
-        for unit in range(side_units):
+        for unit in range(part // channels):
             forward_side(p_sides, unit)
 
         @pl.when(step == pl.num_programs(0) - 1)
@@ -507,47 +482,41 @@
                     ref[r, channels:, :] = narrow(repeat_slots(acc_s[first + r]))
 
 
-def member_step(
-    lat_w, flags, starts, g4, a, a_sides, t, t_sides, p3, x4, xt4, lon_h, lon_l, channels, n_mem, scale, last, step_rows
-):
-    lats, rows, lon = a.shape
+def member_step(lat_w, flags, starts, g4, p3, x4, weights, channels, n_mem, step_rows, final=None):
+    last = final is not None
+    lats, total, lon = p3[0].shape
+    rows = total - channels
     part = step_rows // SLOTS
     mb = pl.BlockSpec((lats, step_rows, lon), lambda i: (0, i, 0))
-    sb = pl.BlockSpec((lats, part, lon), lambda i: (0, i, 0))
     fb = pl.BlockSpec((lats, channels, lon), lambda i: (0, 0, 0))
     tpb = pl.BlockSpec((lats, channels, lon), lambda i: (0, rows // channels, 0))
-    xb = pl.BlockSpec((8, part, lon), lambda i: (0, i, 0))
-    width = lon if last else 2 * lon
-    wb = pl.BlockSpec((2 * lon, width), lambda i: (0, 0))
+    xb = [pl.BlockSpec((n, part, lon), lambda i: (0, i, 0)) for n in (lats, lats, 8, 8)]
+    txb = [pl.BlockSpec((n, channels, lon), lambda i: (0, rows // SLOTS // channels, 0)) for n in (lats, lats, 8, 8)]
     whole = lambda shape: pl.BlockSpec(shape, lambda i: (0,) * len(shape))
     sds = lambda *shape: jax.ShapeDtypeStruct(shape, F32)
     half = channels + channels // 2
-    scratch = [pltpu.VMEM((lats + 8, channels, lon), F32)] * 2 + [pltpu.VMEM((lats * step_rows, 2 * lon), BF16)] * 2
+    gb = [whole(g.shape) for g in g4]
+    scratch = [pltpu.VMEM((lats + 8, channels, lon), F32)] * 2 + [pltpu.VMEM((lats * step_rows, 4 * lon), BF16)]
     if last:
         out_shape = [sds(rows * lats, lon), sds(channels * lats, lon)]
         out_specs = [pl.BlockSpec((step_rows * lats, lon), lambda i: (i, 0)), whole((channels * lats, lon))]
+        extra, extra_specs, scale = [*final[0], *final[1:3]], gb + [mb, fb], final[3]
     else:
-        out_shape = [sds(lats, rows, lon), sds(lats, rows // SLOTS, lon)] + [sds(lats, channels, lon)] * 2
-        out_specs = [mb, sb, fb, fb]
-        for count in (lats + 1, lats + 1, lats + 1, 1):
-            out_shape.append(sds(count, half, lon))
-            out_specs.append(whole((count, half, lon)))
+        out_shape = [sds(count, half, lon) for count in (lats + 1, lats + 1, lats + 1, 1)]
+        out_specs = [whole(shape.shape) for shape in out_shape]
+        extra, extra_specs, scale = [], [], None
         scratch += [pltpu.VMEM((lats, step_rows, lon), F32), pltpu.VMEM((lats, max(part, channels), lon), F32)]
         scratch += [pltpu.VMEM((lats + 9, channels, lon), F32)] * 2
     return call(
         functools.partial(step_body, channels, n_mem, scale, last),
         out_shape,
         grid=(rows // step_rows,),
-        in_specs=[smem()] * 3
-        + [whole(g.shape) for g in g4]
-        + [mb] + [sb] * len(a_sides)
-        + [mb, mb, mb, sb, sb, xb, xb, fb] + [fb] * len(t_sides)
-        + [tpb, tpb, tpb] + [whole(x.shape) for x in xt4] + [wb, wb],
+        in_specs=[smem()] * 3 + gb + extra_specs + [mb] * 3 + xb + [tpb] * 3 + txb + [whole(weights.shape)],
         out_specs=out_specs,
         scratch_shapes=scratch,
-        flops=lats * rows * lon * 800,
-        nbytes=a.size * 40,
-    )(lat_w, flags, starts, *g4, a, *a_sides, *p3, *x4, t, *t_sides, *p3, *xt4, lon_h, lon_l)
+        flops=lats * rows * lon * 600,
+        nbytes=rows * lats * lon * 24,
+    )(lat_w, flags, starts, *g4, *extra, *p3, *x4, *p3, *x4, weights)
 
 
 FIELDS = 24
@@ -595,7 +564,7 @@
     )(tile, coef, weight, cell[None], value[None], precision[None])
 
 
-def index_body(channels, here_ref, left_ref, right_ref, main_ref, side_ref, record_ref, beside_ref):
+def index_body(channels, flag, here_ref, a_ref, b_ref, main_ref, side_ref, record_ref, beside_ref):
     groups = here_ref.shape[0]
     lon = LANES
 
@@ -614,17 +583,18 @@
         row, column = base_of(block)
         mark(main_ref, at, row * lon + column)
         record_ref[:, at] = block
-        block = left_ref[group]
-        row, column = base_of(block)
-        mark(side_ref, at, jnp.where(column >= lon - EDGE + 2, row * SLOT + column - (lon - EDGE), -1))
-        beside_ref[:, at] = block
-        block = right_ref[group]
-        row, column = base_of(block)
-        mark(side_ref, far, jnp.where(column < EDGE - 2, row * SLOT + EDGE + column, -1))
-        beside_ref[:, far] = block
-
-
-def index(here, left, right, channels, lats, lon):
+        for ref, to, left, right in ((a_ref, at, LEFT_A, RIGHT_A), (b_ref, far, LEFT_B, RIGHT_B)):
+            block = ref[group]
+            row, column = base_of(block)
+            from_left = jnp.where(column >= lon - EDGE + 2, row * SLOT + column - (lon - EDGE), -1)
+            from_right = jnp.where(column < EDGE - 2, row * SLOT + EDGE + column, -1)
+            is_left = jnp.full(row.shape, flag[left]) > 0.5
+            is_right = jnp.full(row.shape, flag[right]) > 0.5
+            mark(side_ref, to, jnp.where(is_left, from_left, jnp.where(is_right, from_right, -1)))
+            beside_ref[:, to] = block
+
+
+def index(flags, here, from_a, from_b, channels, lats, lon):
     slots = here.shape[0] * LANES
     assert lon == 128
     return call(
@@ -635,11 +605,11 @@
             jax.ShapeDtypeStruct((FIELDS, slots), F32),
             jax.ShapeDtypeStruct((FIELDS, 2 * slots), F32),
         ),
-        in_specs=[vmem()] * 3,
+        in_specs=[smem()] + [vmem()] * 3,
         out_specs=(vmem(),) * 4,
         flops=lats * lon * slots * 4,
         nbytes=lats * lon * slots * 2,
-    )(here, left, right)
+    )(flags, here, from_a, from_b)
 
 
 def stacked_split(value):
@@ -647,8 +617,8 @@
     return jnp.concatenate([high, value - high], 0).astype(BF16)
 
 
-def obs_body(channels, ens_scale, first, flag, *refs):
-    s_refs, refs = refs[: 3 if first else 8], refs[3 if first else 8 :]
+def obs_body(channels, ens_scale, step_scale, first, flag, *refs):
+    s_refs, refs = refs[: 3 if first else 9], refs[3 if first else 9 :]
     ohm_ref, ohs_ref, record_ref, beside_ref, g_ref, g1_ref, dx_ref = refs
     lats = g_ref.shape[0] - 1
     lon = g_ref.shape[2]
@@ -664,17 +634,21 @@
             edge = pltpu.roll(jnp.where(lane < EDGE, right, left), EDGE, 1)
             b = ens_scale * repeat_slots(jnp.where(slot == 0, edge, 0.0))
         else:
-            own, other, na, na2, nb, nb2, nc, nc2 = s_refs
+            earlier, own, other, na, na2, nb, nb2, nc, nc2 = s_refs
             total = own[r] + other[r]
             total = total + (flag[ABOVE_A] + flag[BELOW_A]) * (na[r] + na2[r])
             total = total + (flag[ABOVE_B] + flag[BELOW_B]) * (nb[r] + nb2[r])
             if r == lats:
                 total = total + flag[TWO_BELOW] * (nc[0] + nc2[0])
-            a = ens_scale * total[:channels]
-            b = ens_scale * widen(total[channels:])
+            total = (1.0 - descent) * earlier[r] - (step_scale * ens_scale) * total
+            a = total[:channels]
+            b = widen(total[channels:])
         main.append(a)
         side.append(b)
-        if r < lats:
+        if first:
+            dx_ref[r, :channels, :] = a
+            dx_ref[r, channels:, :] = narrow(b)
+        elif r < lats:
             dx_ref[pl.ds(r, channels, stride=lats), :] = a
         next_main.append(jnp.where(lane == lon - 1, pltpu.roll(b, lon - 1 - EDGE, 1), pltpu.roll(a, lon - 1, 1)))
 
@@ -751,16 +725,18 @@
             g1_ref[0, channels:, :] = edge
 
 
-def observe(flags, sums, records, channels, ens_scale, lats):
+def observe(flags, sums, records, channels, ens_scale, step_scale, lats):
     lon = sums[0].shape[2]
     slots = records[0].shape[1]
     half = channels + channels // 2
+    first = len(sums) == 3
+    dx_shape = (lats + 1, half, lon) if first else (lats * channels, lon)
     return call(
-        functools.partial(obs_body, channels, ens_scale, len(sums) == 3),
+        functools.partial(obs_body, channels, ens_scale, step_scale, first),
         (
             jax.ShapeDtypeStruct((lats + 1, half, lon), F32),
             jax.ShapeDtypeStruct((1, half, lon), F32),
-            jax.ShapeDtypeStruct((lats * channels, lon), F32),
+            jax.ShapeDtypeStruct(dx_shape, F32),
         ),
         in_specs=[smem()] + [vmem()] * (len(sums) + 4),
         out_specs=(vmem(),) * 3,
@@ -836,7 +812,7 @@
     assert n_mem == 2 and n_gx % 2 == 0 and n_gy % 2 == 0
     ens_scale = ens_share / math.sqrt(members * n_mem - 1)
     rows = members * channels
-    step_rows = 8 * channels
+    step_rows = (16 if members % 16 == 0 else 8) * channels
 
     def lat_major(x, count):
         return x.reshape(count, lats, lon).transpose(1, 0, 2)
@@ -850,14 +826,14 @@
     )
     p_up, p_down = shifted(p_own, "gy", 1), shifted(p_own, "gy", -1)
     p3 = (p_up, p_own, p_down)
-    a, a_edges, t, t_edges = prepare(
+    a, a_edges, t = prepare(
         alpha.reshape(rows * lats, lon), static_control.reshape(channels * lats, lon), lats, channels, step_rows
     )
 
     def from_beside(x):
-        return shifted(x, "gx", 1), shifted(x, "gx", -1)
-
-    a_sides, t_sides = from_beside(a_edges), from_beside(t_edges)
+        return swap(x, "gx", partner_a), swap(x, "gx", partner_b)
+
+    a_sides = from_beside(a_edges)
 
     x, y = lax.axis_index("gx"), lax.axis_index("gy")
     odd = y % 2 == 1
@@ -891,43 +867,34 @@
     arrived = lax.all_to_all(sent, ("gx", "gy"), split_axis=0, concat_axis=0, tiled=True)
     if per_group > 1:
         arrived = arrived.reshape(-1, per_group, FIELDS, capacity).transpose(0, 2, 1, 3).reshape(-1, FIELDS, LANES)
-    from_left, from_right = from_beside(arrived)
-    records = index(arrived, from_left, from_right, channels, lats, lon)
+    records = index(flags, arrived, *from_beside(arrived), channels, lats, lon)
 
     lat_w = jnp.asarray(lat_table(lats, n_gy) * (4.0 / PASS / PASS))[y].reshape(-1)
     kind = jnp.where(x == 0, 0, jnp.where(x == n_gx - 1, min(n_gx, 3) - 1, 1))
-    table = lon_table(lon, n_gx)
-    table_high = table.astype(jnp.bfloat16)
-    table_low = (table - table_high.astype(np.float64)).astype(jnp.bfloat16)
-    lon_h, lon_l = jnp.asarray(table_high)[kind], jnp.asarray(table_low)[kind]
-
-    z, zt, e_own, x_own, xt_own = first_own(
-        lat_w, a, a_sides, t, t_sides, p_own, lon_h[:, :lon], lon_l[:, :lon], channels, n_mem, step_rows
-    )
-    x_own, xt_own = from_beside(x_own), from_beside(xt_own)
-    *e4, x_rest, xt_rest = first_rest(lat_w, starts, z, zt, p_up, p_down, e_own, channels, n_mem, step_rows)
+    own_weights = jnp.asarray(lon_table(lon, n_gx, 4)[:, :, :lon])[kind]
+    twice_weights = jnp.asarray(lon_table(lon, n_gx, 8))[kind]
+
+    z, zt, e_own, x_own = first_own(lat_w, flags, a, a_sides, t, p_own, own_weights, channels, n_mem, step_rows)
+    z, records = lax.optimization_barrier((z, records))
+    *e4, x_rest = first_rest(lat_w, starts, z, zt, p_up, p_down, e_own, channels, n_mem, step_rows)
     own, own2, na, na2, nb, nb2, nc, nc2 = gather_rows(*e4)
     s = own + own2 + (na + na2) + (flags[ABOVE_B] + flags[BELOW_B]) * (nb + nb2)
     s = s + jnp.concatenate([jnp.zeros_like(s[:lats]), flags[TWO_BELOW] * (nc + nc2)], 0)
-    s, x_rest, xt_rest = lax.optimization_barrier((s, x_rest, xt_rest))
+    s, x_rest = lax.optimization_barrier((s, x_rest))
     sums = (s, swap(s, "gx", partner_a), swap(s, "gx", partner_b))
-    x_rest, xt_rest = from_beside(x_rest), from_beside(xt_rest)
-    x4, xt4 = (*x_own, *x_rest), (*xt_own, *xt_rest)
-    g, g_over, _ = observe(flags, sums, records, channels, ens_scale, lats)
+    x4 = (*from_beside(x_own), *from_beside(x_rest))
+    scale = descent * ens_scale
+    g, g_over, dx = observe(flags, sums, records, channels, ens_scale, scale, lats)
 
     def gather_g(g, g_over):
         return swap(g, "gy", partner_a), swap(g, "gy", partner_b), two_away(g_over, 2), g
 
-    scale = descent * ens_scale
-    a, a_side, t, t_side, *e4 = member_step(
-        lat_w, flags, starts, gather_g(g, g_over), a, a_sides, t, t_sides, p3, x4, xt4, lon_h, lon_l,
-        channels, n_mem, scale, False, step_rows,
-    )
-    sums = gather_rows(*e4)
-    g, g_over, dx = observe(flags, sums, records, channels, ens_scale, lats)
+    g0 = gather_g(g, g_over)
+    sums = gather_rows(*member_step(lat_w, flags, starts, g0, p3, x4, twice_weights, channels, n_mem, step_rows))
+    g, g_over, dx = observe(flags, (dx, *sums), records, channels, ens_scale, scale, lats)
+    g1 = gather_g(g, g_over)
     a, t = member_step(
-        lat_w, flags, starts, gather_g(g, g_over), a, (a_side,), t, (t_side,), p3, x4, xt4, lon_h[:, :lon], lon_l[:, :lon],
-        channels, n_mem, scale, True, step_rows,
+        lat_w, flags, starts, g1, p3, x4, own_weights, channels, n_mem, step_rows, final=(g0, a, t, scale)
     )
     return (
         a.reshape(alpha.shape),

time: 208 us -> 187 us (0.90)
  waiting for transfers between devices: 44.9 us -> 84 us
  starting transfers between devices: 86.7 us -> 50.3 us
  Pallas kernels: 54.5 us -> 40.7 us
  local copies, waits for them, and re-layouts: 16.5 us -> 7.97 us
    ppermute x16 -> x2, starting transfers between devices: 43.9 us -> 7.74 us  [shifted(): return lax.ppermute(block, axis, route)]
    all_to_all x1, waiting for transfers between devices: 6.75 us -> 35 us  [assimilate(): lax.all_to_all(sent, ('gx', 'gy'), split_axis=0, concat_axis=0, tiled=True)]
    ppermute x14 -> x22, waiting for transfers between devices: 15.6 us -> 43.6 us  [swap(): lax.ppermute(block, axis, [(i, partner(i, count)) for i in range(count)])]
    ppermute x16 -> x2, waiting for transfers between devices: 17.2 us -> 0.01 us  [shifted(): return lax.ppermute(block, axis, route)]
    unnamed x59 -> x25, local copies, waits for them, and re-layouts: 12.6 us -> 3.18 us
    pallas_call x2, Pallas kernels: 25.3 us -> 17.4 us  [member_step(): call(functools.partial(step_body, channels, n_mem, scale, last), out_shap...]
    ppermute x8, starting transfers between devices: 18.8 us -> 14.4 us  [swap(): lax.ppermute(block, ('mem', axis), [(m * count + i, (1 - m) * count + par...]
    all_to_all x1, starting transfers between devices: 4.18 us -> 7.08 us  [assimilate(): lax.all_to_all(sent, ('gx', 'gy'), split_axis=0, concat_axis=0, tiled=True)]
  transfers between devices with their start and end apart: 39 -> 33, of which waited for: 16 -> 9; matrix products, arithmetic and copies ran while one was open for 2% -> 2% of each run, Pallas kernels for 9% -> 8%
where the time goes in v1:
time: 187 us; the launch traced here: 186 us
  waiting for transfers between devices  84 us (45%)
  starting transfers between devices  50.3 us (27%)
  Pallas kernels  40.7 us (22%)
  local copies, waits for them, and re-layouts  7.97 us (4%)
  between operations  2.28 us (1%)
    ppermute x22, waiting for transfers between devices, swap(): lax.ppermute(block, axis, [(i, partner(i, count)) for i in range(count)])  43.6 us
    all_to_all x1, waiting for transfers between devices, assimilate(): lax.all_to_all(sent, ('gx', 'gy'), split_axis=0, concat_axis=0, tiled=True)  35 us
    ppermute x22, starting transfers between devices, swap(): lax.ppermute(block, axis, [(i, partner(i, count)) for i in range(count)])  21 us
    pallas_call x2, Pallas kernels, member_step(): call(functools.partial(step_body, channels, n_mem, scale, last), out_shap...  17.4 us
    ppermute x8, starting transfers between devices, swap(): lax.ppermute(block, ('mem', axis), [(m * count + i, (1 - m) * count + par...  14.4 us
    ppermute x2, starting transfers between devices, shifted(): return lax.ppermute(block, axis, route)  7.74 us
    all_to_all x1, starting transfers between devices, assimilate(): lax.all_to_all(sent, ('gx', 'gy'), split_axis=0, concat_axis=0, tiled=True)  7.08 us
    pallas_call x2, Pallas kernels, observe(): call(functools.partial(obs_body, channels, ens_scale, step_scale, first),...  6.59 us
  transfers between devices with their start and end apart: 33, of which 9 were waited for; matrix products, arithmetic and copies ran while one was open for 2% of the time, Pallas kernels for 8%

profile of v1, /device:TPU:0, one launch (start us, length us, event | category | flops | bytes accessed | tf_op | source)
XLA Modules:
  0.0 186.2 jit_solution(7173860320718723216)
XLA Ops:
  2.3 6.5 %collective-permute-start.4 = (f32[4,1040,128]{2,1,0:T(8,128)S(1)}, f32[4,1040,128]{2,1,0:T(8,128)}, u32[]{:S(2)}, u32[]{:S(2)}) collective-permute-start(f32[4,1040,128]{2,1,0:T(8,128)S(1)} %pad_maximum_fusion.po.tpo.refs_8_.refs_15_.refs_14_.refs_21_), channel_id=1, source_target_pairs={{0,1},{1,2},{2,3},{4,5},{5,6},{6,7},{8,9},{9,10},{10,11},{12,13},{... | collective-permute-start | bytes 6389768 | tf_op jit(solution)/shard_map/ppermute | solution.py:753
  10.1 1.9 %shard_map.148 = (f32[4,1024,128]{2,1,0:T(8,128)S(1)}, f32[4,272,128]{2,1,0:T(8,128)}, f32[4,16,128]{2,1,0:T(8,128)S(1)}) custom-call(f32[4096,128]{1,0:T(8,128)S(1)} %bitcast.33, f32[64,128]{1,0:T(8,128)S(1)} %bitcast.34), custom_call_target="tpu_custom_call" | custom-call | flops 2097152 | bytes 4718592 | tf_op jit(solution)/shard_map/pallas_call | solution.py:214
  13.6 4.1 %shard_map.150 = f32[16,24,128]{2,1,0:T(8,128)} custom-call(s32[1024,1]{1,0:T(8,128)S(1)} %copy.21.tile_ref, f32[16,1024]{1,0:T(8,128)S(1)} %bitcast.35, f32[4,1024]{1,0:T(4,128)S(1)} %copy-done.6, s32[1,1024]{1,0:T(1,128)S(1)} %bitcast.36, f32[1,1024]{1,0:T(1,128)S(1)} %bitcast.37, f32[1,1024]{1,0:T(1,128)S(1)} %bitcast.38), custom_call_target="tpu_custom_call" | custom-call | flops 314572800 | bytes 409600 | tf_op jit(solution)/shard_map/pallas_call | solution.py:557
  17.7 7.1 %all-to-all-start = ((f32[16,24,128]{2,1,0:T(8,128)}), f32[16,24,128]{2,1,0:T(8,128)S(1)}, u32[]{:S(2)}, u32[]{:S(2)}) async-start(f32[16,24,128]{2,1,0:T(8,128)} %shard_map.150), calls=%async_computation | async-start | bytes 393216 | tf_op jit(solution)/shard_map/all_to_all | solution.py:867
  27.4 35.0 %all-to-all-done.here_ref = f32[16,24,128]{2,1,0:T(8,128)S(1)} async-done(((f32[16,24,128]{2,1,0:T(8,128)}), f32[16,24,128]{2,1,0:T(8,128)S(1)}, u32[]{:S(2)}, u32[]{:S(2)}) %all-to-all-start) | async-done | bytes 196640 | tf_op jit(solution)/shard_map/all_to_all | solution.py:867
  66.2 4.5 %shard_map.149 = (f32[4,1024,128]{2,1,0:T(8,128)S(1)}, f32[4,16,128]{2,1,0:T(8,128)S(1)}, f32[4,16,128]{2,1,0:T(8,128)S(1)}, f32[4,272,128]{2,1,0:T(8,128)S(1)}) custom-call(f32[48]{0:T(128)S(1)} %reshape_squeeze.3.lat_ref.refs_0_, f32[10]{0:T(128)S(1)} %convert_element_type.4.flag.refs_1_, f32[4,1024,128]{2,1,0:T(8,128)S(1)} %copy-done.1, ...), custom_call_target="tpu_custom_call" | custom-call | flops 52428800 | bytes 8388608 | tf_op jit(solution)/shard_map/pallas_call | solution.py:284
  72.3 4.7 %shard_map.152 = (f32[5,16,128]{2,1,0:T(8,128)S(1)}, f32[5,16,128]{2,1,0:T(8,128)S(1)}, f32[5,16,128]{2,1,0:T(8,128)S(1)}, f32[1,16,128]{2,1,0:T(8,128)S(1)}, f32[8,272,128]{2,1,0:T(8,128)S(1)}) custom-call(f32[48]{0:T(128)S(1)} %reshape_squeeze.3.lat_ref.refs_0_, s32[2]{0:T(128)S(1)} %add_select_fusion.start.refs_2_, ...), custom_call_target="tpu_custom_call" | custom-call | flops 31457280 | bytes 7340032 | tf_op jit(solution)/shard_map/pallas_call | solution.py:344
  77.8 3.2 %collective-permute-start.12 = (f32[1,16,128]{2,1,0:T(8,128)S(1)}, f32[1,16,128]{2,1,0:T(8,128)S(1)}, u32[]{:S(2)}, u32[]{:S(2)}) collective-permute-start(f32[1,16,128]{2,1,0:T(8,128)S(1)} %get-tuple-element.52), channel_id=1, source_target_pairs={{0,18},{1,19},{2,16},{3,17},{16,2},{17,3},{18,0},{19,1},{4,22},{5,... | collective-permute-start | bytes 24584 | tf_op jit(solution)/shard_map/ppermute | solution.py:768
  86.0 3.6 %collective-permute-start.9 = (f32[5,16,128]{2,1,0:T(8,128)S(1)}, f32[5,16,128]{2,1,0:T(8,128)S(1)}, u32[]{:S(2)}, u32[]{:S(2)}) collective-permute-start(f32[5,16,128]{2,1,0:T(8,128)S(1)} %get-tuple-element.51), channel_id=1, source_target_pairs={{0,3},{1,2},{2,1},{3,0},{4,7},{5,6},{6,5},{7,4},{8,11},{9,10},{10,... | collective-permute-start | bytes 122888 | tf_op jit(solution)/shard_map/ppermute | solution.py:767
  91.6 2.1 %collective-permute-done.6 = f32[5,16,128]{2,1,0:T(8,128)S(1)} collective-permute-done((f32[5,16,128]{2,1,0:T(8,128)S(1)}, f32[5,16,128]{2,1,0:T(8,128)S(1)}, u32[]{:S(2)}, u32[]{:S(2)}) %collective-permute-start.6) | collective-permute-done | bytes 40992 | tf_op jit(solution)/shard_map/ppermute | solution.py:768
  98.0 34.9 %collective-permute-done.14.refs_2_ = f32[5,16,128]{2,1,0:T(8,128)S(1)} collective-permute-done((f32[5,16,128]{2,1,0:T(8,128)S(1)}, f32[5,16,128]{2,1,0:T(8,128)S(1)}, u32[]{:S(2)}, u32[]{:S(2)}) %collective-permute-start.14) | collective-permute-done | bytes 40992 | tf_op jit(solution)/shard_map/ppermute | solution.py:767
  132.9 3.1 %shard_map.153 = (f32[5,24,128]{2,1,0:T(8,128)S(1)}, f32[1,24,128]{2,1,0:T(8,128)S(1)}, f32[5,24,128]{2,1,0:T(8,128)S(1)}) custom-call(f32[10]{0:T(128)S(1)} %convert_element_type.4.flag.refs_1_, f32[5,16,128]{2,1,0:T(8,128)S(1)} %pad_add_fusion.refs_0_, f32[5,16,128]{2,1,0:T(8,128)S(1)} %collective-permute-done.13.refs_1_, ...), custom_call_target="tpu_custom_call" | custom-call | flops 805306368 | bytes 4194304 | tf_op jit(solution)/shard_map/pallas_call | solution.py:734
  136.1 1.8 collective-permute-start.16
  140.6 3.0 %collective-permute-done.17.refs_5_.refs_9_ = f32[1,24,128]{2,1,0:T(8,128)S(1)} collective-permute-done((f32[1,24,128]{2,1,0:T(8,128)S(1)}, f32[1,24,128]{2,1,0:T(8,128)S(1)}, u32[]{:S(2)}, u32[]{:S(2)}) %collective-permute-start.17) | collective-permute-done | bytes 12320 | tf_op jit(solution)/shard_map/ppermute | solution.py:767
  143.5 9.5 %shard_map.154 = (f32[5,24,128]{2,1,0:T(8,128)S(1)}, f32[5,24,128]{2,1,0:T(8,128)S(1)}, f32[5,24,128]{2,1,0:T(8,128)S(1)}, f32[1,24,128]{2,1,0:T(8,128)S(1)}) custom-call(f32[48]{0:T(128)S(1)} %reshape_squeeze.3.lat_ref.refs_0_, f32[10]{0:T(128)S(1)} %convert_element_type.4.flag.refs_1_, s32[2]{0:T(128)S(1)} %add_select_fusion.start.refs_2_, ...), custom_call_target="tpu_custom_call" | custom-call | flops 314572800 | bytes 12582912 | tf_op jit(solution)/shard_map/pallas_call | solution.py:510
  153.9 2.1 %collective-permute-start.28 = (f32[1,24,128]{2,1,0:T(8,128)S(1)}, f32[1,24,128]{2,1,0:T(8,128)S(1)}, u32[]{:S(2)}, u32[]{:S(2)}) collective-permute-start(f32[1,24,128]{2,1,0:T(8,128)S(1)} %get-tuple-element.67), channel_id=1, source_target_pairs={{0,18},{1,19},{2,16},{3,17},{16,2},{17,3},{18,0},{19,1},{4,22},{5,... | collective-permute-start | bytes 36872 | tf_op jit(solution)/shard_map/ppermute | solution.py:768
  156.4 2.6 %collective-permute-start.24 = (f32[5,24,128]{2,1,0:T(8,128)S(1)}, f32[5,24,128]{2,1,0:T(8,128)S(1)}, u32[]{:S(2)}, u32[]{:S(2)}) collective-permute-start(f32[5,24,128]{2,1,0:T(8,128)S(1)} %get-tuple-element.65), channel_id=1, source_target_pairs={{0,17},{1,16},{2,19},{3,18},{16,1},{17,0},{18,3},{19,2},{4,21},{5,... | collective-permute-start | bytes 184328 | tf_op jit(solution)/shard_map/ppermute | solution.py:768
  159.5 1.8 collective-permute-start.25
  161.3 3.0 %collective-permute-start.26 = (f32[5,24,128]{2,1,0:T(8,128)S(1)}, f32[5,24,128]{2,1,0:T(8,128)S(1)}, u32[]{:S(2)}, u32[]{:S(2)}) collective-permute-start(f32[5,24,128]{2,1,0:T(8,128)S(1)} %get-tuple-element.66), channel_id=1, source_target_pairs={{0,19},{1,18},{2,17},{3,16},{16,3},{17,2},{18,1},{19,0},{4,23},{5,... | collective-permute-start | bytes 184328 | tf_op jit(solution)/shard_map/ppermute | solution.py:768
  165.6 2.6 %collective-permute-done.26.refs_6_ = f32[5,24,128]{2,1,0:T(8,128)S(1)} collective-permute-done((f32[5,24,128]{2,1,0:T(8,128)S(1)}, f32[5,24,128]{2,1,0:T(8,128)S(1)}, u32[]{:S(2)}, u32[]{:S(2)}) %collective-permute-start.26) | collective-permute-done | bytes 61472 | tf_op jit(solution)/shard_map/ppermute | solution.py:768
  168.2 3.5 %shard_map.155 = (f32[5,24,128]{2,1,0:T(8,128)S(1)}, f32[1,24,128]{2,1,0:T(8,128)S(1)}, f32[64,128]{1,0:T(8,128)}) custom-call(f32[10]{0:T(128)S(1)} %convert_element_type.4.flag.refs_1_, f32[5,24,128]{2,1,0:T(8,128)S(1)} %get-tuple-element.59.refs_0_, f32[5,24,128]{2,1,0:T(8,128)S(1)} %get-tuple-element.64.refs_1_, ...), custom_call_target="tpu_custom_call" | custom-call | flops 805306368 | bytes 4194304 | tf_op jit(solution)/shard_map/pallas_call | solution.py:734
  171.7 2.1 %collective-permute-start.30 = (f32[5,24,128]{2,1,0:T(8,128)S(1)}, f32[5,24,128]{2,1,0:T(8,128)S(1)}, u32[]{:S(2)}, u32[]{:S(2)}) collective-permute-start(f32[5,24,128]{2,1,0:T(8,128)S(1)} %get-tuple-element.68.refs_6_), channel_id=1, source_target_pairs={{0,3},{1,2},{2,1},{3,0},{4,7},{5,6},{6,5},{7,4},{8,11},{9,10},{10,... | collective-permute-start | bytes 184328 | tf_op jit(solution)/shard_map/ppermute | solution.py:767
  175.2 3.2 %collective-permute-done.31.refs_5_ = f32[1,24,128]{2,1,0:T(8,128)S(1)} collective-permute-done((f32[1,24,128]{2,1,0:T(8,128)S(1)}, f32[1,24,128]{2,1,0:T(8,128)S(1)}, u32[]{:S(2)}, u32[]{:S(2)}) %collective-permute-start.31) | collective-permute-done | bytes 12320 | tf_op jit(solution)/shard_map/ppermute | solution.py:767
  178.4 7.8 %shard_map.156 = (f32[4096,128]{1,0:T(8,128)}, f32[64,128]{1,0:T(8,128)}) custom-call(f32[48]{0:T(128)S(1)} %reshape_squeeze.3.lat_ref.refs_0_, f32[10]{0:T(128)S(1)} %convert_element_type.4.flag.refs_1_, s32[2]{0:T(128)S(1)} %add_select_fusion.start.refs_2_, f32[5,24,128]{2,1,0:T(8,128)S(1)} %collective-permute-done.29.refs_3_, ...), custom_call_target="tpu_custom_call" | custom-call | flops 314572800 | bytes 12582912 | tf_op jit(solution)/shard_map/pallas_call | solution.py:510
  (90 shorter events, 30.3 us)
Async XLA Ops:
  2.3 69.9 %collective-permute-start.4 = (f32[4,1040,128]{2,1,0:T(8,128)S(1)}, f32[4,1040,128]{2,1,0:T(8,128)}, u32[]{:S(2)}, u32[]{:S(2)}) collective-permute-start(f32[4,1040,128]{2,1,0:T(8,128)S(1)} %pad_maximum_fusion.po.tpo.refs_8_.refs_15_.refs_14_.refs_21_), channel_id=1, source_target_pairs={{0,1},{1,2},{2,3},{4,5},{5,6},{6,7},{8,9},{9,10},{10,11},{12,13},{... | collective-permute-start | bytes 6389768 | tf_op jit(solution)/shard_map/ppermute | solution.py:753
  8.8 63.5 %collective-permute-start.5 = (f32[4,1040,128]{2,1,0:T(8,128)S(1)}, f32[4,1040,128]{2,1,0:T(8,128)}, u32[]{:S(2)}, u32[]{:S(2)}) collective-permute-start(f32[4,1040,128]{2,1,0:T(8,128)S(1)} %pad_maximum_fusion.po.tpo.refs_8_.refs_15_.refs_14_.refs_21_), channel_id=1, source_target_pairs={{1,0},{2,1},{3,2},{5,4},{6,5},{7,6},{9,8},{10,9},{11,10},{13,12},{... | collective-permute-start | bytes 6389768 | tf_op jit(solution)/shard_map/ppermute | solution.py:753
  13.3 49.2 %collective-permute-start = (f32[4,272,128]{2,1,0:T(8,128)}, f32[4,272,128]{2,1,0:T(8,128)S(1)}, u32[]{:S(2)}, u32[]{:S(2)}) collective-permute-start(f32[4,272,128]{2,1,0:T(8,128)} %get-tuple-element.39), channel_id=1, source_target_pairs={{0,4},{4,0},{8,12},{12,8},{1,5},{5,1},{9,13},{13,9},{2,6},{6,2},{1... | collective-permute-start | bytes 1671176 | tf_op jit(solution)/shard_map/ppermute | solution.py:767
  17.7 44.7 %all-to-all-start = ((f32[16,24,128]{2,1,0:T(8,128)}), f32[16,24,128]{2,1,0:T(8,128)S(1)}, u32[]{:S(2)}, u32[]{:S(2)}) async-start(f32[16,24,128]{2,1,0:T(8,128)} %shard_map.150), calls=%async_computation | async-start | bytes 393216 | tf_op jit(solution)/shard_map/all_to_all | solution.py:867
  24.8 39.8 %collective-permute-start.1 = (f32[4,272,128]{2,1,0:T(8,128)}, f32[4,272,128]{2,1,0:T(8,128)S(1)}, u32[]{:S(2)}, u32[]{:S(2)}) collective-permute-start(f32[4,272,128]{2,1,0:T(8,128)} %get-tuple-element.39), channel_id=1, source_target_pairs={{0,12},{4,8},{8,4},{12,0},{1,13},{5,9},{9,5},{13,1},{2,14},{6,10},... | collective-permute-start | bytes 1671176 | tf_op jit(solution)/shard_map/ppermute | solution.py:767
  62.4 8.3 %collective-permute-start.2 = (f32[16,24,128]{2,1,0:T(8,128)S(1)}, f32[16,24,128]{2,1,0:T(8,128)S(1)}, u32[]{:S(2)}, u32[]{:S(2)}) collective-permute-start(f32[16,24,128]{2,1,0:T(8,128)S(1)} %all-to-all-done.here_ref), channel_id=1, source_target_pairs={{0,4},{4,0},{8,12},{12,8},{1,5},{5,1},{9,13},{13,9},{2,6},{6,2},{1... | collective-permute-start | bytes 589832 | tf_op jit(solution)/shard_map/ppermute | solution.py:767
  62.6 8.2 %collective-permute-start.3 = (f32[16,24,128]{2,1,0:T(8,128)S(1)}, f32[16,24,128]{2,1,0:T(8,128)S(1)}, u32[]{:S(2)}, u32[]{:S(2)}) collective-permute-start(f32[16,24,128]{2,1,0:T(8,128)S(1)} %all-to-all-done.here_ref), channel_id=1, source_target_pairs={{0,12},{4,8},{8,4},{12,0},{1,13},{5,9},{9,5},{13,1},{2,14},{6,10},... | collective-permute-start | bytes 589832 | tf_op jit(solution)/shard_map/ppermute | solution.py:767
  77.0 9.0 %collective-permute-start.11 = (f32[1,16,128]{2,1,0:T(8,128)S(1)}, f32[1,16,128]{2,1,0:T(8,128)S(1)}, u32[]{:S(2)}, u32[]{:S(2)}) collective-permute-start(f32[1,16,128]{2,1,0:T(8,128)S(1)} %get-tuple-element.52), channel_id=1, source_target_pairs={{0,2},{1,3},{2,0},{3,1},{4,6},{5,7},{6,4},{7,5},{8,10},{9,11},{10,... | collective-permute-start | bytes 24584 | tf_op jit(solution)/shard_map/ppermute | solution.py:767
  77.8 11.9 %collective-permute-start.12 = (f32[1,16,128]{2,1,0:T(8,128)S(1)}, f32[1,16,128]{2,1,0:T(8,128)S(1)}, u32[]{:S(2)}, u32[]{:S(2)}) collective-permute-start(f32[1,16,128]{2,1,0:T(8,128)S(1)} %get-tuple-element.52), channel_id=1, source_target_pairs={{0,18},{1,19},{2,16},{3,17},{16,2},{17,3},{18,0},{19,1},{4,22},{5,... | collective-permute-start | bytes 24584 | tf_op jit(solution)/shard_map/ppermute | solution.py:768
  82.8 10.8 %collective-permute-start.7 = (f32[5,16,128]{2,1,0:T(8,128)S(1)}, f32[5,16,128]{2,1,0:T(8,128)S(1)}, u32[]{:S(2)}, u32[]{:S(2)}) collective-permute-start(f32[5,16,128]{2,1,0:T(8,128)S(1)} %get-tuple-element.50), channel_id=1, source_target_pairs={{0,1},{1,0},{2,3},{3,2},{4,5},{5,4},{6,7},{7,6},{8,9},{9,8},{10,11... | collective-permute-start | bytes 122888 | tf_op jit(solution)/shard_map/ppermute | solution.py:767
  83.5 10.2 %collective-permute-start.8 = (f32[5,16,128]{2,1,0:T(8,128)S(1)}, f32[5,16,128]{2,1,0:T(8,128)S(1)}, u32[]{:S(2)}, u32[]{:S(2)}) collective-permute-start(f32[5,16,128]{2,1,0:T(8,128)S(1)} %get-tuple-element.50), channel_id=1, source_target_pairs={{0,17},{1,16},{2,19},{3,18},{16,1},{17,0},{18,3},{19,2},{4,21},{5,... | collective-permute-start | bytes 122888 | tf_op jit(solution)/shard_map/ppermute | solution.py:768
  84.9 6.7 %collective-permute-start.10 = (f32[5,16,128]{2,1,0:T(8,128)S(1)}, f32[5,16,128]{2,1,0:T(8,128)S(1)}, u32[]{:S(2)}, u32[]{:S(2)}) collective-permute-start(f32[5,16,128]{2,1,0:T(8,128)S(1)} %get-tuple-element.51), channel_id=1, source_target_pairs={{0,19},{1,18},{2,17},{3,16},{16,3},{17,2},{18,1},{19,0},{4,23},{5,... | collective-permute-start | bytes 122888 | tf_op jit(solution)/shard_map/ppermute | solution.py:768
  86.0 7.6 %collective-permute-start.9 = (f32[5,16,128]{2,1,0:T(8,128)S(1)}, f32[5,16,128]{2,1,0:T(8,128)S(1)}, u32[]{:S(2)}, u32[]{:S(2)}) collective-permute-start(f32[5,16,128]{2,1,0:T(8,128)S(1)} %get-tuple-element.51), channel_id=1, source_target_pairs={{0,3},{1,2},{2,1},{3,0},{4,7},{5,6},{6,5},{7,4},{8,11},{9,10},{10,... | collective-permute-start | bytes 122888 | tf_op jit(solution)/shard_map/ppermute | solution.py:767
  93.7 49.8 %collective-permute-start.20 = (f32[8,272,128]{2,1,0:T(8,128)S(1)}, f32[8,272,128]{2,1,0:T(8,128)S(1)}, u32[]{:S(2)}, u32[]{:S(2)}) collective-permute-start(f32[8,272,128]{2,1,0:T(8,128)S(1)} %get-tuple-element.63), channel_id=1, source_target_pairs={{0,4},{4,0},{8,12},{12,8},{1,5},{5,1},{9,13},{13,9},{2,6},{6,2},{1... | collective-permute-start | bytes 3342344 | tf_op jit(solution)/shard_map/ppermute | solution.py:767
  93.8 49.8 %collective-permute-start.21 = (f32[8,272,128]{2,1,0:T(8,128)S(1)}, f32[8,272,128]{2,1,0:T(8,128)S(1)}, u32[]{:S(2)}, u32[]{:S(2)}) collective-permute-start(f32[8,272,128]{2,1,0:T(8,128)S(1)} %get-tuple-element.63), channel_id=1, source_target_pairs={{0,12},{4,8},{8,4},{12,0},{1,13},{5,9},{9,5},{13,1},{2,14},{6,10},... | collective-permute-start | bytes 3342344 | tf_op jit(solution)/shard_map/ppermute | solution.py:767
  94.8 41.3 %collective-permute-start.18 = (f32[4,272,128]{2,1,0:T(8,128)S(1)}, f32[4,272,128]{2,1,0:T(8,128)S(1)}, u32[]{:S(2)}, u32[]{:S(2)}) collective-permute-start(f32[4,272,128]{2,1,0:T(8,128)S(1)} %get-tuple-element.62), channel_id=1, source_target_pairs={{0,4},{4,0},{8,12},{12,8},{1,5},{5,1},{9,13},{13,9},{2,6},{6,2},{1... | collective-permute-start | bytes 1671176 | tf_op jit(solution)/shard_map/ppermute | solution.py:767
  94.9 43.1 %collective-permute-start.19 = (f32[4,272,128]{2,1,0:T(8,128)S(1)}, f32[4,272,128]{2,1,0:T(8,128)S(1)}, u32[]{:S(2)}, u32[]{:S(2)}) collective-permute-start(f32[4,272,128]{2,1,0:T(8,128)S(1)} %get-tuple-element.62), channel_id=1, source_target_pairs={{0,12},{4,8},{8,4},{12,0},{1,13},{5,9},{9,5},{13,1},{2,14},{6,10},... | collective-permute-start | bytes 1671176 | tf_op jit(solution)/shard_map/ppermute | solution.py:767
  97.4 35.5 %collective-permute-start.14 = (f32[5,16,128]{2,1,0:T(8,128)S(1)}, f32[5,16,128]{2,1,0:T(8,128)S(1)}, u32[]{:S(2)}, u32[]{:S(2)}) collective-permute-start(f32[5,16,128]{2,1,0:T(8,128)S(1)} %pad_add_fusion.refs_0_), channel_id=1, source_target_pairs={{0,12},{4,8},{8,4},{12,0},{1,13},{5,9},{9,5},{13,1},{2,14},{6,10},... | collective-permute-start | bytes 122888 | tf_op jit(solution)/shard_map/ppermute | solution.py:767
  136.0 7.5 %collective-permute-start.15 = (f32[5,24,128]{2,1,0:T(8,128)S(1)}, f32[5,24,128]{2,1,0:T(8,128)S(1)}, u32[]{:S(2)}, u32[]{:S(2)}) collective-permute-start(f32[5,24,128]{2,1,0:T(8,128)S(1)} %get-tuple-element.60.refs_6_.refs_10_), channel_id=1, source_target_pairs={{0,1},{1,0},{2,3},{3,2},{4,5},{5,4},{6,7},{7,6},{8,9},{9,8},{10,11... | collective-permute-start | bytes 184328 | tf_op jit(solution)/shard_map/ppermute | solution.py:767
  136.1 7.4 %collective-permute-start.16 = (f32[5,24,128]{2,1,0:T(8,128)S(1)}, f32[5,24,128]{2,1,0:T(8,128)S(1)}, u32[]{:S(2)}, u32[]{:S(2)}) collective-permute-start(f32[5,24,128]{2,1,0:T(8,128)S(1)} %get-tuple-element.60.refs_6_.refs_10_), channel_id=1, source_target_pairs={{0,3},{1,2},{2,1},{3,0},{4,7},{5,6},{6,5},{7,4},{8,11},{9,10},{10,... | collective-permute-start | bytes 184328 | tf_op jit(solution)/shard_map/ppermute | solution.py:767
  153.9 7.4 %collective-permute-start.28 = (f32[1,24,128]{2,1,0:T(8,128)S(1)}, f32[1,24,128]{2,1,0:T(8,128)S(1)}, u32[]{:S(2)}, u32[]{:S(2)}) collective-permute-start(f32[1,24,128]{2,1,0:T(8,128)S(1)} %get-tuple-element.67), channel_id=1, source_target_pairs={{0,18},{1,19},{2,16},{3,17},{16,2},{17,3},{18,0},{19,1},{4,22},{5,... | collective-permute-start | bytes 36872 | tf_op jit(solution)/shard_map/ppermute | solution.py:768
  156.0 8.3 %collective-permute-start.23 = (f32[5,24,128]{2,1,0:T(8,128)S(1)}, f32[5,24,128]{2,1,0:T(8,128)S(1)}, u32[]{:S(2)}, u32[]{:S(2)}) collective-permute-start(f32[5,24,128]{2,1,0:T(8,128)S(1)} %get-tuple-element.65), channel_id=1, source_target_pairs={{0,1},{1,0},{2,3},{3,2},{4,5},{5,4},{6,7},{7,6},{8,9},{9,8},{10,11... | collective-permute-start | bytes 184328 | tf_op jit(solution)/shard_map/ppermute | solution.py:767
  156.4 7.9 %collective-permute-start.24 = (f32[5,24,128]{2,1,0:T(8,128)S(1)}, f32[5,24,128]{2,1,0:T(8,128)S(1)}, u32[]{:S(2)}, u32[]{:S(2)}) collective-permute-start(f32[5,24,128]{2,1,0:T(8,128)S(1)} %get-tuple-element.65), channel_id=1, source_target_pairs={{0,17},{1,16},{2,19},{3,18},{16,1},{17,0},{18,3},{19,2},{4,21},{5,... | collective-permute-start | bytes 184328 | tf_op jit(solution)/shard_map/ppermute | solution.py:768
  161.3 6.9 %collective-permute-start.26 = (f32[5,24,128]{2,1,0:T(8,128)S(1)}, f32[5,24,128]{2,1,0:T(8,128)S(1)}, u32[]{:S(2)}, u32[]{:S(2)}) collective-permute-start(f32[5,24,128]{2,1,0:T(8,128)S(1)} %get-tuple-element.66), channel_id=1, source_target_pairs={{0,19},{1,18},{2,17},{3,16},{16,3},{17,2},{18,1},{19,0},{4,23},{5,... | collective-permute-start | bytes 184328 | tf_op jit(solution)/shard_map/ppermute | solution.py:768
  (21 other events, 144.6 us)

commit v2 on v1

--- a/solution.py
+++ b/solution.py
@@ -831,7 +831,8 @@
     )
 
     def from_beside(x):
-        return swap(x, "gx", partner_a), swap(x, "gx", partner_b)
+        inner = [(i, partner_b(i, n_gx)) for i in range(n_gx) if abs(i - partner_b(i, n_gx)) == 1]
+        return swap(x, "gx", partner_a), lax.ppermute(x, "gx", inner)
 
     a_sides = from_beside(a_edges)
 
@@ -861,28 +862,30 @@
     sent = route(
         obs_tile, obs_coef.reshape(channels, obs_rows), interp_weights, obs_cell, obs_values, obs_weights, capacity, slots
     )
+    lat_w = jnp.asarray(lat_table(lats, n_gy) * (4.0 / PASS / PASS))[y].reshape(-1)
+    kind = jnp.where(x == 0, 0, jnp.where(x == n_gx - 1, min(n_gx, 3) - 1, 1))
+    own_weights = jnp.asarray(lon_table(lon, n_gx, 4)[:, :, :lon])[kind]
+    twice_weights = jnp.asarray(lon_table(lon, n_gx, 8))[kind]
+
+    z, zt, e_own, x_own = first_own(lat_w, flags, a, a_sides, t, p_own, own_weights, channels, n_mem, step_rows)
+    z, sent = lax.optimization_barrier((z, sent))
+    x_own = from_beside(x_own)
+    *e4, x_rest = first_rest(lat_w, starts, z, zt, p_up, p_down, e_own, channels, n_mem, step_rows)
+    x_rest = from_beside(x_rest)
     per_group = LANES // capacity if capacity < LANES else 1
     if per_group > 1:
         sent = sent.reshape(-1, FIELDS, per_group, capacity).transpose(0, 2, 1, 3).reshape(tile_count, FIELDS, capacity)
     arrived = lax.all_to_all(sent, ("gx", "gy"), split_axis=0, concat_axis=0, tiled=True)
     if per_group > 1:
         arrived = arrived.reshape(-1, per_group, FIELDS, capacity).transpose(0, 2, 1, 3).reshape(-1, FIELDS, LANES)
-    records = index(flags, arrived, *from_beside(arrived), channels, lats, lon)
-
-    lat_w = jnp.asarray(lat_table(lats, n_gy) * (4.0 / PASS / PASS))[y].reshape(-1)
-    kind = jnp.where(x == 0, 0, jnp.where(x == n_gx - 1, min(n_gx, 3) - 1, 1))
-    own_weights = jnp.asarray(lon_table(lon, n_gx, 4)[:, :, :lon])[kind]
-    twice_weights = jnp.asarray(lon_table(lon, n_gx, 8))[kind]
-
-    z, zt, e_own, x_own = first_own(lat_w, flags, a, a_sides, t, p_own, own_weights, channels, n_mem, step_rows)
-    z, records = lax.optimization_barrier((z, records))
-    *e4, x_rest = first_rest(lat_w, starts, z, zt, p_up, p_down, e_own, channels, n_mem, step_rows)
+    arrived, e4[0] = lax.optimization_barrier((arrived, e4[0]))
+    arrived_beside = from_beside(arrived)
+    records = index(flags, arrived, *arrived_beside, channels, lats, lon)
     own, own2, na, na2, nb, nb2, nc, nc2 = gather_rows(*e4)
     s = own + own2 + (na + na2) + (flags[ABOVE_B] + flags[BELOW_B]) * (nb + nb2)
     s = s + jnp.concatenate([jnp.zeros_like(s[:lats]), flags[TWO_BELOW] * (nc + nc2)], 0)
-    s, x_rest = lax.optimization_barrier((s, x_rest))
     sums = (s, swap(s, "gx", partner_a), swap(s, "gx", partner_b))
-    x4 = (*from_beside(x_own), *from_beside(x_rest))
+    x4 = (*x_own, *x_rest)
     scale = descent * ens_scale
     g, g_over, dx = observe(flags, sums, records, channels, ens_scale, scale, lats)
 

time: 187 us -> 162 us (0.87)
  the two profiles are of different devices: /device:TPU:0 before, /device:TPU:2 now
where the time goes in v2:
time: 162 us; the launch traced here: 161 us
  starting transfers between devices  54.9 us (34%)
  waiting for transfers between devices  48.7 us (30%)
  Pallas kernels  39.5 us (24%)
  local copies, waits for them, and re-layouts  14.7 us (9%)
  between operations  2.37 us (1%)
    ppermute x2, waiting for transfers between devices, shifted(): return lax.ppermute(block, axis, route)  19.9 us
    pallas_call x2, Pallas kernels, member_step(): call(functools.partial(step_body, channels, n_mem, scale, last), out_shap...  16.8 us
    ppermute x8, starting transfers between devices, swap(): lax.ppermute(block, ('mem', axis), [(m * count + i, (1 - m) * count + par...  15.5 us
    ppermute x18, starting transfers between devices, swap(): lax.ppermute(block, axis, [(i, partner(i, count)) for i in range(count)])  14.9 us
    ppermute x4, waiting for transfers between devices, from_beside(): return (swap(x, 'gx', partner_a), lax.ppermute(x, 'gx', inner))  14.7 us
    ppermute x18, waiting for transfers between devices, swap(): lax.ppermute(block, axis, [(i, partner(i, count)) for i in range(count)])  11.4 us
    ppermute x4, starting transfers between devices, from_beside(): return (swap(x, 'gx', partner_a), lax.ppermute(x, 'gx', inner))  10.8 us
    unnamed x39, local copies, waits for them, and re-layouts  9.79 us
  transfers between devices with their start and end apart: 33, of which 11 were waited for; matrix products, arithmetic and copies ran while one was open for 3% of the time, Pallas kernels for 12%

profile of v2, /device:TPU:2, one launch (start us, length us, event | category | flops | bytes accessed | tf_op | source)
XLA Modules:
  0.0 161.0 jit_solution(101865460626003483)
XLA Ops:
  2.3 5.0 %collective-permute-start.2 = (f32[4,1040,128]{2,1,0:T(8,128)S(1)}, f32[4,1040,128]{2,1,0:T(8,128)}, u32[]{:S(2)}, u32[]{:S(2)}) collective-permute-start(f32[4,1040,128]{2,1,0:T(8,128)S(1)} %pad_maximum_fusion.po.tpo.refs_8_.refs_15_.refs_14_.refs_21_), channel_id=1, source_target_pairs={{0,1},{1,2},{2,3},{4,5},{5,6},{6,7},{8,9},{9,10},{10,11},{12,13},{... | collective-permute-start | bytes 6389768 | tf_op jit(solution)/shard_map/ppermute | solution.py:753
  11.8 2.5 %collective-permute-start.1 = (f32[4,272,128]{2,1,0:T(8,128)}, f32[4,272,128]{2,1,0:T(8,128)S(1)}, u32[]{:S(2)}, u32[]{:S(2)}) collective-permute-start(f32[4,272,128]{2,1,0:T(8,128)} %get-tuple-element.36), channel_id=1, source_target_pairs={{4,8},{8,4},{5,9},{9,5},{6,10},{10,6},{7,11},{11,7},{20,24},{24,20... | collective-permute-start | bytes 1671176 | tf_op jit(solution)/shard_map/ppermute | solution.py:835
  17.4 3.4 %shard_map.150 = f32[16,24,128]{2,1,0:T(8,128)S(1)} custom-call(s32[1024,1]{1,0:T(8,128)S(1)} %copy-done.6, f32[16,1024]{1,0:T(8,128)S(1)} %bitcast.35, f32[4,1024]{1,0:T(4,128)S(1)} %copy-done.13, s32[1,1024]{1,0:T(1,128)S(1)} %bitcast.36, f32[1,1024]{1,0:T(1,128)S(1)} %bitcast.37, f32[1,1024]{1,0:T(1,128)S(1)} %bitcast.38), custom_call_target="tpu_custom_call" | custom-call | flops 314572800 | bytes 409600 | tf_op jit(solution)/shard_map/pallas_call | solution.py:557
  24.5 4.5 %shard_map.149 = (f32[4,1024,128]{2,1,0:T(8,128)S(1)}, f32[4,16,128]{2,1,0:T(8,128)S(1)}, f32[4,16,128]{2,1,0:T(8,128)S(1)}, f32[4,272,128]{2,1,0:T(8,128)S(1)}) custom-call(f32[48]{0:T(128)S(1)} %reshape_squeeze.3.lat_ref.refs_0_, f32[10]{0:T(128)S(1)} %convert_element_type.4.flag.refs_1_, f32[4,1024,128]{2,1,0:T(8,128)S(1)} %copy-done.1, ...), custom_call_target="tpu_custom_call" | custom-call | flops 52428800 | bytes 8388608 | tf_op jit(solution)/shard_map/pallas_call | solution.py:284
  31.1 7.4 %all-to-all-start = ((f32[16,24,128]{2,1,0:T(8,128)}), f32[16,24,128]{2,1,0:T(8,128)S(1)}, u32[]{:S(2)}, u32[]{:S(2)}) async-start(f32[16,24,128]{2,1,0:T(8,128)} %copy-done.7), calls=%async_computation | async-start | bytes 393216 | tf_op jit(solution)/shard_map/all_to_all | solution.py:878
  38.6 14.0 %collective-permute-done.2.pu.tpu_.refs_7_.refs_14_.refs_13_.refs_20_ = f32[4,1040,128]{2,1,0:T(8,128)} collective-permute-done((f32[4,1040,128]{2,1,0:T(8,128)S(1)}, f32[4,1040,128]{2,1,0:T(8,128)}, u32[]{:S(2)}, u32[]{:S(2)}) %collective-permute-start.2) | collective-permute-done | bytes 2129952 | tf_op jit(solution)/shard_map/ppermute | solution.py:753
  52.7 5.9 %collective-permute-done.3.pd.tpd.refs_9_.refs_16_.refs_15_.refs_22_ = f32[4,1040,128]{2,1,0:T(8,128)} collective-permute-done((f32[4,1040,128]{2,1,0:T(8,128)S(1)}, f32[4,1040,128]{2,1,0:T(8,128)}, u32[]{:S(2)}, u32[]{:S(2)}) %collective-permute-start.3) | collective-permute-done | bytes 2129952 | tf_op jit(solution)/shard_map/ppermute | solution.py:753
  60.1 4.7 %shard_map.151 = (f32[5,16,128]{2,1,0:T(8,128)S(1)}, f32[5,16,128]{2,1,0:T(8,128)S(1)}, f32[5,16,128]{2,1,0:T(8,128)S(1)}, f32[1,16,128]{2,1,0:T(8,128)S(1)}, f32[8,272,128]{2,1,0:T(8,128)S(1)}) custom-call(f32[48]{0:T(128)S(1)} %reshape_squeeze.3.lat_ref.refs_0_, s32[2]{0:T(128)S(1)} %add_select_fusion.start.refs_2_, f32[4,1024,128]{2,1,0:T(8,128)S(1)} %copy-done.5, ...), custom_call_target="tpu_custom_call" | custom-call | flops 31457280 | bytes 7340032 | tf_op jit(solution)/shard_map/pallas_call | solution.py:344
  65.9 2.2 %collective-permute-start.10 = (f32[1,16,128]{2,1,0:T(8,128)S(1)}, f32[1,16,128]{2,1,0:T(8,128)S(1)}, u32[]{:S(2)}, u32[]{:S(2)}) collective-permute-start(f32[1,16,128]{2,1,0:T(8,128)S(1)} %get-tuple-element.47), channel_id=1, source_target_pairs={{0,18},{1,19},{2,16},{3,17},{16,2},{17,3},{18,0},{19,1},{4,22},{5,... | collective-permute-start | bytes 24584 | tf_op jit(solution)/shard_map/ppermute | solution.py:768
  72.8 2.4 %collective-permute-start.6 = (f32[5,16,128]{2,1,0:T(8,128)S(1)}, f32[5,16,128]{2,1,0:T(8,128)S(1)}, u32[]{:S(2)}, u32[]{:S(2)}) collective-permute-start(f32[5,16,128]{2,1,0:T(8,128)S(1)} %get-tuple-element.45), channel_id=1, source_target_pairs={{0,17},{1,16},{2,19},{3,18},{16,1},{17,0},{18,3},{19,2},{4,21},{5,... | collective-permute-start | bytes 122888 | tf_op jit(solution)/shard_map/ppermute | solution.py:768
  75.9 3.1 %collective-permute-start.8 = (f32[5,16,128]{2,1,0:T(8,128)S(1)}, f32[5,16,128]{2,1,0:T(8,128)S(1)}, u32[]{:S(2)}, u32[]{:S(2)}) collective-permute-start(f32[5,16,128]{2,1,0:T(8,128)S(1)} %get-tuple-element.46), channel_id=1, source_target_pairs={{0,19},{1,18},{2,17},{3,16},{16,3},{17,2},{18,1},{19,0},{4,23},{5,... | collective-permute-start | bytes 122888 | tf_op jit(solution)/shard_map/ppermute | solution.py:768
  79.0 2.5 %collective-permute-start.21 = (f32[8,272,128]{2,1,0:T(8,128)}, f32[8,272,128]{2,1,0:T(8,128)S(1)}, u32[]{:S(2)}, u32[]{:S(2)}) collective-permute-start(f32[8,272,128]{2,1,0:T(8,128)} %copy-done.9), channel_id=1, source_target_pairs={{4,8},{8,4},{5,9},{9,5},{6,10},{10,6},{7,11},{11,7},{20,24},{24,20... | collective-permute-start | bytes 3342344 | tf_op jit(solution)/shard_map/ppermute | solution.py:835
  82.4 3.0 %collective-permute-start.19 = (f32[4,272,128]{2,1,0:T(8,128)S(1)}, f32[4,272,128]{2,1,0:T(8,128)S(1)}, u32[]{:S(2)}, u32[]{:S(2)}) collective-permute-start(f32[4,272,128]{2,1,0:T(8,128)S(1)} %copy-done.11), channel_id=1, source_target_pairs={{4,8},{8,4},{5,9},{9,5},{6,10},{10,6},{7,11},{11,7},{20,24},{24,20... | collective-permute-start | bytes 1671176 | tf_op jit(solution)/shard_map/ppermute | solution.py:835
  88.2 2.7 %collective-permute-start.14 = (f32[16,24,128]{2,1,0:T(8,128)S(1)}, f32[16,24,128]{2,1,0:T(8,128)S(1)}, u32[]{:S(2)}, u32[]{:S(2)}) collective-permute-start(f32[16,24,128]{2,1,0:T(8,128)S(1)} %all-to-all-done.here_ref), channel_id=1, source_target_pairs={{4,8},{8,4},{5,9},{9,5},{6,10},{10,6},{7,11},{11,7},{20,24},{24,20... | collective-permute-start | bytes 589832 | tf_op jit(solution)/shard_map/ppermute | solution.py:835
  90.9 13.7 %collective-permute-done.14.b_ref = f32[16,24,128]{2,1,0:T(8,128)S(1)} collective-permute-done((f32[16,24,128]{2,1,0:T(8,128)S(1)}, f32[16,24,128]{2,1,0:T(8,128)S(1)}, u32[]{:S(2)}, u32[]{:S(2)}) %collective-permute-start.14) | collective-permute-done | bytes 196640 | tf_op jit(solution)/shard_map/ppermute | solution.py:835
  108.0 3.1 %shard_map.153 = (f32[5,24,128]{2,1,0:T(8,128)S(1)}, f32[1,24,128]{2,1,0:T(8,128)S(1)}, f32[5,24,128]{2,1,0:T(8,128)S(1)}) custom-call(f32[10]{0:T(128)S(1)} %convert_element_type.4.flag.refs_1_, f32[5,16,128]{2,1,0:T(8,128)S(1)} %pad_add_fusion.refs_0_, f32[5,16,128]{2,1,0:T(8,128)S(1)} %collective-permute-done.11.refs_1_, ...), custom_call_target="tpu_custom_call" | custom-call | flops 805306368 | bytes 4194304 | tf_op jit(solution)/shard_map/pallas_call | solution.py:734
  112.1 2.6 %collective-permute-start.17 = (f32[1,24,128]{2,1,0:T(8,128)S(1)}, f32[1,24,128]{2,1,0:T(8,128)S(1)}, u32[]{:S(2)}, u32[]{:S(2)}) collective-permute-start(f32[1,24,128]{2,1,0:T(8,128)S(1)} %get-tuple-element.55), channel_id=1, source_target_pairs={{0,2},{1,3},{2,0},{3,1},{4,6},{5,7},{6,4},{7,5},{8,10},{9,11},{10,... | collective-permute-start | bytes 36872 | tf_op jit(solution)/shard_map/ppermute | solution.py:767
  115.7 2.4 %collective-permute-done.17.refs_5_.refs_9_ = f32[1,24,128]{2,1,0:T(8,128)S(1)} collective-permute-done((f32[1,24,128]{2,1,0:T(8,128)S(1)}, f32[1,24,128]{2,1,0:T(8,128)S(1)}, u32[]{:S(2)}, u32[]{:S(2)}) %collective-permute-start.17) | collective-permute-done | bytes 12320 | tf_op jit(solution)/shard_map/ppermute | solution.py:767
  118.1 9.2 %shard_map.154 = (f32[5,24,128]{2,1,0:T(8,128)S(1)}, f32[5,24,128]{2,1,0:T(8,128)S(1)}, f32[5,24,128]{2,1,0:T(8,128)S(1)}, f32[1,24,128]{2,1,0:T(8,128)S(1)}) custom-call(f32[48]{0:T(128)S(1)} %reshape_squeeze.3.lat_ref.refs_0_, f32[10]{0:T(128)S(1)} %convert_element_type.4.flag.refs_1_, s32[2]{0:T(128)S(1)} %add_select_fusion.start.refs_2_, ...), custom_call_target="tpu_custom_call" | custom-call | flops 314572800 | bytes 12582912 | tf_op jit(solution)/shard_map/pallas_call | solution.py:510
  128.6 2.5 %collective-permute-start.28 = (f32[1,24,128]{2,1,0:T(8,128)S(1)}, f32[1,24,128]{2,1,0:T(8,128)S(1)}, u32[]{:S(2)}, u32[]{:S(2)}) collective-permute-start(f32[1,24,128]{2,1,0:T(8,128)S(1)} %get-tuple-element.61), channel_id=1, source_target_pairs={{0,18},{1,19},{2,16},{3,17},{16,2},{17,3},{18,0},{19,1},{4,22},{5,... | collective-permute-start | bytes 36872 | tf_op jit(solution)/shard_map/ppermute | solution.py:768
  140.7 2.7 %collective-permute-done.26.refs_6_ = f32[5,24,128]{2,1,0:T(8,128)S(1)} collective-permute-done((f32[5,24,128]{2,1,0:T(8,128)S(1)}, f32[5,24,128]{2,1,0:T(8,128)S(1)}, u32[]{:S(2)}, u32[]{:S(2)}) %collective-permute-start.26) | collective-permute-done | bytes 61472 | tf_op jit(solution)/shard_map/ppermute | solution.py:768
  143.4 3.5 %shard_map.155 = (f32[5,24,128]{2,1,0:T(8,128)S(1)}, f32[1,24,128]{2,1,0:T(8,128)S(1)}, f32[64,128]{1,0:T(8,128)}) custom-call(f32[10]{0:T(128)S(1)} %convert_element_type.4.flag.refs_1_, f32[5,24,128]{2,1,0:T(8,128)S(1)} %get-tuple-element.53.refs_0_, f32[5,24,128]{2,1,0:T(8,128)S(1)} %get-tuple-element.58.refs_1_, ...), custom_call_target="tpu_custom_call" | custom-call | flops 805306368 | bytes 4194304 | tf_op jit(solution)/shard_map/pallas_call | solution.py:734
  150.4 3.0 %collective-permute-done.31.refs_5_ = f32[1,24,128]{2,1,0:T(8,128)S(1)} collective-permute-done((f32[1,24,128]{2,1,0:T(8,128)S(1)}, f32[1,24,128]{2,1,0:T(8,128)S(1)}, u32[]{:S(2)}, u32[]{:S(2)}) %collective-permute-start.31) | collective-permute-done | bytes 12320 | tf_op jit(solution)/shard_map/ppermute | solution.py:767
  153.4 7.6 %shard_map.156 = (f32[4096,128]{1,0:T(8,128)}, f32[64,128]{1,0:T(8,128)}) custom-call(f32[48]{0:T(128)S(1)} %reshape_squeeze.3.lat_ref.refs_0_, f32[10]{0:T(128)S(1)} %convert_element_type.4.flag.refs_1_, s32[2]{0:T(128)S(1)} %add_select_fusion.start.refs_2_, f32[5,24,128]{2,1,0:T(8,128)S(1)} %collective-permute-done.29.refs_3_, ...), custom_call_target="tpu_custom_call" | custom-call | flops 314572800 | bytes 12582912 | tf_op jit(solution)/shard_map/pallas_call | solution.py:510
  (104 shorter events, 44.8 us)
Async XLA Ops:
  2.3 50.3 %collective-permute-start.2 = (f32[4,1040,128]{2,1,0:T(8,128)S(1)}, f32[4,1040,128]{2,1,0:T(8,128)}, u32[]{:S(2)}, u32[]{:S(2)}) collective-permute-start(f32[4,1040,128]{2,1,0:T(8,128)S(1)} %pad_maximum_fusion.po.tpo.refs_8_.refs_15_.refs_14_.refs_21_), channel_id=1, source_target_pairs={{0,1},{1,2},{2,3},{4,5},{5,6},{6,7},{8,9},{9,10},{10,11},{12,13},{... | collective-permute-start | bytes 6389768 | tf_op jit(solution)/shard_map/ppermute | solution.py:753
  7.3 51.2 %collective-permute-start.3 = (f32[4,1040,128]{2,1,0:T(8,128)S(1)}, f32[4,1040,128]{2,1,0:T(8,128)}, u32[]{:S(2)}, u32[]{:S(2)}) collective-permute-start(f32[4,1040,128]{2,1,0:T(8,128)S(1)} %pad_maximum_fusion.po.tpo.refs_8_.refs_15_.refs_14_.refs_21_), channel_id=1, source_target_pairs={{1,0},{2,1},{3,2},{5,4},{6,5},{7,6},{9,8},{10,9},{11,10},{13,12},{... | collective-permute-start | bytes 6389768 | tf_op jit(solution)/shard_map/ppermute | solution.py:753
  11.8 10.1 %collective-permute-start = (f32[4,272,128]{2,1,0:T(8,128)}, f32[4,272,128]{2,1,0:T(8,128)S(1)}, u32[]{:S(2)}, u32[]{:S(2)}) collective-permute-start(f32[4,272,128]{2,1,0:T(8,128)} %get-tuple-element.36), channel_id=1, source_target_pairs={{0,4},{4,0},{8,12},{12,8},{1,5},{5,1},{9,13},{13,9},{2,6},{6,2},{1... | collective-permute-start | bytes 1671176 | tf_op jit(solution)/shard_map/ppermute | solution.py:767
  11.8 11.0 %collective-permute-start.1 = (f32[4,272,128]{2,1,0:T(8,128)}, f32[4,272,128]{2,1,0:T(8,128)S(1)}, u32[]{:S(2)}, u32[]{:S(2)}) collective-permute-start(f32[4,272,128]{2,1,0:T(8,128)} %get-tuple-element.36), channel_id=1, source_target_pairs={{4,8},{8,4},{5,9},{9,5},{6,10},{10,6},{7,11},{11,7},{20,24},{24,20... | collective-permute-start | bytes 1671176 | tf_op jit(solution)/shard_map/ppermute | solution.py:835
  31.1 38.7 %all-to-all-start = ((f32[16,24,128]{2,1,0:T(8,128)}), f32[16,24,128]{2,1,0:T(8,128)S(1)}, u32[]{:S(2)}, u32[]{:S(2)}) async-start(f32[16,24,128]{2,1,0:T(8,128)} %copy-done.7), calls=%async_computation | async-start | bytes 393216 | tf_op jit(solution)/shard_map/all_to_all | solution.py:878
  65.9 9.4 %collective-permute-start.10 = (f32[1,16,128]{2,1,0:T(8,128)S(1)}, f32[1,16,128]{2,1,0:T(8,128)S(1)}, u32[]{:S(2)}, u32[]{:S(2)}) collective-permute-start(f32[1,16,128]{2,1,0:T(8,128)S(1)} %get-tuple-element.47), channel_id=1, source_target_pairs={{0,18},{1,19},{2,16},{3,17},{16,2},{17,3},{18,0},{19,1},{4,22},{5,... | collective-permute-start | bytes 24584 | tf_op jit(solution)/shard_map/ppermute | solution.py:768
  68.1 7.8 %collective-permute-start.9 = (f32[1,16,128]{2,1,0:T(8,128)S(1)}, f32[1,16,128]{2,1,0:T(8,128)S(1)}, u32[]{:S(2)}, u32[]{:S(2)}) collective-permute-start(f32[1,16,128]{2,1,0:T(8,128)S(1)} %get-tuple-element.47), channel_id=1, source_target_pairs={{0,2},{1,3},{2,0},{3,1},{4,6},{5,7},{6,4},{7,5},{8,10},{9,11},{10,... | collective-permute-start | bytes 24584 | tf_op jit(solution)/shard_map/ppermute | solution.py:767
  69.8 9.3 %collective-permute-start.4 = (f32[5,16,128]{2,1,0:T(8,128)S(1)}, f32[5,16,128]{2,1,0:T(8,128)S(1)}, u32[]{:S(2)}, u32[]{:S(2)}) collective-permute-start(f32[5,16,128]{2,1,0:T(8,128)S(1)} %get-tuple-element.44), channel_id=1, source_target_pairs={{0,16},{1,17},{2,18},{3,19},{16,0},{17,1},{18,2},{19,3},{4,20},{5,... | collective-permute-start | bytes 122888 | tf_op jit(solution)/shard_map/ppermute | solution.py:768
  70.3 8.8 %collective-permute-start.5 = (f32[5,16,128]{2,1,0:T(8,128)S(1)}, f32[5,16,128]{2,1,0:T(8,128)S(1)}, u32[]{:S(2)}, u32[]{:S(2)}) collective-permute-start(f32[5,16,128]{2,1,0:T(8,128)S(1)} %get-tuple-element.45), channel_id=1, source_target_pairs={{0,1},{1,0},{2,3},{3,2},{4,5},{5,4},{6,7},{7,6},{8,9},{9,8},{10,11... | collective-permute-start | bytes 122888 | tf_op jit(solution)/shard_map/ppermute | solution.py:767
  72.8 9.4 %collective-permute-start.6 = (f32[5,16,128]{2,1,0:T(8,128)S(1)}, f32[5,16,128]{2,1,0:T(8,128)S(1)}, u32[]{:S(2)}, u32[]{:S(2)}) collective-permute-start(f32[5,16,128]{2,1,0:T(8,128)S(1)} %get-tuple-element.45), channel_id=1, source_target_pairs={{0,17},{1,16},{2,19},{3,18},{16,1},{17,0},{18,3},{19,2},{4,21},{5,... | collective-permute-start | bytes 122888 | tf_op jit(solution)/shard_map/ppermute | solution.py:768
  75.3 7.1 %collective-permute-start.7 = (f32[5,16,128]{2,1,0:T(8,128)S(1)}, f32[5,16,128]{2,1,0:T(8,128)S(1)}, u32[]{:S(2)}, u32[]{:S(2)}) collective-permute-start(f32[5,16,128]{2,1,0:T(8,128)S(1)} %get-tuple-element.46), channel_id=1, source_target_pairs={{0,3},{1,2},{2,1},{3,0},{4,7},{5,6},{6,5},{7,4},{8,11},{9,10},{10,... | collective-permute-start | bytes 122888 | tf_op jit(solution)/shard_map/ppermute | solution.py:767
  75.9 9.5 %collective-permute-start.8 = (f32[5,16,128]{2,1,0:T(8,128)S(1)}, f32[5,16,128]{2,1,0:T(8,128)S(1)}, u32[]{:S(2)}, u32[]{:S(2)}) collective-permute-start(f32[5,16,128]{2,1,0:T(8,128)S(1)} %get-tuple-element.46), channel_id=1, source_target_pairs={{0,19},{1,18},{2,17},{3,16},{16,3},{17,2},{18,1},{19,0},{4,23},{5,... | collective-permute-start | bytes 122888 | tf_op jit(solution)/shard_map/ppermute | solution.py:768
  79.0 39.0 %collective-permute-start.20 = (f32[8,272,128]{2,1,0:T(8,128)}, f32[8,272,128]{2,1,0:T(8,128)S(1)}, u32[]{:S(2)}, u32[]{:S(2)}) collective-permute-start(f32[8,272,128]{2,1,0:T(8,128)} %copy-done.9), channel_id=1, source_target_pairs={{0,4},{4,0},{8,12},{12,8},{1,5},{5,1},{9,13},{13,9},{2,6},{6,2},{1... | collective-permute-start | bytes 3342344 | tf_op jit(solution)/shard_map/ppermute | solution.py:767
  79.0 39.0 %collective-permute-start.21 = (f32[8,272,128]{2,1,0:T(8,128)}, f32[8,272,128]{2,1,0:T(8,128)S(1)}, u32[]{:S(2)}, u32[]{:S(2)}) collective-permute-start(f32[8,272,128]{2,1,0:T(8,128)} %copy-done.9), channel_id=1, source_target_pairs={{4,8},{8,4},{5,9},{9,5},{6,10},{10,6},{7,11},{11,7},{20,24},{24,20... | collective-permute-start | bytes 3342344 | tf_op jit(solution)/shard_map/ppermute | solution.py:835
  82.3 28.9 %collective-permute-start.18 = (f32[4,272,128]{2,1,0:T(8,128)S(1)}, f32[4,272,128]{2,1,0:T(8,128)S(1)}, u32[]{:S(2)}, u32[]{:S(2)}) collective-permute-start(f32[4,272,128]{2,1,0:T(8,128)S(1)} %copy-done.11), channel_id=1, source_target_pairs={{0,4},{4,0},{8,12},{12,8},{1,5},{5,1},{9,13},{13,9},{2,6},{6,2},{1... | collective-permute-start | bytes 1671176 | tf_op jit(solution)/shard_map/ppermute | solution.py:767
  82.4 29.7 %collective-permute-start.19 = (f32[4,272,128]{2,1,0:T(8,128)S(1)}, f32[4,272,128]{2,1,0:T(8,128)S(1)}, u32[]{:S(2)}, u32[]{:S(2)}) collective-permute-start(f32[4,272,128]{2,1,0:T(8,128)S(1)} %copy-done.11), channel_id=1, source_target_pairs={{4,8},{8,4},{5,9},{9,5},{6,10},{10,6},{7,11},{11,7},{20,24},{24,20... | collective-permute-start | bytes 1671176 | tf_op jit(solution)/shard_map/ppermute | solution.py:835
  88.2 16.4 %collective-permute-start.14 = (f32[16,24,128]{2,1,0:T(8,128)S(1)}, f32[16,24,128]{2,1,0:T(8,128)S(1)}, u32[]{:S(2)}, u32[]{:S(2)}) collective-permute-start(f32[16,24,128]{2,1,0:T(8,128)S(1)} %all-to-all-done.here_ref), channel_id=1, source_target_pairs={{4,8},{8,4},{5,9},{9,5},{6,10},{10,6},{7,11},{11,7},{20,24},{24,20... | collective-permute-start | bytes 589832 | tf_op jit(solution)/shard_map/ppermute | solution.py:835
  111.1 6.9 %collective-permute-start.15 = (f32[5,24,128]{2,1,0:T(8,128)S(1)}, f32[5,24,128]{2,1,0:T(8,128)S(1)}, u32[]{:S(2)}, u32[]{:S(2)}) collective-permute-start(f32[5,24,128]{2,1,0:T(8,128)S(1)} %get-tuple-element.54.refs_6_.refs_10_), channel_id=1, source_target_pairs={{0,1},{1,0},{2,3},{3,2},{4,5},{5,4},{6,7},{7,6},{8,9},{9,8},{10,11... | collective-permute-start | bytes 184328 | tf_op jit(solution)/shard_map/ppermute | solution.py:767
  111.2 6.9 %collective-permute-start.16 = (f32[5,24,128]{2,1,0:T(8,128)S(1)}, f32[5,24,128]{2,1,0:T(8,128)S(1)}, u32[]{:S(2)}, u32[]{:S(2)}) collective-permute-start(f32[5,24,128]{2,1,0:T(8,128)S(1)} %get-tuple-element.54.refs_6_.refs_10_), channel_id=1, source_target_pairs={{0,3},{1,2},{2,1},{3,0},{4,7},{5,6},{6,5},{7,4},{8,11},{9,10},{10,... | collective-permute-start | bytes 184328 | tf_op jit(solution)/shard_map/ppermute | solution.py:767
  127.3 7.3 %collective-permute-start.27 = (f32[1,24,128]{2,1,0:T(8,128)S(1)}, f32[1,24,128]{2,1,0:T(8,128)S(1)}, u32[]{:S(2)}, u32[]{:S(2)}) collective-permute-start(f32[1,24,128]{2,1,0:T(8,128)S(1)} %get-tuple-element.61), channel_id=1, source_target_pairs={{0,2},{1,3},{2,0},{3,1},{4,6},{5,7},{6,4},{7,5},{8,10},{9,11},{10,... | collective-permute-start | bytes 36872 | tf_op jit(solution)/shard_map/ppermute | solution.py:767
  128.6 7.9 %collective-permute-start.28 = (f32[1,24,128]{2,1,0:T(8,128)S(1)}, f32[1,24,128]{2,1,0:T(8,128)S(1)}, u32[]{:S(2)}, u32[]{:S(2)}) collective-permute-start(f32[1,24,128]{2,1,0:T(8,128)S(1)} %get-tuple-element.61), channel_id=1, source_target_pairs={{0,18},{1,19},{2,16},{3,17},{16,2},{17,3},{18,0},{19,1},{4,22},{5,... | collective-permute-start | bytes 36872 | tf_op jit(solution)/shard_map/ppermute | solution.py:768
  131.1 7.5 %collective-permute-start.23 = (f32[5,24,128]{2,1,0:T(8,128)S(1)}, f32[5,24,128]{2,1,0:T(8,128)S(1)}, u32[]{:S(2)}, u32[]{:S(2)}) collective-permute-start(f32[5,24,128]{2,1,0:T(8,128)S(1)} %get-tuple-element.59), channel_id=1, source_target_pairs={{0,1},{1,0},{2,3},{3,2},{4,5},{5,4},{6,7},{7,6},{8,9},{9,8},{10,11... | collective-permute-start | bytes 184328 | tf_op jit(solution)/shard_map/ppermute | solution.py:767
  131.8 6.7 %collective-permute-start.24 = (f32[5,24,128]{2,1,0:T(8,128)S(1)}, f32[5,24,128]{2,1,0:T(8,128)S(1)}, u32[]{:S(2)}, u32[]{:S(2)}) collective-permute-start(f32[5,24,128]{2,1,0:T(8,128)S(1)} %get-tuple-element.59), channel_id=1, source_target_pairs={{0,17},{1,16},{2,19},{3,18},{16,1},{17,0},{18,3},{19,2},{4,21},{5,... | collective-permute-start | bytes 184328 | tf_op jit(solution)/shard_map/ppermute | solution.py:768
  136.5 6.9 %collective-permute-start.26 = (f32[5,24,128]{2,1,0:T(8,128)S(1)}, f32[5,24,128]{2,1,0:T(8,128)S(1)}, u32[]{:S(2)}, u32[]{:S(2)}) collective-permute-start(f32[5,24,128]{2,1,0:T(8,128)S(1)} %get-tuple-element.60), channel_id=1, source_target_pairs={{0,19},{1,18},{2,17},{3,16},{16,3},{17,2},{18,1},{19,0},{4,23},{5,... | collective-permute-start | bytes 184328 | tf_op jit(solution)/shard_map/ppermute | solution.py:768
  (28 other events, 182.1 us)

commit v3 on v2

--- a/solution.py
+++ b/solution.py
@@ -293,34 +293,37 @@
     )(lat_w, flags, a, *a_sides, p_own, t, *a_sides, p_own, weights)
 
 
-def first_rest_body(
-    channels, n_mem, lat_ref, start, z_in, zt, pu, pd, tpu_, tpd, e_in, eo_ref, ea_ref, eb_ref, ec_ref, x_ref, acc
-):
+def first_rest_body(channels, n_mem, above, lat_ref, *refs):
+    if above:
+        z_in, zt, p, tp, e_in, up_ref, ec_ref, x_ref, acc = refs
+    else:
+        start, z_in, zt, p, tp, e_in, up_in, eo_ref, ea_ref, eb_ref, x_ref, acc = refs
     step = pl.program_id(0)
     lats, rows, lon = z_in.shape
     members = rows // channels
     part = rows // SLOTS
-    halo = list(range(4)) + list(range(4 + lats, 8 + lats))
-
-    def get(above, below, l12, sel):
-        return above[l12, sel, :] if l12 < 4 else below[l12 - 4 - lats, sel, :]
+    halo = range(4) if above else range(4 + lats, 8 + lats)
+    first = halo[0]
 
     @pl.when(step == 0)
     def _():
-        out = forward_rows(lat_ref, lambda l: zt[l], lambda l12: get(tpu_, tpd, l12, slice(None)), lats, halo)
+        out = forward_rows(lat_ref, lambda l: zt[l], lambda l12: tp[l12 - first], lats, halo)
         acc[4 : 4 + lats] = e_in[...]
-        acc[8 + lats] = jnp.zeros((channels, lon), F32)
-        for i, (l12, value) in enumerate(zip(halo, out)):
-            acc[l12] = value * (1.0 / n_mem)
-            x_ref[i, pl.ds(pl.num_programs(0) * part, channels), :] = edges([get(tpu_, tpd, l12, slice(None))])
-
-    for i, l12 in enumerate(halo):
+        if not above:
+            acc[8 + lats] = jnp.zeros((channels, lon), F32)
+            for r in range(4):
+                acc[r] = up_in[r]
+        for i, value in enumerate(out):
+            acc[first + i] = value * (1.0 / n_mem)
+            x_ref[i, pl.ds(pl.num_programs(0) * part, channels), :] = edges([tp[i]])
+
+    for i in range(4):
         at = pl.ds(pl.multiple_of(step * part, part), part)
-        x_ref[i, at, :] = edges([get(pu, pd, l12, slice(j * part, (j + 1) * part)) for j in range(SLOTS)])
+        x_ref[i, at, :] = edges([p[i, j * part : (j + 1) * part, :] for j in range(SLOTS)])
 
     def one(k, sums):
         sel = pl.ds(pl.multiple_of(k * channels, channels), channels)
-        out = forward_rows(lat_ref, lambda l: z_in[l, sel, :], lambda l12: get(pu, pd, l12, sel), lats, halo)
+        out = forward_rows(lat_ref, lambda l: z_in[l, sel, :], lambda l12: p[l12 - first, sel, :], lats, halo)
         return tuple(a + b for a, b in zip(sums, out))
 
     sums = lax.fori_loop(0, members, one, tuple(acc[l12] for l12 in halo), unroll=2)
@@ -329,28 +332,32 @@
 
     @pl.when(step == pl.num_programs(0) - 1)
     def _():
-        for ref, first in ((eo_ref, 4), (ea_ref, start[0]), (eb_ref, start[1]), (ec_ref, 0)):
+        outs = ((up_ref, 0), (ec_ref, 0)) if above else ((eo_ref, 4), (ea_ref, start[0]), (eb_ref, start[1]))
+        for ref, at in outs:
             for r in range(ref.shape[0]):
-                ref[r] = acc[first + r]
-
-
-def first_rest(lat_w, starts, z, zt, p_up, p_down, e_own, channels, n_mem, step_rows):
+                ref[r] = acc[at + r]
+
+
+def first_rest(lat_w, z, zt, p, e_own, channels, n_mem, step_rows, starts=None, up=None):
+    above = up is None
     lats, rows, lon = z.shape
     mb = pl.BlockSpec((lats, step_rows, lon), lambda i: (0, i, 0))
     fb = pl.BlockSpec((lats, channels, lon), lambda i: (0, 0, 0))
     tb = pl.BlockSpec((lats, channels, lon), lambda i: (0, rows // channels, 0))
     whole = lambda *shape: pl.BlockSpec(shape, lambda i: (0,) * len(shape))
-    shapes = [(lats + 1, channels, lon)] * 3 + [(1, channels, lon), (8, rows // SLOTS + channels, lon)]
+    five = (lats + 1, channels, lon)
+    shapes = [five, (1, channels, lon)] if above else [five] * 3
+    shapes.append((4, rows // SLOTS + channels, lon))
     return call(
-        functools.partial(first_rest_body, channels, n_mem),
+        functools.partial(first_rest_body, channels, n_mem, above),
         [jax.ShapeDtypeStruct(shape, F32) for shape in shapes],
         grid=(rows // step_rows,),
-        in_specs=[smem(), smem(), mb, fb, mb, mb, tb, tb, fb],
+        in_specs=[smem()] * (1 if above else 2) + [mb, fb, mb, tb, fb] + ([] if above else [whole(*five)]),
         out_specs=[whole(*shape) for shape in shapes],
         scratch_shapes=[pltpu.VMEM((lats + 9, channels, lon), F32)],
-        flops=lats * rows * lon * 60,
-        nbytes=z.size * 14,
-    )(lat_w, starts, z, zt, p_up, p_down, p_up, p_down, e_own)
+        flops=lats * rows * lon * 30,
+        nbytes=z.size * 8,
+    )(lat_w, *([] if above else [starts]), z, zt, p, p, e_own, *([] if above else [up]))
 
 
 ABOVE_A, BELOW_A, ABOVE_B, BELOW_B, TWO_BELOW, TWO_ABOVE, LEFT_A, RIGHT_A, LEFT_B, RIGHT_B = range(10)
@@ -381,8 +388,8 @@
     before = None
     if last:
         before, am, tm, refs = refs[:4], refs[4], refs[5], refs[6:]
-    p_main, p_sides, tp_main, tp_sides, w_ref = refs[:3], refs[3:7], refs[7:10], refs[10:14], refs[14]
-    refs = refs[15:]
+    p_main, p_sides, tp_main, tp_sides, w_ref = refs[:3], refs[3:9], refs[9:12], refs[12:18], refs[18]
+    refs = refs[19:]
     if last:
         am_out, tm_out, gm_ref, gs_ref, h = refs
     else:
@@ -396,10 +403,11 @@
     unroll = 2 if members % 2 == 0 else 1
 
     def side_get(sides, l12, sel):
-        if 4 <= l12 < 4 + lats:
+        if l12 < 4:
+            return beside(odd, sides[2][l12, sel, :], sides[3][l12, sel, :])
+        if l12 < 4 + lats:
             return beside(odd, sides[0][l12 - 4, sel, :], sides[1][l12 - 4, sel, :])
-        i = l12 if l12 < 4 else l12 - lats
-        return beside(odd, sides[2][i, sel, :], sides[3][i, sel, :])
+        return beside(odd, sides[4][l12 - 4 - lats, sel, :], sides[5][l12 - 4 - lats, sel, :])
 
     def adjoint_main(p, k, count):
         sel = pl.ds(pl.multiple_of(k * channels, channels), channels)
@@ -482,7 +490,7 @@
                     ref[r, channels:, :] = narrow(repeat_slots(acc_s[first + r]))
 
 
-def member_step(lat_w, flags, starts, g4, p3, x4, weights, channels, n_mem, step_rows, final=None):
+def member_step(lat_w, flags, starts, g4, p3, x6, weights, channels, n_mem, step_rows, final=None):
     last = final is not None
     lats, total, lon = p3[0].shape
     rows = total - channels
@@ -490,8 +498,8 @@
     mb = pl.BlockSpec((lats, step_rows, lon), lambda i: (0, i, 0))
     fb = pl.BlockSpec((lats, channels, lon), lambda i: (0, 0, 0))
     tpb = pl.BlockSpec((lats, channels, lon), lambda i: (0, rows // channels, 0))
-    xb = [pl.BlockSpec((n, part, lon), lambda i: (0, i, 0)) for n in (lats, lats, 8, 8)]
-    txb = [pl.BlockSpec((n, channels, lon), lambda i: (0, rows // SLOTS // channels, 0)) for n in (lats, lats, 8, 8)]
+    xb = [pl.BlockSpec((n, part, lon), lambda i: (0, i, 0)) for n in (lats, lats, 4, 4, 4, 4)]
+    txb = [pl.BlockSpec((n, channels, lon), lambda i: (0, rows // SLOTS // channels, 0)) for n in (lats, lats, 4, 4, 4, 4)]
     whole = lambda shape: pl.BlockSpec(shape, lambda i: (0,) * len(shape))
     sds = lambda *shape: jax.ShapeDtypeStruct(shape, F32)
     half = channels + channels // 2
@@ -516,7 +524,7 @@
         scratch_shapes=scratch,
         flops=lats * rows * lon * 600,
         nbytes=rows * lats * lon * 24,
-    )(lat_w, flags, starts, *g4, *extra, *p3, *x4, *p3, *x4, weights)
+    )(lat_w, flags, starts, *g4, *extra, *p3, *x6, *p3, *x6, weights)
 
 
 FIELDS = 24
@@ -824,7 +832,8 @@
         ],
         1,
     )
-    p_up, p_down = shifted(p_own, "gy", 1), shifted(p_own, "gy", -1)
+    p_up = shifted(p_own, "gy", 1)
+    p_down = shifted(p_own, "gy", -1)
     p3 = (p_up, p_own, p_down)
     a, a_edges, t = prepare(
         alpha.reshape(rows * lats, lon), static_control.reshape(channels * lats, lon), lats, channels, step_rows
@@ -870,8 +879,11 @@
     z, zt, e_own, x_own = first_own(lat_w, flags, a, a_sides, t, p_own, own_weights, channels, n_mem, step_rows)
     z, sent = lax.optimization_barrier((z, sent))
     x_own = from_beside(x_own)
-    *e4, x_rest = first_rest(lat_w, starts, z, zt, p_up, p_down, e_own, channels, n_mem, step_rows)
-    x_rest = from_beside(x_rest)
+    e_up, e_up1, x_up = first_rest(lat_w, z, zt, p_up, e_own, channels, n_mem, step_rows)
+    x_up = from_beside(x_up)
+    e_mid, e_a, e_b, x_down = first_rest(lat_w, z, zt, p_down, e_own, channels, n_mem, step_rows, starts, e_up)
+    e4 = [e_mid, e_a, e_b, e_up1]
+    x_down = from_beside(x_down)
     per_group = LANES // capacity if capacity < LANES else 1
     if per_group > 1:
         sent = sent.reshape(-1, FIELDS, per_group, capacity).transpose(0, 2, 1, 3).reshape(tile_count, FIELDS, capacity)
@@ -885,7 +897,7 @@
     s = own + own2 + (na + na2) + (flags[ABOVE_B] + flags[BELOW_B]) * (nb + nb2)
     s = s + jnp.concatenate([jnp.zeros_like(s[:lats]), flags[TWO_BELOW] * (nc + nc2)], 0)
     sums = (s, swap(s, "gx", partner_a), swap(s, "gx", partner_b))
-    x4 = (*x_own, *x_rest)
+    x6 = (*x_own, *x_up, *x_down)
     scale = descent * ens_scale
     g, g_over, dx = observe(flags, sums, records, channels, ens_scale, scale, lats)
 
@@ -893,11 +905,11 @@
         return swap(g, "gy", partner_a), swap(g, "gy", partner_b), two_away(g_over, 2), g
 
     g0 = gather_g(g, g_over)
-    sums = gather_rows(*member_step(lat_w, flags, starts, g0, p3, x4, twice_weights, channels, n_mem, step_rows))
+    sums = gather_rows(*member_step(lat_w, flags, starts, g0, p3, x6, twice_weights, channels, n_mem, step_rows))
     g, g_over, dx = observe(flags, (dx, *sums), records, channels, ens_scale, scale, lats)
     g1 = gather_g(g, g_over)
     a, t = member_step(
-        lat_w, flags, starts, g1, p3, x4, own_weights, channels, n_mem, step_rows, final=(g0, a, t, scale)
+        lat_w, flags, starts, g1, p3, x6, own_weights, channels, n_mem, step_rows, final=(g0, a, t, scale)
     )
     return (
         a.reshape(alpha.shape),

time: 162 us -> 165 us (1.019)
  the two profiles are of different devices: /device:TPU:2 before, /device:TPU:0 now
where the time goes in v3:
time: 165 us; the launch traced here: 164 us
  starting transfers between devices  65.4 us (40%)
  Pallas kernels  42.5 us (26%)
  waiting for transfers between devices  36.6 us (22%)
  local copies, waits for them, and re-layouts  15.2 us (9%)
  between operations  2.34 us (1%)
  other arithmetic  1.67 us (1%)
    ppermute x19, starting transfers between devices, swap(): lax.ppermute(block, axis, [(i, partner(i, count)) for i in range(count)])  29.2 us
    ppermute x19, waiting for transfers between devices, swap(): lax.ppermute(block, axis, [(i, partner(i, count)) for i in range(count)])  18.5 us
    pallas_call x2, Pallas kernels, member_step(): call(functools.partial(step_body, channels, n_mem, scale, last), out_shap...  17.6 us
    ppermute x8, starting transfers between devices, swap(): lax.ppermute(block, ('mem', axis), [(m * count + i, (1 - m) * count + par...  15.2 us
    ppermute x2, waiting for transfers between devices, shifted(): return lax.ppermute(block, axis, route)  14.1 us
    unnamed x37, local copies, waits for them, and re-layouts  10.3 us
    all_to_all x1, starting transfers between devices, assimilate(): lax.all_to_all(sent, ('gx', 'gy'), split_axis=0, concat_axis=0, tiled=True)  9.76 us
    ppermute x2, starting transfers between devices, shifted(): return lax.ppermute(block, axis, route)  7.73 us
  transfers between devices with their start and end apart: 35, of which 9 were waited for; matrix products, arithmetic and copies ran while one was open for 3% of the time, Pallas kernels for 13%

profile of v3, /device:TPU:0, one launch (start us, length us, event | category | flops | bytes accessed | tf_op | source)
XLA Modules:
  0.0 163.7 jit_solution(10824419440471999383)
XLA Ops:
  3.1 6.5 %collective-permute-start.3 = (f32[4,1040,128]{2,1,0:T(8,128)S(1)}, f32[4,1040,128]{2,1,0:T(8,128)}, u32[]{:S(2)}, u32[]{:S(2)}) collective-permute-start(f32[4,1040,128]{2,1,0:T(8,128)S(1)} %pad_maximum_fusion.po.tpo.refs_8_.refs_17_.refs_14_.refs_23_), channel_id=1, source_target_pairs={{0,1},{1,2},{2,3},{4,5},{5,6},{6,7},{8,9},{9,10},{10,11},{12,13},{... | collective-permute-start | bytes 6389768 | tf_op jit(solution)/shard_map/ppermute | solution.py:761
  17.8 3.4 %shard_map.150 = f32[16,24,128]{2,1,0:T(8,128)S(1)} custom-call(s32[1024,1]{1,0:T(8,128)S(1)} %copy-done.6, f32[16,1024]{1,0:T(8,128)S(1)} %bitcast.35, f32[4,1024]{1,0:T(4,128)S(1)} %copy-done.13, s32[1,1024]{1,0:T(1,128)S(1)} %bitcast.36, f32[1,1024]{1,0:T(1,128)S(1)} %bitcast.37, f32[1,1024]{1,0:T(1,128)S(1)} %bitcast.38), custom_call_target="tpu_custom_call" | custom-call | flops 314572800 | bytes 409600 | tf_op jit(solution)/shard_map/pallas_call | solution.py:565
  23.9 4.5 %shard_map.149 = (f32[4,1024,128]{2,1,0:T(8,128)S(1)}, f32[4,16,128]{2,1,0:T(8,128)S(1)}, f32[4,16,128]{2,1,0:T(8,128)S(1)}, f32[4,272,128]{2,1,0:T(8,128)S(1)}) custom-call(f32[48]{0:T(128)S(1)} %reshape_squeeze.3.lat_ref.refs_0_, f32[10]{0:T(128)S(1)} %convert_element_type.4.flag.refs_1_, f32[4,1024,128]{2,1,0:T(8,128)S(1)} %copy-done.1, ...), custom_call_target="tpu_custom_call" | custom-call | flops 52428800 | bytes 8388608 | tf_op jit(solution)/shard_map/pallas_call | solution.py:284
  30.5 9.8 %all-to-all-start = ((f32[16,24,128]{2,1,0:T(8,128)}), f32[16,24,128]{2,1,0:T(8,128)S(1)}, u32[]{:S(2)}, u32[]{:S(2)}) async-start(f32[16,24,128]{2,1,0:T(8,128)} %copy-done.7), calls=%async_computation | async-start | bytes 393216 | tf_op jit(solution)/shard_map/all_to_all | solution.py:890
  40.8 14.1 %collective-permute-done.3.refs_2_.refs_3_.refs_7_.refs_16_.refs_13_.refs_22_ = f32[4,1040,128]{2,1,0:T(8,128)} collective-permute-done((f32[4,1040,128]{2,1,0:T(8,128)S(1)}, f32[4,1040,128]{2,1,0:T(8,128)}, u32[]{:S(2)}, u32[]{:S(2)}) %collective-permute-start.3) | collective-permute-done | bytes 2129952 | tf_op jit(solution)/shard_map/ppermute | solution.py:761
  56.4 3.5 %shard_map.151 = (f32[5,16,128]{2,1,0:T(8,128)S(1)}, f32[1,16,128]{2,1,0:T(8,128)S(1)}, f32[4,272,128]{2,1,0:T(8,128)S(1)}) custom-call(f32[48]{0:T(128)S(1)} %reshape_squeeze.3.lat_ref.refs_0_, f32[4,1024,128]{2,1,0:T(8,128)S(1)} %copy-done.4, f32[4,16,128]{2,1,0:T(8,128)S(1)} %get-tuple-element.43.refs_1_.refs_2_, ...), custom_call_target="tpu_custom_call" | custom-call | flops 15728640 | bytes 4194304 | tf_op jit(solution)/shard_map/pallas_call | solution.py:351
  60.8 5.6 %collective-permute-start.9 = (f32[1,16,128]{2,1,0:T(8,128)S(1)}, f32[1,16,128]{2,1,0:T(8,128)S(1)}, u32[]{:S(2)}, u32[]{:S(2)}) collective-permute-start(f32[1,16,128]{2,1,0:T(8,128)S(1)} %get-tuple-element.50), channel_id=1, source_target_pairs={{0,2},{1,3},{2,0},{3,1},{4,6},{5,7},{6,4},{7,5},{8,10},{9,11},{10,... | collective-permute-start | bytes 24584 | tf_op jit(solution)/shard_map/ppermute | solution.py:775
  67.4 3.5 %shard_map.152 = (f32[5,16,128]{2,1,0:T(8,128)S(1)}, f32[5,16,128]{2,1,0:T(8,128)S(1)}, f32[5,16,128]{2,1,0:T(8,128)S(1)}, f32[4,272,128]{2,1,0:T(8,128)S(1)}) custom-call(f32[48]{0:T(128)S(1)} %reshape_squeeze.3.lat_ref.refs_0_, s32[2]{0:T(128)S(1)} %add_select_fusion.refs_0_.refs_2_, f32[4,1024,128]{2,1,0:T(8,128)S(1)} %copy-done.4, ...), custom_call_target="tpu_custom_call" | custom-call | flops 15728640 | bytes 4194304 | tf_op jit(solution)/shard_map/pallas_call | solution.py:351
  77.5 2.9 %collective-permute-start.6 = (f32[5,16,128]{2,1,0:T(8,128)S(1)}, f32[5,16,128]{2,1,0:T(8,128)S(1)}, u32[]{:S(2)}, u32[]{:S(2)}) collective-permute-start(f32[5,16,128]{2,1,0:T(8,128)S(1)} %get-tuple-element.48), channel_id=1, source_target_pairs={{0,17},{1,16},{2,19},{3,18},{16,1},{17,0},{18,3},{19,2},{4,21},{5,... | collective-permute-start | bytes 122888 | tf_op jit(solution)/shard_map/ppermute | solution.py:776
  83.2 2.9 %collective-permute-start.13 = (f32[16,24,128]{2,1,0:T(8,128)S(1)}, f32[16,24,128]{2,1,0:T(8,128)S(1)}, u32[]{:S(2)}, u32[]{:S(2)}) collective-permute-start(f32[16,24,128]{2,1,0:T(8,128)S(1)} %all-to-all-done.here_ref), channel_id=1, source_target_pairs={{0,4},{4,0},{8,12},{12,8},{1,5},{5,1},{9,13},{13,9},{2,6},{6,2},{1... | collective-permute-start | bytes 589832 | tf_op jit(solution)/shard_map/ppermute | solution.py:775
  92.7 7.4 %collective-permute-start.22 = (f32[4,272,128]{2,1,0:T(8,128)}, f32[4,272,128]{2,1,0:T(8,128)S(1)}, u32[]{:S(2)}, u32[]{:S(2)}) collective-permute-start(f32[4,272,128]{2,1,0:T(8,128)} %copy-done.10), channel_id=1, source_target_pairs={{0,4},{4,0},{8,12},{12,8},{1,5},{5,1},{9,13},{13,9},{2,6},{6,2},{1... | collective-permute-start | bytes 1671176 | tf_op jit(solution)/shard_map/ppermute | solution.py:775
  102.5 3.1 %shard_map.154 = (f32[5,24,128]{2,1,0:T(8,128)S(1)}, f32[1,24,128]{2,1,0:T(8,128)S(1)}, f32[5,24,128]{2,1,0:T(8,128)S(1)}) custom-call(f32[10]{0:T(128)S(1)} %convert_element_type.4.flag.refs_1_, f32[5,16,128]{2,1,0:T(8,128)S(1)} %pad_add_fusion.refs_0_, f32[5,16,128]{2,1,0:T(8,128)S(1)} %collective-permute-done.11.refs_1_, ...), custom_call_target="tpu_custom_call" | custom-call | flops 805306368 | bytes 4194304 | tf_op jit(solution)/shard_map/pallas_call | solution.py:742
  105.9 4.5 %collective-permute-done.17.refs_5_.refs_9_ = f32[1,24,128]{2,1,0:T(8,128)S(1)} collective-permute-done((f32[1,24,128]{2,1,0:T(8,128)S(1)}, f32[1,24,128]{2,1,0:T(8,128)S(1)}, u32[]{:S(2)}, u32[]{:S(2)}) %collective-permute-start.17) | collective-permute-done | bytes 12320 | tf_op jit(solution)/shard_map/ppermute | solution.py:775
  110.3 4.2 %collective-permute-done.15.refs_3_.refs_7_ = f32[5,24,128]{2,1,0:T(8,128)S(1)} collective-permute-done((f32[5,24,128]{2,1,0:T(8,128)S(1)}, f32[5,24,128]{2,1,0:T(8,128)S(1)}, u32[]{:S(2)}, u32[]{:S(2)}) %collective-permute-start.15) | collective-permute-done | bytes 61472 | tf_op jit(solution)/shard_map/ppermute | solution.py:775
  117.1 3.5 %collective-permute-done.16.refs_4_.refs_8_ = f32[5,24,128]{2,1,0:T(8,128)S(1)} collective-permute-done((f32[5,24,128]{2,1,0:T(8,128)S(1)}, f32[5,24,128]{2,1,0:T(8,128)S(1)}, u32[]{:S(2)}, u32[]{:S(2)}) %collective-permute-start.16) | collective-permute-done | bytes 61472 | tf_op jit(solution)/shard_map/ppermute | solution.py:775
  120.6 9.7 %shard_map.155 = (f32[5,24,128]{2,1,0:T(8,128)S(1)}, f32[5,24,128]{2,1,0:T(8,128)S(1)}, f32[5,24,128]{2,1,0:T(8,128)S(1)}, f32[1,24,128]{2,1,0:T(8,128)S(1)}) custom-call(f32[48]{0:T(128)S(1)} %reshape_squeeze.3.lat_ref.refs_0_, f32[10]{0:T(128)S(1)} %convert_element_type.4.flag.refs_1_, s32[2]{0:T(128)S(1)} %add_select_fusion.refs_0_.refs_2_, ...), custom_call_target="tpu_custom_call" | custom-call | flops 314572800 | bytes 12582912 | tf_op jit(solution)/shard_map/pallas_call | solution.py:518
  130.4 2.9 %collective-permute-start.30 = (f32[1,24,128]{2,1,0:T(8,128)S(1)}, f32[1,24,128]{2,1,0:T(8,128)S(1)}, u32[]{:S(2)}, u32[]{:S(2)}) collective-permute-start(f32[1,24,128]{2,1,0:T(8,128)S(1)} %get-tuple-element.65), channel_id=1, source_target_pairs={{0,18},{1,19},{2,16},{3,17},{16,2},{17,3},{18,0},{19,1},{4,22},{5,... | collective-permute-start | bytes 36872 | tf_op jit(solution)/shard_map/ppermute | solution.py:776
  133.2 3.0 %collective-permute-start.26 = (f32[5,24,128]{2,1,0:T(8,128)S(1)}, f32[5,24,128]{2,1,0:T(8,128)S(1)}, u32[]{:S(2)}, u32[]{:S(2)}) collective-permute-start(f32[5,24,128]{2,1,0:T(8,128)S(1)} %get-tuple-element.63), channel_id=1, source_target_pairs={{0,17},{1,16},{2,19},{3,18},{16,1},{17,0},{18,3},{19,2},{4,21},{5,... | collective-permute-start | bytes 184328 | tf_op jit(solution)/shard_map/ppermute | solution.py:776
  136.7 2.2 %collective-permute-start.27 = (f32[5,24,128]{2,1,0:T(8,128)S(1)}, f32[5,24,128]{2,1,0:T(8,128)S(1)}, u32[]{:S(2)}, u32[]{:S(2)}) collective-permute-start(f32[5,24,128]{2,1,0:T(8,128)S(1)} %get-tuple-element.64), channel_id=1, source_target_pairs={{0,3},{1,2},{2,1},{3,0},{4,7},{5,6},{6,5},{7,4},{8,11},{9,10},{10,... | collective-permute-start | bytes 184328 | tf_op jit(solution)/shard_map/ppermute | solution.py:775
  138.9 2.6 %collective-permute-start.28 = (f32[5,24,128]{2,1,0:T(8,128)S(1)}, f32[5,24,128]{2,1,0:T(8,128)S(1)}, u32[]{:S(2)}, u32[]{:S(2)}) collective-permute-start(f32[5,24,128]{2,1,0:T(8,128)S(1)} %get-tuple-element.64), channel_id=1, source_target_pairs={{0,19},{1,18},{2,17},{3,16},{16,3},{17,2},{18,1},{19,0},{4,23},{5,... | collective-permute-start | bytes 184328 | tf_op jit(solution)/shard_map/ppermute | solution.py:776
  142.8 3.0 %collective-permute-done.28.refs_6_ = f32[5,24,128]{2,1,0:T(8,128)S(1)} collective-permute-done((f32[5,24,128]{2,1,0:T(8,128)S(1)}, f32[5,24,128]{2,1,0:T(8,128)S(1)}, u32[]{:S(2)}, u32[]{:S(2)}) %collective-permute-start.28) | collective-permute-done | bytes 61472 | tf_op jit(solution)/shard_map/ppermute | solution.py:776
  145.8 3.5 %shard_map.156 = (f32[5,24,128]{2,1,0:T(8,128)S(1)}, f32[1,24,128]{2,1,0:T(8,128)S(1)}, f32[64,128]{1,0:T(8,128)}) custom-call(f32[10]{0:T(128)S(1)} %convert_element_type.4.flag.refs_1_, f32[5,24,128]{2,1,0:T(8,128)S(1)} %get-tuple-element.56.refs_0_, f32[5,24,128]{2,1,0:T(8,128)S(1)} %get-tuple-element.62.refs_1_, ...), custom_call_target="tpu_custom_call" | custom-call | flops 805306368 | bytes 4194304 | tf_op jit(solution)/shard_map/pallas_call | solution.py:742
  152.8 3.0 %collective-permute-done.33.refs_5_ = f32[1,24,128]{2,1,0:T(8,128)S(1)} collective-permute-done((f32[1,24,128]{2,1,0:T(8,128)S(1)}, f32[1,24,128]{2,1,0:T(8,128)S(1)}, u32[]{:S(2)}, u32[]{:S(2)}) %collective-permute-start.33) | collective-permute-done | bytes 12320 | tf_op jit(solution)/shard_map/ppermute | solution.py:775
  155.8 7.9 %shard_map.157 = (f32[4096,128]{1,0:T(8,128)}, f32[64,128]{1,0:T(8,128)}) custom-call(f32[48]{0:T(128)S(1)} %reshape_squeeze.3.lat_ref.refs_0_, f32[10]{0:T(128)S(1)} %convert_element_type.4.flag.refs_1_, s32[2]{0:T(128)S(1)} %add_select_fusion.refs_0_.refs_2_, f32[5,24,128]{2,1,0:T(8,128)S(1)} %collective-permute-done.31.refs_3_, ...), custom_call_target="tpu_custom_call" | custom-call | flops 314572800 | bytes 12582912 | tf_op jit(solution)/shard_map/pallas_call | solution.py:518
  (107 shorter events, 44.4 us)
Async XLA Ops:
  3.1 51.8 %collective-permute-start.3 = (f32[4,1040,128]{2,1,0:T(8,128)S(1)}, f32[4,1040,128]{2,1,0:T(8,128)}, u32[]{:S(2)}, u32[]{:S(2)}) collective-permute-start(f32[4,1040,128]{2,1,0:T(8,128)S(1)} %pad_maximum_fusion.po.tpo.refs_8_.refs_17_.refs_14_.refs_23_), channel_id=1, source_target_pairs={{0,1},{1,2},{2,3},{4,5},{5,6},{6,7},{8,9},{9,10},{10,11},{12,13},{... | collective-permute-start | bytes 6389768 | tf_op jit(solution)/shard_map/ppermute | solution.py:761
  9.5 57.9 %collective-permute-start.2 = (f32[4,1040,128]{2,1,0:T(8,128)S(1)}, f32[4,1040,128]{2,1,0:T(8,128)}, u32[]{:S(2)}, u32[]{:S(2)}) collective-permute-start(f32[4,1040,128]{2,1,0:T(8,128)S(1)} %pad_maximum_fusion.po.tpo.refs_8_.refs_17_.refs_14_.refs_23_), channel_id=1, source_target_pairs={{1,0},{2,1},{3,2},{5,4},{6,5},{7,6},{9,8},{10,9},{11,10},{13,12},{... | collective-permute-start | bytes 6389768 | tf_op jit(solution)/shard_map/ppermute | solution.py:761
  14.0 8.2 %collective-permute-start = (f32[4,272,128]{2,1,0:T(8,128)}, f32[4,272,128]{2,1,0:T(8,128)S(1)}, u32[]{:S(2)}, u32[]{:S(2)}) collective-permute-start(f32[4,272,128]{2,1,0:T(8,128)} %get-tuple-element.38), channel_id=1, source_target_pairs={{0,4},{4,0},{8,12},{12,8},{1,5},{5,1},{9,13},{13,9},{2,6},{6,2},{1... | collective-permute-start | bytes 1671176 | tf_op jit(solution)/shard_map/ppermute | solution.py:775
  14.0 8.2 %collective-permute-start.1 = (f32[4,272,128]{2,1,0:T(8,128)}, f32[4,272,128]{2,1,0:T(8,128)S(1)}, u32[]{:S(2)}, u32[]{:S(2)}) collective-permute-start(f32[4,272,128]{2,1,0:T(8,128)} %get-tuple-element.38), channel_id=1, source_target_pairs={{4,8},{8,4},{5,9},{9,5},{6,10},{10,6},{7,11},{11,7},{20,24},{24,20... | collective-permute-start | bytes 1671176 | tf_op jit(solution)/shard_map/ppermute | solution.py:844
  30.5 46.9 %all-to-all-start = ((f32[16,24,128]{2,1,0:T(8,128)}), f32[16,24,128]{2,1,0:T(8,128)S(1)}, u32[]{:S(2)}, u32[]{:S(2)}) async-start(f32[16,24,128]{2,1,0:T(8,128)} %copy-done.7), calls=%async_computation | async-start | bytes 393216 | tf_op jit(solution)/shard_map/all_to_all | solution.py:890
  40.3 47.8 %collective-permute-start.18 = (f32[4,272,128]{2,1,0:T(8,128)}, f32[4,272,128]{2,1,0:T(8,128)S(1)}, u32[]{:S(2)}, u32[]{:S(2)}) collective-permute-start(f32[4,272,128]{2,1,0:T(8,128)} %copy-done.11), channel_id=1, source_target_pairs={{0,4},{4,0},{8,12},{12,8},{1,5},{5,1},{9,13},{13,9},{2,6},{6,2},{1... | collective-permute-start | bytes 1671176 | tf_op jit(solution)/shard_map/ppermute | solution.py:775
  60.8 16.6 %collective-permute-start.9 = (f32[1,16,128]{2,1,0:T(8,128)S(1)}, f32[1,16,128]{2,1,0:T(8,128)S(1)}, u32[]{:S(2)}, u32[]{:S(2)}) collective-permute-start(f32[1,16,128]{2,1,0:T(8,128)S(1)} %get-tuple-element.50), channel_id=1, source_target_pairs={{0,2},{1,3},{2,0},{3,1},{4,6},{5,7},{6,4},{7,5},{8,10},{9,11},{10,... | collective-permute-start | bytes 24584 | tf_op jit(solution)/shard_map/ppermute | solution.py:775
  66.5 11.0 %collective-permute-start.10 = (f32[1,16,128]{2,1,0:T(8,128)S(1)}, f32[1,16,128]{2,1,0:T(8,128)S(1)}, u32[]{:S(2)}, u32[]{:S(2)}) collective-permute-start(f32[1,16,128]{2,1,0:T(8,128)S(1)} %get-tuple-element.50), channel_id=1, source_target_pairs={{0,18},{1,19},{2,16},{3,17},{16,2},{17,3},{18,0},{19,1},{4,22},{5,... | collective-permute-start | bytes 24584 | tf_op jit(solution)/shard_map/ppermute | solution.py:776
  71.7 8.6 %collective-permute-start.7 = (f32[5,16,128]{2,1,0:T(8,128)S(1)}, f32[5,16,128]{2,1,0:T(8,128)S(1)}, u32[]{:S(2)}, u32[]{:S(2)}) collective-permute-start(f32[5,16,128]{2,1,0:T(8,128)S(1)} %get-tuple-element.49), channel_id=1, source_target_pairs={{0,3},{1,2},{2,1},{3,0},{4,7},{5,6},{6,5},{7,4},{8,11},{9,10},{10,... | collective-permute-start | bytes 122888 | tf_op jit(solution)/shard_map/ppermute | solution.py:775
  75.7 6.9 %collective-permute-start.8 = (f32[5,16,128]{2,1,0:T(8,128)S(1)}, f32[5,16,128]{2,1,0:T(8,128)S(1)}, u32[]{:S(2)}, u32[]{:S(2)}) collective-permute-start(f32[5,16,128]{2,1,0:T(8,128)S(1)} %get-tuple-element.49), channel_id=1, source_target_pairs={{0,19},{1,18},{2,17},{3,16},{16,3},{17,2},{18,1},{19,0},{4,23},{5,... | collective-permute-start | bytes 122888 | tf_op jit(solution)/shard_map/ppermute | solution.py:776
  77.5 8.6 %collective-permute-start.6 = (f32[5,16,128]{2,1,0:T(8,128)S(1)}, f32[5,16,128]{2,1,0:T(8,128)S(1)}, u32[]{:S(2)}, u32[]{:S(2)}) collective-permute-start(f32[5,16,128]{2,1,0:T(8,128)S(1)} %get-tuple-element.48), channel_id=1, source_target_pairs={{0,17},{1,16},{2,19},{3,18},{16,1},{17,0},{18,3},{19,2},{4,21},{5,... | collective-permute-start | bytes 122888 | tf_op jit(solution)/shard_map/ppermute | solution.py:776
  82.5 23.1 %collective-permute-start.19 = (f32[4,272,128]{2,1,0:T(8,128)}, f32[4,272,128]{2,1,0:T(8,128)S(1)}, u32[]{:S(2)}, u32[]{:S(2)}) collective-permute-start(f32[4,272,128]{2,1,0:T(8,128)} %copy-done.11), channel_id=1, source_target_pairs={{4,8},{8,4},{5,9},{9,5},{6,10},{10,6},{7,11},{11,7},{20,24},{24,20... | collective-permute-start | bytes 1671176 | tf_op jit(solution)/shard_map/ppermute | solution.py:844
  83.2 9.5 %collective-permute-start.13 = (f32[16,24,128]{2,1,0:T(8,128)S(1)}, f32[16,24,128]{2,1,0:T(8,128)S(1)}, u32[]{:S(2)}, u32[]{:S(2)}) collective-permute-start(f32[16,24,128]{2,1,0:T(8,128)S(1)} %all-to-all-done.here_ref), channel_id=1, source_target_pairs={{0,4},{4,0},{8,12},{12,8},{1,5},{5,1},{9,13},{13,9},{2,6},{6,2},{1... | collective-permute-start | bytes 589832 | tf_op jit(solution)/shard_map/ppermute | solution.py:775
  86.1 14.0 %collective-permute-start.14 = (f32[16,24,128]{2,1,0:T(8,128)S(1)}, f32[16,24,128]{2,1,0:T(8,128)S(1)}, u32[]{:S(2)}, u32[]{:S(2)}) collective-permute-start(f32[16,24,128]{2,1,0:T(8,128)S(1)} %all-to-all-done.here_ref), channel_id=1, source_target_pairs={{4,8},{8,4},{5,9},{9,5},{6,10},{10,6},{7,11},{11,7},{20,24},{24,20... | collective-permute-start | bytes 589832 | tf_op jit(solution)/shard_map/ppermute | solution.py:844
  89.9 30.7 %collective-permute-start.20 = (f32[4,272,128]{2,1,0:T(8,128)}, f32[4,272,128]{2,1,0:T(8,128)S(1)}, u32[]{:S(2)}, u32[]{:S(2)}) collective-permute-start(f32[4,272,128]{2,1,0:T(8,128)} %copy-done.9), channel_id=1, source_target_pairs={{0,4},{4,0},{8,12},{12,8},{1,5},{5,1},{9,13},{13,9},{2,6},{6,2},{1... | collective-permute-start | bytes 1671176 | tf_op jit(solution)/shard_map/ppermute | solution.py:775
  92.0 28.5 %collective-permute-start.21 = (f32[4,272,128]{2,1,0:T(8,128)}, f32[4,272,128]{2,1,0:T(8,128)S(1)}, u32[]{:S(2)}, u32[]{:S(2)}) collective-permute-start(f32[4,272,128]{2,1,0:T(8,128)} %copy-done.9), channel_id=1, source_target_pairs={{4,8},{8,4},{5,9},{9,5},{6,10},{10,6},{7,11},{11,7},{20,24},{24,20... | collective-permute-start | bytes 1671176 | tf_op jit(solution)/shard_map/ppermute | solution.py:844
  92.7 27.8 %collective-permute-start.22 = (f32[4,272,128]{2,1,0:T(8,128)}, f32[4,272,128]{2,1,0:T(8,128)S(1)}, u32[]{:S(2)}, u32[]{:S(2)}) collective-permute-start(f32[4,272,128]{2,1,0:T(8,128)} %copy-done.10), channel_id=1, source_target_pairs={{0,4},{4,0},{8,12},{12,8},{1,5},{5,1},{9,13},{13,9},{2,6},{6,2},{1... | collective-permute-start | bytes 1671176 | tf_op jit(solution)/shard_map/ppermute | solution.py:775
  100.2 20.4 %collective-permute-start.23 = (f32[4,272,128]{2,1,0:T(8,128)}, f32[4,272,128]{2,1,0:T(8,128)S(1)}, u32[]{:S(2)}, u32[]{:S(2)}) collective-permute-start(f32[4,272,128]{2,1,0:T(8,128)} %copy-done.10), channel_id=1, source_target_pairs={{4,8},{8,4},{5,9},{9,5},{6,10},{10,6},{7,11},{11,7},{20,24},{24,20... | collective-permute-start | bytes 1671176 | tf_op jit(solution)/shard_map/ppermute | solution.py:844
  130.4 8.5 %collective-permute-start.30 = (f32[1,24,128]{2,1,0:T(8,128)S(1)}, f32[1,24,128]{2,1,0:T(8,128)S(1)}, u32[]{:S(2)}, u32[]{:S(2)}) collective-permute-start(f32[1,24,128]{2,1,0:T(8,128)S(1)} %get-tuple-element.65), channel_id=1, source_target_pairs={{0,18},{1,19},{2,16},{3,17},{16,2},{17,3},{18,0},{19,1},{4,22},{5,... | collective-permute-start | bytes 36872 | tf_op jit(solution)/shard_map/ppermute | solution.py:776
  133.2 8.3 %collective-permute-start.25 = (f32[5,24,128]{2,1,0:T(8,128)S(1)}, f32[5,24,128]{2,1,0:T(8,128)S(1)}, u32[]{:S(2)}, u32[]{:S(2)}) collective-permute-start(f32[5,24,128]{2,1,0:T(8,128)S(1)} %get-tuple-element.63), channel_id=1, source_target_pairs={{0,1},{1,0},{2,3},{3,2},{4,5},{5,4},{6,7},{7,6},{8,9},{9,8},{10,11... | collective-permute-start | bytes 184328 | tf_op jit(solution)/shard_map/ppermute | solution.py:775
  133.2 8.3 %collective-permute-start.26 = (f32[5,24,128]{2,1,0:T(8,128)S(1)}, f32[5,24,128]{2,1,0:T(8,128)S(1)}, u32[]{:S(2)}, u32[]{:S(2)}) collective-permute-start(f32[5,24,128]{2,1,0:T(8,128)S(1)} %get-tuple-element.63), channel_id=1, source_target_pairs={{0,17},{1,16},{2,19},{3,18},{16,1},{17,0},{18,3},{19,2},{4,21},{5,... | collective-permute-start | bytes 184328 | tf_op jit(solution)/shard_map/ppermute | solution.py:776
  138.9 6.9 %collective-permute-start.28 = (f32[5,24,128]{2,1,0:T(8,128)S(1)}, f32[5,24,128]{2,1,0:T(8,128)S(1)}, u32[]{:S(2)}, u32[]{:S(2)}) collective-permute-start(f32[5,24,128]{2,1,0:T(8,128)S(1)} %get-tuple-element.64), channel_id=1, source_target_pairs={{0,19},{1,18},{2,17},{3,16},{16,3},{17,2},{18,1},{19,0},{4,23},{5,... | collective-permute-start | bytes 184328 | tf_op jit(solution)/shard_map/ppermute | solution.py:776
  149.3 6.5 %collective-permute-start.31 = (f32[5,24,128]{2,1,0:T(8,128)S(1)}, f32[5,24,128]{2,1,0:T(8,128)S(1)}, u32[]{:S(2)}, u32[]{:S(2)}) collective-permute-start(f32[5,24,128]{2,1,0:T(8,128)S(1)} %get-tuple-element.66.refs_6_), channel_id=1, source_target_pairs={{0,1},{1,0},{2,3},{3,2},{4,5},{5,4},{6,7},{7,6},{8,9},{9,8},{10,11... | collective-permute-start | bytes 184328 | tf_op jit(solution)/shard_map/ppermute | solution.py:775
  149.3 6.5 %collective-permute-start.32 = (f32[5,24,128]{2,1,0:T(8,128)S(1)}, f32[5,24,128]{2,1,0:T(8,128)S(1)}, u32[]{:S(2)}, u32[]{:S(2)}) collective-permute-start(f32[5,24,128]{2,1,0:T(8,128)S(1)} %get-tuple-element.66.refs_6_), channel_id=1, source_target_pairs={{0,3},{1,2},{2,1},{3,0},{4,7},{5,6},{6,5},{7,4},{8,11},{9,10},{10,... | collective-permute-start | bytes 184328 | tf_op jit(solution)/shard_map/ppermute | solution.py:775
  (29 other events, 174.3 us)

commit v4 on v2

--- a/solution.py
+++ b/solution.py
@@ -21,6 +21,7 @@
 SLOT = 2 * EDGE
 SLOTS = LANES // SLOT
 VMEM_CAP = 28 * 2**20
+VMEM_MOST = 60 * 2**20
 
 
 def passes(inside, times=4):
@@ -77,12 +78,12 @@
     return pl.BlockSpec(memory_space=pltpu.SMEM)
 
 
-def call(body, out_shape, flops=0, nbytes=0, **kw):
+def call(body, out_shape, flops=0, nbytes=0, cap=VMEM_CAP, **kw):
     return pl.pallas_call(
         body,
         out_shape=out_shape,
         cost_estimate=pl.CostEstimate(flops=int(flops), bytes_accessed=int(nbytes), transcendentals=0),
-        compiler_params=pltpu.CompilerParams(vmem_limit_bytes=VMEM_CAP),
+        compiler_params=pltpu.CompilerParams(vmem_limit_bytes=cap),
         **kw,
     )
 
@@ -323,7 +324,7 @@
         out = forward_rows(lat_ref, lambda l: z_in[l, sel, :], lambda l12: get(pu, pd, l12, sel), lats, halo)
         return tuple(a + b for a, b in zip(sums, out))
 
-    sums = lax.fori_loop(0, members, one, tuple(acc[l12] for l12 in halo), unroll=2)
+    sums = lax.fori_loop(0, members, one, tuple(acc[l12] for l12 in halo), unroll=4)
     for l12, value in zip(halo, sums):
         acc[l12] = value
 
@@ -350,6 +351,7 @@
         scratch_shapes=[pltpu.VMEM((lats + 9, channels, lon), F32)],
         flops=lats * rows * lon * 60,
         nbytes=z.size * 14,
+        cap=VMEM_MOST,
     )(lat_w, starts, z, zt, p_up, p_down, p_up, p_down, e_own)
 
 
@@ -393,7 +395,7 @@
     part = rows // SLOTS
     weights = w_ref[...]
     odd = flag[LEFT_A]
-    unroll = 2 if members % 2 == 0 else 1
+    unroll = 4 if members % 4 == 0 else 1
 
     def side_get(sides, l12, sel):
         if 4 <= l12 < 4 + lats:
@@ -634,12 +636,8 @@
             edge = pltpu.roll(jnp.where(lane < EDGE, right, left), EDGE, 1)
             b = ens_scale * repeat_slots(jnp.where(slot == 0, edge, 0.0))
         else:
-            earlier, own, other, na, na2, nb, nb2, nc, nc2 = s_refs
-            total = own[r] + other[r]
-            total = total + (flag[ABOVE_A] + flag[BELOW_A]) * (na[r] + na2[r])
-            total = total + (flag[ABOVE_B] + flag[BELOW_B]) * (nb[r] + nb2[r])
-            if r == lats:
-                total = total + flag[TWO_BELOW] * (nc[0] + nc2[0])
+            earlier, *parts = s_refs
+            total = neighbour_sum(flag, parts, r, lats)
             total = (1.0 - descent) * earlier[r] - (step_scale * ens_scale) * total
             a = total[:channels]
             b = widen(total[channels:])
@@ -725,6 +723,32 @@
             g1_ref[0, channels:, :] = edge
 
 
+def neighbour_sum(flag, parts, r, last):
+    own, other, na, na2, nb, nb2, nc, nc2 = parts
+    total = own[r] + other[r]
+    total = total + (flag[ABOVE_A] + flag[BELOW_A]) * (na[r] + na2[r])
+    total = total + (flag[ABOVE_B] + flag[BELOW_B]) * (nb[r] + nb2[r])
+    return total + flag[TWO_BELOW] * (nc[0] + nc2[0]) if r == last else total
+
+
+def combine_body(flag, *refs):
+    *parts, out_ref = refs
+    last = out_ref.shape[0] - 1
+    for r in range(last + 1):
+        out_ref[r] = neighbour_sum(flag, parts, r, last)
+
+
+def combine(flags, parts):
+    return call(
+        combine_body,
+        jax.ShapeDtypeStruct(parts[0].shape, F32),
+        in_specs=[smem()] + [vmem()] * len(parts),
+        out_specs=vmem(),
+        flops=parts[0].size * 8,
+        nbytes=parts[0].size * 32,
+    )(flags, *parts)
+
+
 def observe(flags, sums, records, channels, ens_scale, step_scale, lats):
     lon = sums[0].shape[2]
     slots = records[0].shape[1]
@@ -882,8 +906,7 @@
     arrived_beside = from_beside(arrived)
     records = index(flags, arrived, *arrived_beside, channels, lats, lon)
     own, own2, na, na2, nb, nb2, nc, nc2 = gather_rows(*e4)
-    s = own + own2 + (na + na2) + (flags[ABOVE_B] + flags[BELOW_B]) * (nb + nb2)
-    s = s + jnp.concatenate([jnp.zeros_like(s[:lats]), flags[TWO_BELOW] * (nc + nc2)], 0)
+    s = combine(flags, (own, own2, na, na2, nb, nb2, nc, nc2))
     sums = (s, swap(s, "gx", partner_a), swap(s, "gx", partner_b))
     x4 = (*x_own, *x_rest)
     scale = descent * ens_scale

time: 162 us -> 158 us (0.975)
  Pallas kernels: 39.5 us -> 41.6 us
  waiting for transfers between devices: 48.7 us -> 46.8 us
    ppermute x4, waiting for transfers between devices: 14.7 us -> 4.55 us  [from_beside(): return (swap(x, 'gx', partner_a), lax.ppermute(x, 'gx', inner))]
    ppermute x8, waiting for transfers between devices: 2.74 us -> 7.84 us  [swap(): lax.ppermute(block, ('mem', axis), [(m * count + i, (1 - m) * count + par...]
    ppermute x18, waiting for transfers between devices: 11.4 us -> 16.3 us  [swap(): lax.ppermute(block, axis, [(i, partner(i, count)) for i in range(count)])]
    ppermute x2, waiting for transfers between devices: 19.9 us -> 18.1 us  [shifted(): return lax.ppermute(block, axis, route)]
    unnamed x39 -> x45, local copies, waits for them, and re-layouts: 9.79 us -> 9.24 us
  transfers between devices with their start and end apart: 33 -> 33, of which waited for: 11 -> 13; matrix products, arithmetic and copies ran while one was open for 3% -> 3% of each run, Pallas kernels for 12% -> 14%
where the time goes in v4:
time: 158 us
  starting transfers between devices  54 us (34%)
  waiting for transfers between devices  46.8 us (30%)
  Pallas kernels  41.6 us (26%)
  local copies, waits for them, and re-layouts  13.5 us (9%)
    ppermute x2, waiting for transfers between devices, shifted(): return lax.ppermute(block, axis, route)  18.1 us
    pallas_call x2, Pallas kernels, member_step(): call(functools.partial(step_body, channels, n_mem, scale, last), out_shap...  16.8 us
    ppermute x18, waiting for transfers between devices, swap(): lax.ppermute(block, axis, [(i, partner(i, count)) for i in range(count)])  16.3 us
    ppermute x8, starting transfers between devices, swap(): lax.ppermute(block, ('mem', axis), [(m * count + i, (1 - m) * count + par...  15 us
    ppermute x18, starting transfers between devices, swap(): lax.ppermute(block, axis, [(i, partner(i, count)) for i in range(count)])  14.6 us
    ppermute x4, starting transfers between devices, from_beside(): return (swap(x, 'gx', partner_a), lax.ppermute(x, 'gx', inner))  10.8 us
    unnamed x45, local copies, waits for them, and re-layouts  9.24 us
    ppermute x8, waiting for transfers between devices, swap(): lax.ppermute(block, ('mem', axis), [(m * count + i, (1 - m) * count + par...  7.84 us
  transfers between devices with their start and end apart: 33, of which 13 were waited for; matrix products, arithmetic and copies ran while one was open for 3% of the time, Pallas kernels for 14%

profile of v4, /device:TPU:2, one launch (start us, length us, event | category | flops | bytes accessed | tf_op | source)
XLA Modules:
  0.0 157.7 jit_solution(2541773508410341651)
XLA Ops:
  2.3 5.0 %collective-permute-start.2 = (f32[4,1040,128]{2,1,0:T(8,128)S(1)}, f32[4,1040,128]{2,1,0:T(8,128)}, u32[]{:S(2)}, u32[]{:S(2)}) collective-permute-start(f32[4,1040,128]{2,1,0:T(8,128)S(1)} %pad_maximum_fusion.po.tpo.refs_8_.refs_15_.refs_14_.refs_21_), channel_id=1, source_target_pairs={{0,1},{1,2},{2,3},{4,5},{5,6},{6,7},{8,9},{9,10},{10,11},{12,13},{... | collective-permute-start | bytes 6389768 | tf_op jit(solution)/shard_map/ppermute | solution.py:777
  11.8 2.5 %collective-permute-start.1 = (f32[4,272,128]{2,1,0:T(8,128)}, f32[4,272,128]{2,1,0:T(8,128)S(1)}, u32[]{:S(2)}, u32[]{:S(2)}) collective-permute-start(f32[4,272,128]{2,1,0:T(8,128)} %get-tuple-element.36), channel_id=1, source_target_pairs={{4,8},{8,4},{5,9},{9,5},{6,10},{10,6},{7,11},{11,7},{20,24},{24,20... | collective-permute-start | bytes 1671176 | tf_op jit(solution)/shard_map/ppermute | solution.py:859
  17.4 3.4 %shard_map.150 = f32[16,24,128]{2,1,0:T(8,128)S(1)} custom-call(s32[1024,1]{1,0:T(8,128)S(1)} %copy-done.5, f32[16,1024]{1,0:T(8,128)S(1)} %bitcast.33, f32[4,1024]{1,0:T(4,128)S(1)} %copy-done.16, s32[1,1024]{1,0:T(1,128)S(1)} %bitcast.34, f32[1,1024]{1,0:T(1,128)S(1)} %bitcast.35, f32[1,1024]{1,0:T(1,128)S(1)} %bitcast.36), custom_call_target="tpu_custom_call" | custom-call | flops 314572800 | bytes 409600 | tf_op jit(solution)/shard_map/pallas_call | solution.py:559
  24.5 4.5 %shard_map.149 = (f32[4,1024,128]{2,1,0:T(8,128)S(1)}, f32[4,16,128]{2,1,0:T(8,128)S(1)}, f32[4,16,128]{2,1,0:T(8,128)S(1)}, f32[4,272,128]{2,1,0:T(8,128)S(1)}) custom-call(f32[48]{0:T(128)S(1)} %reshape_squeeze.3.lat_ref.refs_0_, f32[10]{0:T(128)S(1)} %convert_element_type.4.flag.refs_1_, f32[4,1024,128]{2,1,0:T(8,128)S(1)} %copy-done.1, ...), custom_call_target="tpu_custom_call" | custom-call | flops 52428800 | bytes 8388608 | tf_op jit(solution)/shard_map/pallas_call | solution.py:285
  32.4 7.4 %all-to-all-start = ((f32[16,24,128]{2,1,0:T(8,128)}), f32[16,24,128]{2,1,0:T(8,128)}, u32[]{:S(2)}, u32[]{:S(2)}) async-start(f32[16,24,128]{2,1,0:T(8,128)} %copy-done.6), calls=%async_computation | async-start | bytes 393216 | tf_op jit(solution)/shard_map/all_to_all | solution.py:902
  40.4 12.2 %collective-permute-done.2.pu.tpu_.refs_7_.refs_14_.refs_13_.refs_20_ = f32[4,1040,128]{2,1,0:T(8,128)} collective-permute-done((f32[4,1040,128]{2,1,0:T(8,128)S(1)}, f32[4,1040,128]{2,1,0:T(8,128)}, u32[]{:S(2)}, u32[]{:S(2)}) %collective-permute-start.2) | collective-permute-done | bytes 2129952 | tf_op jit(solution)/shard_map/ppermute | solution.py:777
  52.7 5.9 %collective-permute-done.3.pd.tpd.refs_9_.refs_16_.refs_15_.refs_22_ = f32[4,1040,128]{2,1,0:T(8,128)} collective-permute-done((f32[4,1040,128]{2,1,0:T(8,128)S(1)}, f32[4,1040,128]{2,1,0:T(8,128)}, u32[]{:S(2)}, u32[]{:S(2)}) %collective-permute-start.3) | collective-permute-done | bytes 2129952 | tf_op jit(solution)/shard_map/ppermute | solution.py:777
  58.5 5.9 %shard_map.151 = (f32[5,16,128]{2,1,0:T(8,128)}, f32[5,16,128]{2,1,0:T(8,128)}, f32[5,16,128]{2,1,0:T(8,128)}, f32[1,16,128]{2,1,0:T(8,128)}, f32[8,272,128]{2,1,0:T(8,128)}) custom-call(f32[48]{0:T(128)} %copy-done.11, s32[2]{0:T(128)} %add_select_fusion.start.refs_2_, f32[4,1024,128]{2,1,0:T(8,128)} %copy-done.4, f32[4,16,128]{2,1,0:T(8,128)} %copy-done.9, ...), custom_call_target="tpu_custom_call" | custom-call | flops 31457280 | bytes 7340032 | tf_op jit(solution)/shard_map/pallas_call | solution.py:345
  64.4 2.5 %collective-permute-start.21 = (f32[8,272,128]{2,1,0:T(8,128)}, f32[8,272,128]{2,1,0:T(8,128)}, u32[]{:S(2)}, u32[]{:S(2)}) collective-permute-start(f32[8,272,128]{2,1,0:T(8,128)} %get-tuple-element.57), channel_id=1, source_target_pairs={{4,8},{8,4},{5,9},{9,5},{6,10},{10,6},{7,11},{11,7},{20,24},{24,20... | collective-permute-start | bytes 3342344 | tf_op jit(solution)/shard_map/ppermute | solution.py:859
  69.7 5.1 %collective-permute-done.10.refs_7_ = f32[1,16,128]{2,1,0:T(8,128)S(1)} collective-permute-done((f32[1,16,128]{2,1,0:T(8,128)}, f32[1,16,128]{2,1,0:T(8,128)S(1)}, u32[]{:S(2)}, u32[]{:S(2)}) %collective-permute-start.10) | collective-permute-done | bytes 8224 | tf_op jit(solution)/shard_map/ppermute | solution.py:792
  75.5 4.2 %collective-permute-done.9.refs_6_ = f32[1,16,128]{2,1,0:T(8,128)S(1)} collective-permute-done((f32[1,16,128]{2,1,0:T(8,128)}, f32[1,16,128]{2,1,0:T(8,128)S(1)}, u32[]{:S(2)}, u32[]{:S(2)}) %collective-permute-start.9) | collective-permute-done | bytes 8224 | tf_op jit(solution)/shard_map/ppermute | solution.py:791
  81.7 4.2 %collective-permute-start.8 = (f32[5,16,128]{2,1,0:T(8,128)}, f32[5,16,128]{2,1,0:T(8,128)S(1)}, u32[]{:S(2)}, u32[]{:S(2)}) collective-permute-start(f32[5,16,128]{2,1,0:T(8,128)} %get-tuple-element.46), channel_id=1, source_target_pairs={{0,19},{1,18},{2,17},{3,16},{16,3},{17,2},{18,1},{19,0},{4,23},{5,... | collective-permute-start | bytes 122888 | tf_op jit(solution)/shard_map/ppermute | solution.py:792
  93.3 3.8 %collective-permute-start.14 = (f32[16,24,128]{2,1,0:T(8,128)}, f32[16,24,128]{2,1,0:T(8,128)S(1)}, u32[]{:S(2)}, u32[]{:S(2)}) collective-permute-start(f32[16,24,128]{2,1,0:T(8,128)} %all-to-all-done.here_ref), channel_id=1, source_target_pairs={{4,8},{8,4},{5,9},{9,5},{6,10},{10,6},{7,11},{11,7},{20,24},{24,20... | collective-permute-start | bytes 589832 | tf_op jit(solution)/shard_map/ppermute | solution.py:859
  97.1 3.6 %collective-permute-done.14.b_ref = f32[16,24,128]{2,1,0:T(8,128)S(1)} collective-permute-done((f32[16,24,128]{2,1,0:T(8,128)}, f32[16,24,128]{2,1,0:T(8,128)S(1)}, u32[]{:S(2)}, u32[]{:S(2)}) %collective-permute-start.14) | collective-permute-done | bytes 196640 | tf_op jit(solution)/shard_map/ppermute | solution.py:859
  104.1 3.1 %shard_map.154 = (f32[5,24,128]{2,1,0:T(8,128)S(1)}, f32[1,24,128]{2,1,0:T(8,128)S(1)}, f32[5,24,128]{2,1,0:T(8,128)S(1)}) custom-call(f32[10]{0:T(128)S(1)} %convert_element_type.4.flag.refs_1_, f32[5,16,128]{2,1,0:T(8,128)S(1)} %shard_map.152.refs_0_, f32[5,16,128]{2,1,0:T(8,128)S(1)} %collective-permute-done.11.refs_1_, ...), custom_call_target="tpu_custom_call" | custom-call | flops 805306368 | bytes 4194304 | tf_op jit(solution)/shard_map/pallas_call | solution.py:758
  107.3 2.6 %collective-permute-start.16 = (f32[5,24,128]{2,1,0:T(8,128)S(1)}, f32[5,24,128]{2,1,0:T(8,128)S(1)}, u32[]{:S(2)}, u32[]{:S(2)}) collective-permute-start(f32[5,24,128]{2,1,0:T(8,128)S(1)} %get-tuple-element.54.refs_6_.refs_10_), channel_id=1, source_target_pairs={{0,3},{1,2},{2,1},{3,0},{4,7},{5,6},{6,5},{7,4},{8,11},{9,10},{10,... | collective-permute-start | bytes 184328 | tf_op jit(solution)/shard_map/ppermute | solution.py:791
  111.8 2.8 %collective-permute-done.17.refs_5_.refs_9_ = f32[1,24,128]{2,1,0:T(8,128)S(1)} collective-permute-done((f32[1,24,128]{2,1,0:T(8,128)S(1)}, f32[1,24,128]{2,1,0:T(8,128)S(1)}, u32[]{:S(2)}, u32[]{:S(2)}) %collective-permute-start.17) | collective-permute-done | bytes 12320 | tf_op jit(solution)/shard_map/ppermute | solution.py:791
  114.6 9.2 %shard_map.155 = (f32[5,24,128]{2,1,0:T(8,128)S(1)}, f32[5,24,128]{2,1,0:T(8,128)S(1)}, f32[5,24,128]{2,1,0:T(8,128)S(1)}, f32[1,24,128]{2,1,0:T(8,128)S(1)}) custom-call(f32[48]{0:T(128)S(1)} %copy-done.12, f32[10]{0:T(128)S(1)} %convert_element_type.4.flag.refs_1_, s32[2]{0:T(128)S(1)} %copy-done.13, ...), custom_call_target="tpu_custom_call" | custom-call | flops 314572800 | bytes 12582912 | tf_op jit(solution)/shard_map/pallas_call | solution.py:512
  124.7 3.1 %collective-permute-start.28 = (f32[1,24,128]{2,1,0:T(8,128)S(1)}, f32[1,24,128]{2,1,0:T(8,128)S(1)}, u32[]{:S(2)}, u32[]{:S(2)}) collective-permute-start(f32[1,24,128]{2,1,0:T(8,128)S(1)} %get-tuple-element.61), channel_id=1, source_target_pairs={{0,18},{1,19},{2,16},{3,17},{16,2},{17,3},{18,0},{19,1},{4,22},{5,... | collective-permute-start | bytes 36872 | tf_op jit(solution)/shard_map/ppermute | solution.py:792
  135.0 2.4 %collective-permute-done.25.refs_5_ = f32[5,24,128]{2,1,0:T(8,128)S(1)} collective-permute-done((f32[5,24,128]{2,1,0:T(8,128)S(1)}, f32[5,24,128]{2,1,0:T(8,128)S(1)}, u32[]{:S(2)}, u32[]{:S(2)}) %collective-permute-start.25) | collective-permute-done | bytes 61472 | tf_op jit(solution)/shard_map/ppermute | solution.py:791
  137.4 2.7 %collective-permute-done.26.refs_6_ = f32[5,24,128]{2,1,0:T(8,128)S(1)} collective-permute-done((f32[5,24,128]{2,1,0:T(8,128)S(1)}, f32[5,24,128]{2,1,0:T(8,128)S(1)}, u32[]{:S(2)}, u32[]{:S(2)}) %collective-permute-start.26) | collective-permute-done | bytes 61472 | tf_op jit(solution)/shard_map/ppermute | solution.py:792
  140.1 3.5 %shard_map.156 = (f32[5,24,128]{2,1,0:T(8,128)S(1)}, f32[1,24,128]{2,1,0:T(8,128)S(1)}, f32[64,128]{1,0:T(8,128)}) custom-call(f32[10]{0:T(128)S(1)} %convert_element_type.4.flag.refs_1_, f32[5,24,128]{2,1,0:T(8,128)S(1)} %get-tuple-element.53.refs_0_, f32[5,24,128]{2,1,0:T(8,128)S(1)} %get-tuple-element.58.refs_1_, ...), custom_call_target="tpu_custom_call" | custom-call | flops 805306368 | bytes 4194304 | tf_op jit(solution)/shard_map/pallas_call | solution.py:758
  147.1 3.0 %collective-permute-done.31.refs_5_ = f32[1,24,128]{2,1,0:T(8,128)S(1)} collective-permute-done((f32[1,24,128]{2,1,0:T(8,128)S(1)}, f32[1,24,128]{2,1,0:T(8,128)S(1)}, u32[]{:S(2)}, u32[]{:S(2)}) %collective-permute-start.31) | collective-permute-done | bytes 12320 | tf_op jit(solution)/shard_map/ppermute | solution.py:791
  150.1 7.6 %shard_map.157 = (f32[4096,128]{1,0:T(8,128)}, f32[64,128]{1,0:T(8,128)}) custom-call(f32[48]{0:T(128)S(1)} %copy-done.12, f32[10]{0:T(128)S(1)} %convert_element_type.4.flag.refs_1_, s32[2]{0:T(128)S(1)} %copy-done.13, f32[5,24,128]{2,1,0:T(8,128)S(1)} %collective-permute-done.29.refs_3_, f32[5,24,128]{2,1,0:T(8,128)S(1)} %collective-permute-done.30.refs_4_, ...), custom_call_target="tpu_custom_call" | custom-call | flops 314572800 | bytes 12582912 | tf_op jit(solution)/shard_map/pallas_call | solution.py:512
  (108 shorter events, 46.4 us)
Async XLA Ops:
  2.3 50.3 %collective-permute-start.2 = (f32[4,1040,128]{2,1,0:T(8,128)S(1)}, f32[4,1040,128]{2,1,0:T(8,128)}, u32[]{:S(2)}, u32[]{:S(2)}) collective-permute-start(f32[4,1040,128]{2,1,0:T(8,128)S(1)} %pad_maximum_fusion.po.tpo.refs_8_.refs_15_.refs_14_.refs_21_), channel_id=1, source_target_pairs={{0,1},{1,2},{2,3},{4,5},{5,6},{6,7},{8,9},{9,10},{10,11},{12,13},{... | collective-permute-start | bytes 6389768 | tf_op jit(solution)/shard_map/ppermute | solution.py:777
  7.3 51.2 %collective-permute-start.3 = (f32[4,1040,128]{2,1,0:T(8,128)S(1)}, f32[4,1040,128]{2,1,0:T(8,128)}, u32[]{:S(2)}, u32[]{:S(2)}) collective-permute-start(f32[4,1040,128]{2,1,0:T(8,128)S(1)} %pad_maximum_fusion.po.tpo.refs_8_.refs_15_.refs_14_.refs_21_), channel_id=1, source_target_pairs={{1,0},{2,1},{3,2},{5,4},{6,5},{7,6},{9,8},{10,9},{11,10},{13,12},{... | collective-permute-start | bytes 6389768 | tf_op jit(solution)/shard_map/ppermute | solution.py:777
  11.8 10.1 %collective-permute-start = (f32[4,272,128]{2,1,0:T(8,128)}, f32[4,272,128]{2,1,0:T(8,128)S(1)}, u32[]{:S(2)}, u32[]{:S(2)}) collective-permute-start(f32[4,272,128]{2,1,0:T(8,128)} %get-tuple-element.36), channel_id=1, source_target_pairs={{0,4},{4,0},{8,12},{12,8},{1,5},{5,1},{9,13},{13,9},{2,6},{6,2},{1... | collective-permute-start | bytes 1671176 | tf_op jit(solution)/shard_map/ppermute | solution.py:791
  11.8 11.0 %collective-permute-start.1 = (f32[4,272,128]{2,1,0:T(8,128)}, f32[4,272,128]{2,1,0:T(8,128)S(1)}, u32[]{:S(2)}, u32[]{:S(2)}) collective-permute-start(f32[4,272,128]{2,1,0:T(8,128)} %get-tuple-element.36), channel_id=1, source_target_pairs={{4,8},{8,4},{5,9},{9,5},{6,10},{10,6},{7,11},{11,7},{20,24},{24,20... | collective-permute-start | bytes 1671176 | tf_op jit(solution)/shard_map/ppermute | solution.py:859
  32.4 34.6 %all-to-all-start = ((f32[16,24,128]{2,1,0:T(8,128)}), f32[16,24,128]{2,1,0:T(8,128)}, u32[]{:S(2)}, u32[]{:S(2)}) async-start(f32[16,24,128]{2,1,0:T(8,128)} %copy-done.6), calls=%async_computation | async-start | bytes 393216 | tf_op jit(solution)/shard_map/all_to_all | solution.py:902
  64.4 50.1 %collective-permute-start.20 = (f32[8,272,128]{2,1,0:T(8,128)}, f32[8,272,128]{2,1,0:T(8,128)S(1)}, u32[]{:S(2)}, u32[]{:S(2)}) collective-permute-start(f32[8,272,128]{2,1,0:T(8,128)} %get-tuple-element.57), channel_id=1, source_target_pairs={{0,4},{4,0},{8,12},{12,8},{1,5},{5,1},{9,13},{13,9},{2,6},{6,2},{1... | collective-permute-start | bytes 3342344 | tf_op jit(solution)/shard_map/ppermute | solution.py:791
  64.4 50.1 %collective-permute-start.21 = (f32[8,272,128]{2,1,0:T(8,128)}, f32[8,272,128]{2,1,0:T(8,128)}, u32[]{:S(2)}, u32[]{:S(2)}) collective-permute-start(f32[8,272,128]{2,1,0:T(8,128)} %get-tuple-element.57), channel_id=1, source_target_pairs={{4,8},{8,4},{5,9},{9,5},{6,10},{10,6},{7,11},{11,7},{20,24},{24,20... | collective-permute-start | bytes 3342344 | tf_op jit(solution)/shard_map/ppermute | solution.py:859
  67.0 14.0 %collective-permute-start.4 = (f32[5,16,128]{2,1,0:T(8,128)}, f32[5,16,128]{2,1,0:T(8,128)S(1)}, u32[]{:S(2)}, u32[]{:S(2)}) collective-permute-start(f32[5,16,128]{2,1,0:T(8,128)} %get-tuple-element.44.refs_0_), channel_id=1, source_target_pairs={{0,16},{1,17},{2,18},{3,19},{16,0},{17,1},{18,2},{19,3},{4,20},{5,... | collective-permute-start | bytes 122888 | tf_op jit(solution)/shard_map/ppermute | solution.py:792
  68.6 13.1 %collective-permute-start.5 = (f32[5,16,128]{2,1,0:T(8,128)}, f32[5,16,128]{2,1,0:T(8,128)S(1)}, u32[]{:S(2)}, u32[]{:S(2)}) collective-permute-start(f32[5,16,128]{2,1,0:T(8,128)} %get-tuple-element.45), channel_id=1, source_target_pairs={{0,1},{1,0},{2,3},{3,2},{4,5},{5,4},{6,7},{7,6},{8,9},{9,8},{10,11... | collective-permute-start | bytes 122888 | tf_op jit(solution)/shard_map/ppermute | solution.py:791
  79.6 6.2 %collective-permute-start.6 = (f32[5,16,128]{2,1,0:T(8,128)}, f32[5,16,128]{2,1,0:T(8,128)S(1)}, u32[]{:S(2)}, u32[]{:S(2)}) collective-permute-start(f32[5,16,128]{2,1,0:T(8,128)} %get-tuple-element.45), channel_id=1, source_target_pairs={{0,17},{1,16},{2,19},{3,18},{16,1},{17,0},{18,3},{19,2},{4,21},{5,... | collective-permute-start | bytes 122888 | tf_op jit(solution)/shard_map/ppermute | solution.py:792
  81.7 7.3 %collective-permute-start.8 = (f32[5,16,128]{2,1,0:T(8,128)}, f32[5,16,128]{2,1,0:T(8,128)S(1)}, u32[]{:S(2)}, u32[]{:S(2)}) collective-permute-start(f32[5,16,128]{2,1,0:T(8,128)} %get-tuple-element.46), channel_id=1, source_target_pairs={{0,19},{1,18},{2,17},{3,16},{16,3},{17,2},{18,1},{19,0},{4,23},{5,... | collective-permute-start | bytes 122888 | tf_op jit(solution)/shard_map/ppermute | solution.py:792
  85.9 21.5 %collective-permute-start.18 = (f32[4,272,128]{2,1,0:T(8,128)}, f32[4,272,128]{2,1,0:T(8,128)S(1)}, u32[]{:S(2)}, u32[]{:S(2)}) collective-permute-start(f32[4,272,128]{2,1,0:T(8,128)} %copy-done.14), channel_id=1, source_target_pairs={{0,4},{4,0},{8,12},{12,8},{1,5},{5,1},{9,13},{13,9},{2,6},{6,2},{1... | collective-permute-start | bytes 1671176 | tf_op jit(solution)/shard_map/ppermute | solution.py:791
  87.1 22.9 %collective-permute-start.19 = (f32[4,272,128]{2,1,0:T(8,128)}, f32[4,272,128]{2,1,0:T(8,128)S(1)}, u32[]{:S(2)}, u32[]{:S(2)}) collective-permute-start(f32[4,272,128]{2,1,0:T(8,128)} %copy-done.14), channel_id=1, source_target_pairs={{4,8},{8,4},{5,9},{9,5},{6,10},{10,6},{7,11},{11,7},{20,24},{24,20... | collective-permute-start | bytes 1671176 | tf_op jit(solution)/shard_map/ppermute | solution.py:859
  93.3 7.4 %collective-permute-start.14 = (f32[16,24,128]{2,1,0:T(8,128)}, f32[16,24,128]{2,1,0:T(8,128)S(1)}, u32[]{:S(2)}, u32[]{:S(2)}) collective-permute-start(f32[16,24,128]{2,1,0:T(8,128)} %all-to-all-done.here_ref), channel_id=1, source_target_pairs={{4,8},{8,4},{5,9},{9,5},{6,10},{10,6},{7,11},{11,7},{20,24},{24,20... | collective-permute-start | bytes 589832 | tf_op jit(solution)/shard_map/ppermute | solution.py:859
  107.2 7.3 %collective-permute-start.15 = (f32[5,24,128]{2,1,0:T(8,128)S(1)}, f32[5,24,128]{2,1,0:T(8,128)S(1)}, u32[]{:S(2)}, u32[]{:S(2)}) collective-permute-start(f32[5,24,128]{2,1,0:T(8,128)S(1)} %get-tuple-element.54.refs_6_.refs_10_), channel_id=1, source_target_pairs={{0,1},{1,0},{2,3},{3,2},{4,5},{5,4},{6,7},{7,6},{8,9},{9,8},{10,11... | collective-permute-start | bytes 184328 | tf_op jit(solution)/shard_map/ppermute | solution.py:791
  107.3 7.2 %collective-permute-start.16 = (f32[5,24,128]{2,1,0:T(8,128)S(1)}, f32[5,24,128]{2,1,0:T(8,128)S(1)}, u32[]{:S(2)}, u32[]{:S(2)}) collective-permute-start(f32[5,24,128]{2,1,0:T(8,128)S(1)} %get-tuple-element.54.refs_6_.refs_10_), channel_id=1, source_target_pairs={{0,3},{1,2},{2,1},{3,0},{4,7},{5,6},{6,5},{7,4},{8,11},{9,10},{10,... | collective-permute-start | bytes 184328 | tf_op jit(solution)/shard_map/ppermute | solution.py:791
  123.8 7.5 %collective-permute-start.27 = (f32[1,24,128]{2,1,0:T(8,128)S(1)}, f32[1,24,128]{2,1,0:T(8,128)S(1)}, u32[]{:S(2)}, u32[]{:S(2)}) collective-permute-start(f32[1,24,128]{2,1,0:T(8,128)S(1)} %get-tuple-element.61), channel_id=1, source_target_pairs={{0,2},{1,3},{2,0},{3,1},{4,6},{5,7},{6,4},{7,5},{8,10},{9,11},{10,... | collective-permute-start | bytes 36872 | tf_op jit(solution)/shard_map/ppermute | solution.py:791
  124.7 8.5 %collective-permute-start.28 = (f32[1,24,128]{2,1,0:T(8,128)S(1)}, f32[1,24,128]{2,1,0:T(8,128)S(1)}, u32[]{:S(2)}, u32[]{:S(2)}) collective-permute-start(f32[1,24,128]{2,1,0:T(8,128)S(1)} %get-tuple-element.61), channel_id=1, source_target_pairs={{0,18},{1,19},{2,16},{3,17},{16,2},{17,3},{18,0},{19,1},{4,22},{5,... | collective-permute-start | bytes 36872 | tf_op jit(solution)/shard_map/ppermute | solution.py:792
  127.8 7.2 %collective-permute-start.23 = (f32[5,24,128]{2,1,0:T(8,128)S(1)}, f32[5,24,128]{2,1,0:T(8,128)S(1)}, u32[]{:S(2)}, u32[]{:S(2)}) collective-permute-start(f32[5,24,128]{2,1,0:T(8,128)S(1)} %get-tuple-element.59), channel_id=1, source_target_pairs={{0,1},{1,0},{2,3},{3,2},{4,5},{5,4},{6,7},{7,6},{8,9},{9,8},{10,11... | collective-permute-start | bytes 184328 | tf_op jit(solution)/shard_map/ppermute | solution.py:791
  128.8 6.2 %collective-permute-start.24 = (f32[5,24,128]{2,1,0:T(8,128)S(1)}, f32[5,24,128]{2,1,0:T(8,128)S(1)}, u32[]{:S(2)}, u32[]{:S(2)}) collective-permute-start(f32[5,24,128]{2,1,0:T(8,128)S(1)} %get-tuple-element.59), channel_id=1, source_target_pairs={{0,17},{1,16},{2,19},{3,18},{16,1},{17,0},{18,3},{19,2},{4,21},{5,... | collective-permute-start | bytes 184328 | tf_op jit(solution)/shard_map/ppermute | solution.py:792
  131.3 6.2 %collective-permute-start.25 = (f32[5,24,128]{2,1,0:T(8,128)S(1)}, f32[5,24,128]{2,1,0:T(8,128)S(1)}, u32[]{:S(2)}, u32[]{:S(2)}) collective-permute-start(f32[5,24,128]{2,1,0:T(8,128)S(1)} %get-tuple-element.60), channel_id=1, source_target_pairs={{0,3},{1,2},{2,1},{3,0},{4,7},{5,6},{6,5},{7,4},{8,11},{9,10},{10,... | collective-permute-start | bytes 184328 | tf_op jit(solution)/shard_map/ppermute | solution.py:791
  133.2 6.9 %collective-permute-start.26 = (f32[5,24,128]{2,1,0:T(8,128)S(1)}, f32[5,24,128]{2,1,0:T(8,128)S(1)}, u32[]{:S(2)}, u32[]{:S(2)}) collective-permute-start(f32[5,24,128]{2,1,0:T(8,128)S(1)} %get-tuple-element.60), channel_id=1, source_target_pairs={{0,19},{1,18},{2,17},{3,16},{16,3},{17,2},{18,1},{19,0},{4,23},{5,... | collective-permute-start | bytes 184328 | tf_op jit(solution)/shard_map/ppermute | solution.py:792
  143.6 6.5 %collective-permute-start.29 = (f32[5,24,128]{2,1,0:T(8,128)S(1)}, f32[5,24,128]{2,1,0:T(8,128)S(1)}, u32[]{:S(2)}, u32[]{:S(2)}) collective-permute-start(f32[5,24,128]{2,1,0:T(8,128)S(1)} %get-tuple-element.62.refs_6_), channel_id=1, source_target_pairs={{0,1},{1,0},{2,3},{3,2},{4,5},{5,4},{6,7},{7,6},{8,9},{9,8},{10,11... | collective-permute-start | bytes 184328 | tf_op jit(solution)/shard_map/ppermute | solution.py:791
  143.6 6.5 %collective-permute-start.30 = (f32[5,24,128]{2,1,0:T(8,128)S(1)}, f32[5,24,128]{2,1,0:T(8,128)S(1)}, u32[]{:S(2)}, u32[]{:S(2)}) collective-permute-start(f32[5,24,128]{2,1,0:T(8,128)S(1)} %get-tuple-element.62.refs_6_), channel_id=1, source_target_pairs={{0,3},{1,2},{2,1},{3,0},{4,7},{5,6},{6,5},{7,4},{8,11},{9,10},{10,... | collective-permute-start | bytes 184328 | tf_op jit(solution)/shard_map/ppermute | solution.py:791
  (31 other events, 190.0 us)

commit v5 on v4

--- a/solution.py
+++ b/solution.py
@@ -324,7 +324,7 @@
         out = forward_rows(lat_ref, lambda l: z_in[l, sel, :], lambda l12: get(pu, pd, l12, sel), lats, halo)
         return tuple(a + b for a, b in zip(sums, out))
 
-    sums = lax.fori_loop(0, members, one, tuple(acc[l12] for l12 in halo), unroll=4)
+    sums = lax.fori_loop(0, members, one, tuple(acc[l12] for l12 in halo), unroll=8)
     for l12, value in zip(halo, sums):
         acc[l12] = value
 
@@ -395,7 +395,7 @@
     part = rows // SLOTS
     weights = w_ref[...]
     odd = flag[LEFT_A]
-    unroll = 4 if members % 4 == 0 else 1
+    unroll = 8 if members % 8 == 0 else 1
 
     def side_get(sides, l12, sel):
         if 4 <= l12 < 4 + lats:
@@ -836,7 +836,7 @@
     assert n_mem == 2 and n_gx % 2 == 0 and n_gy % 2 == 0
     ens_scale = ens_share / math.sqrt(members * n_mem - 1)
     rows = members * channels
-    step_rows = (16 if members % 16 == 0 else 8) * channels
+    step_rows = next(c for c in (32, 16, 8) if members % c == 0) * channels
 
     def lat_major(x, count):
         return x.reshape(count, lats, lon).transpose(1, 0, 2)

time: 158 us -> 157 us (level)
  the two profiles are of different devices: /device:TPU:2 before, /device:TPU:0 now
where the time goes in v5:
time: 157 us; the launch traced here: 154 us
  starting transfers between devices  52.4 us (33%)
  waiting for transfers between devices  46.7 us (30%)
  Pallas kernels  39.1 us (25%)
  local copies, waits for them, and re-layouts  13.5 us (9%)
    ppermute x2, waiting for transfers between devices, shifted(): return lax.ppermute(block, axis, route)  19.3 us
    ppermute x18, waiting for transfers between devices, swap(): lax.ppermute(block, axis, [(i, partner(i, count)) for i in range(count)])  18.3 us
    ppermute x18, starting transfers between devices, swap(): lax.ppermute(block, axis, [(i, partner(i, count)) for i in range(count)])  16.2 us
    pallas_call x2, Pallas kernels, member_step(): call(functools.partial(step_body, channels, n_mem, scale, last), out_shap...  15.9 us
    ppermute x8, starting transfers between devices, swap(): lax.ppermute(block, ('mem', axis), [(m * count + i, (1 - m) * count + par...  14.7 us
    all_to_all x1, starting transfers between devices, assimilate(): lax.all_to_all(sent, ('gx', 'gy'), split_axis=0, concat_axis=0, tiled=True)  9.82 us
    unnamed x45, local copies, waits for them, and re-layouts  9.24 us
    ppermute x8, waiting for transfers between devices, swap(): lax.ppermute(block, ('mem', axis), [(m * count + i, (1 - m) * count + par...  9.1 us
  transfers between devices with their start and end apart: 33, of which 13 were waited for; matrix products, arithmetic and copies ran while one was open for 3% of the time, Pallas kernels for 13%

profile of v5, /device:TPU:0, one launch (start us, length us, event | category | flops | bytes accessed | tf_op | source)
XLA Modules:
  0.0 153.6 jit_solution(3516805730190538971)
XLA Ops:
  2.3 6.5 %collective-permute-start.2 = (f32[4,1040,128]{2,1,0:T(8,128)S(1)}, f32[4,1040,128]{2,1,0:T(8,128)}, u32[]{:S(2)}, u32[]{:S(2)}) collective-permute-start(f32[4,1040,128]{2,1,0:T(8,128)S(1)} %pad_maximum_fusion.po.tpo.refs_8_.refs_15_.refs_14_.refs_21_), channel_id=1, source_target_pairs={{0,1},{1,2},{2,3},{4,5},{5,6},{6,7},{8,9},{9,10},{10,11},{12,13},{... | collective-permute-start | bytes 6389768 | tf_op jit(solution)/shard_map/ppermute | solution.py:777
  16.9 3.4 %shard_map.150 = f32[16,24,128]{2,1,0:T(8,128)S(1)} custom-call(s32[1024,1]{1,0:T(8,128)S(1)} %copy-done.5, f32[16,1024]{1,0:T(8,128)S(1)} %bitcast.33, f32[4,1024]{1,0:T(4,128)S(1)} %copy-done.16, s32[1,1024]{1,0:T(1,128)S(1)} %bitcast.34, f32[1,1024]{1,0:T(1,128)S(1)} %bitcast.35, f32[1,1024]{1,0:T(1,128)S(1)} %bitcast.36), custom_call_target="tpu_custom_call" | custom-call | flops 314572800 | bytes 409600 | tf_op jit(solution)/shard_map/pallas_call | solution.py:559
  23.0 3.8 %shard_map.149 = (f32[4,1024,128]{2,1,0:T(8,128)S(1)}, f32[4,16,128]{2,1,0:T(8,128)S(1)}, f32[4,16,128]{2,1,0:T(8,128)S(1)}, f32[4,272,128]{2,1,0:T(8,128)S(1)}) custom-call(f32[48]{0:T(128)S(1)} %reshape_squeeze.3.lat_ref.refs_0_, f32[10]{0:T(128)S(1)} %convert_element_type.4.flag.refs_1_, f32[4,1024,128]{2,1,0:T(8,128)S(1)} %copy-done.1, ...), custom_call_target="tpu_custom_call" | custom-call | flops 52428800 | bytes 8388608 | tf_op jit(solution)/shard_map/pallas_call | solution.py:285
  30.2 9.8 %all-to-all-start = ((f32[16,24,128]{2,1,0:T(8,128)}), f32[16,24,128]{2,1,0:T(8,128)}, u32[]{:S(2)}, u32[]{:S(2)}) async-start(f32[16,24,128]{2,1,0:T(8,128)} %copy-done.6), calls=%async_computation | async-start | bytes 393216 | tf_op jit(solution)/shard_map/all_to_all | solution.py:902
  40.7 13.5 %collective-permute-done.2.pu.tpu_.refs_7_.refs_14_.refs_13_.refs_20_ = f32[4,1040,128]{2,1,0:T(8,128)} collective-permute-done((f32[4,1040,128]{2,1,0:T(8,128)S(1)}, f32[4,1040,128]{2,1,0:T(8,128)}, u32[]{:S(2)}, u32[]{:S(2)}) %collective-permute-start.2) | collective-permute-done | bytes 2129952 | tf_op jit(solution)/shard_map/ppermute | solution.py:777
  54.1 5.9 %collective-permute-done.3.pd.tpd.refs_9_.refs_16_.refs_15_.refs_22_ = f32[4,1040,128]{2,1,0:T(8,128)} collective-permute-done((f32[4,1040,128]{2,1,0:T(8,128)S(1)}, f32[4,1040,128]{2,1,0:T(8,128)}, u32[]{:S(2)}, u32[]{:S(2)}) %collective-permute-start.3) | collective-permute-done | bytes 2129952 | tf_op jit(solution)/shard_map/ppermute | solution.py:777
  60.0 5.2 %shard_map.151 = (f32[5,16,128]{2,1,0:T(8,128)}, f32[5,16,128]{2,1,0:T(8,128)}, f32[5,16,128]{2,1,0:T(8,128)}, f32[1,16,128]{2,1,0:T(8,128)}, f32[8,272,128]{2,1,0:T(8,128)}) custom-call(f32[48]{0:T(128)} %copy-done.11, s32[2]{0:T(128)} %add_select_fusion.start.refs_2_, f32[4,1024,128]{2,1,0:T(8,128)} %copy-done.4, f32[4,16,128]{2,1,0:T(8,128)} %copy-done.9, ...), custom_call_target="tpu_custom_call" | custom-call | flops 31457280 | bytes 7340032 | tf_op jit(solution)/shard_map/pallas_call | solution.py:345
  69.6 5.1 %collective-permute-done.10.refs_7_ = f32[1,16,128]{2,1,0:T(8,128)S(1)} collective-permute-done((f32[1,16,128]{2,1,0:T(8,128)}, f32[1,16,128]{2,1,0:T(8,128)S(1)}, u32[]{:S(2)}, u32[]{:S(2)}) %collective-permute-start.10) | collective-permute-done | bytes 8224 | tf_op jit(solution)/shard_map/ppermute | solution.py:792
  75.4 4.2 %collective-permute-done.9.refs_6_ = f32[1,16,128]{2,1,0:T(8,128)S(1)} collective-permute-done((f32[1,16,128]{2,1,0:T(8,128)}, f32[1,16,128]{2,1,0:T(8,128)S(1)}, u32[]{:S(2)}, u32[]{:S(2)}) %collective-permute-start.9) | collective-permute-done | bytes 8224 | tf_op jit(solution)/shard_map/ppermute | solution.py:791
  81.6 4.1 %collective-permute-start.8 = (f32[5,16,128]{2,1,0:T(8,128)}, f32[5,16,128]{2,1,0:T(8,128)S(1)}, u32[]{:S(2)}, u32[]{:S(2)}) collective-permute-start(f32[5,16,128]{2,1,0:T(8,128)} %get-tuple-element.46), channel_id=1, source_target_pairs={{0,19},{1,18},{2,17},{3,16},{16,3},{17,2},{18,1},{19,0},{4,23},{5,... | collective-permute-start | bytes 122888 | tf_op jit(solution)/shard_map/ppermute | solution.py:792
  89.8 3.0 %collective-permute-start.11 = (f32[5,16,128]{2,1,0:T(8,128)S(1)}, f32[5,16,128]{2,1,0:T(8,128)S(1)}, u32[]{:S(2)}, u32[]{:S(2)}) collective-permute-start(f32[5,16,128]{2,1,0:T(8,128)S(1)} %shard_map.152.refs_0_), channel_id=1, source_target_pairs={{0,4},{4,0},{8,12},{12,8},{1,5},{5,1},{9,13},{13,9},{2,6},{6,2},{1... | collective-permute-start | bytes 122888 | tf_op jit(solution)/shard_map/ppermute | solution.py:791
  96.3 1.9 %shard_map.153 = (bf16[512,2048]{1,0:T(8,128)(2,1)S(1)}, bf16[128,4096]{1,0:T(8,128)(2,1)S(1)}, f32[24,2048]{1,0:T(8,128)S(1)}, f32[24,4096]{1,0:T(8,128)S(1)}) custom-call(f32[10]{0:T(128)S(1)} %convert_element_type.4.flag.refs_1_, f32[16,24,128]{2,1,0:T(8,128)} %all-to-all-done.here_ref, f32[16,24,128]{2,1,0:T(8,128)S(1)} %collective-permute-done.13.a_ref, ...), custom_call_target="tpu_custom_call" | custom-call | flops 4194304 | bytes 2097152 | tf_op jit(solution)/shard_map/pallas_call | solution.py:602
  99.7 3.1 %shard_map.154 = (f32[5,24,128]{2,1,0:T(8,128)S(1)}, f32[1,24,128]{2,1,0:T(8,128)S(1)}, f32[5,24,128]{2,1,0:T(8,128)S(1)}) custom-call(f32[10]{0:T(128)S(1)} %convert_element_type.4.flag.refs_1_, f32[5,16,128]{2,1,0:T(8,128)S(1)} %shard_map.152.refs_0_, f32[5,16,128]{2,1,0:T(8,128)S(1)} %collective-permute-done.11.refs_1_, ...), custom_call_target="tpu_custom_call" | custom-call | flops 805306368 | bytes 4194304 | tf_op jit(solution)/shard_map/pallas_call | solution.py:758
  104.3 2.0 %collective-permute-start.17 = (f32[1,24,128]{2,1,0:T(8,128)S(1)}, f32[1,24,128]{2,1,0:T(8,128)S(1)}, u32[]{:S(2)}, u32[]{:S(2)}) collective-permute-start(f32[1,24,128]{2,1,0:T(8,128)S(1)} %get-tuple-element.55), channel_id=1, source_target_pairs={{0,2},{1,3},{2,0},{3,1},{4,6},{5,7},{6,4},{7,5},{8,10},{9,11},{10,... | collective-permute-start | bytes 36872 | tf_op jit(solution)/shard_map/ppermute | solution.py:791
  107.3 2.1 %collective-permute-done.17.refs_5_.refs_9_ = f32[1,24,128]{2,1,0:T(8,128)S(1)} collective-permute-done((f32[1,24,128]{2,1,0:T(8,128)S(1)}, f32[1,24,128]{2,1,0:T(8,128)S(1)}, u32[]{:S(2)}, u32[]{:S(2)}) %collective-permute-start.17) | collective-permute-done | bytes 12320 | tf_op jit(solution)/shard_map/ppermute | solution.py:791
  109.5 8.7 %shard_map.155 = (f32[5,24,128]{2,1,0:T(8,128)S(1)}, f32[5,24,128]{2,1,0:T(8,128)S(1)}, f32[5,24,128]{2,1,0:T(8,128)S(1)}, f32[1,24,128]{2,1,0:T(8,128)S(1)}) custom-call(f32[48]{0:T(128)S(1)} %copy-done.12, f32[10]{0:T(128)S(1)} %convert_element_type.4.flag.refs_1_, s32[2]{0:T(128)S(1)} %copy-done.13, ...), custom_call_target="tpu_custom_call" | custom-call | flops 314572800 | bytes 12582912 | tf_op jit(solution)/shard_map/pallas_call | solution.py:512
  119.7 2.4 %collective-permute-start.28 = (f32[1,24,128]{2,1,0:T(8,128)S(1)}, f32[1,24,128]{2,1,0:T(8,128)S(1)}, u32[]{:S(2)}, u32[]{:S(2)}) collective-permute-start(f32[1,24,128]{2,1,0:T(8,128)S(1)} %get-tuple-element.61), channel_id=1, source_target_pairs={{0,18},{1,19},{2,16},{3,17},{16,2},{17,3},{18,0},{19,1},{4,22},{5,... | collective-permute-start | bytes 36872 | tf_op jit(solution)/shard_map/ppermute | solution.py:792
  125.7 1.9 %collective-permute-start.25 = (f32[5,24,128]{2,1,0:T(8,128)S(1)}, f32[5,24,128]{2,1,0:T(8,128)S(1)}, u32[]{:S(2)}, u32[]{:S(2)}) collective-permute-start(f32[5,24,128]{2,1,0:T(8,128)S(1)} %get-tuple-element.60), channel_id=1, source_target_pairs={{0,3},{1,2},{2,1},{3,0},{4,7},{5,6},{6,5},{7,4},{8,11},{9,10},{10,... | collective-permute-start | bytes 184328 | tf_op jit(solution)/shard_map/ppermute | solution.py:791
  127.6 1.8 %collective-permute-start.26 = (f32[5,24,128]{2,1,0:T(8,128)S(1)}, f32[5,24,128]{2,1,0:T(8,128)S(1)}, u32[]{:S(2)}, u32[]{:S(2)}) collective-permute-start(f32[5,24,128]{2,1,0:T(8,128)S(1)} %get-tuple-element.60), channel_id=1, source_target_pairs={{0,19},{1,18},{2,17},{3,16},{16,3},{17,2},{18,1},{19,0},{4,23},{5,... | collective-permute-start | bytes 184328 | tf_op jit(solution)/shard_map/ppermute | solution.py:792
  129.4 2.7 %collective-permute-done.25.refs_5_ = f32[5,24,128]{2,1,0:T(8,128)S(1)} collective-permute-done((f32[5,24,128]{2,1,0:T(8,128)S(1)}, f32[5,24,128]{2,1,0:T(8,128)S(1)}, u32[]{:S(2)}, u32[]{:S(2)}) %collective-permute-start.25) | collective-permute-done | bytes 61472 | tf_op jit(solution)/shard_map/ppermute | solution.py:791
  132.2 3.0 %collective-permute-done.26.refs_6_ = f32[5,24,128]{2,1,0:T(8,128)S(1)} collective-permute-done((f32[5,24,128]{2,1,0:T(8,128)S(1)}, f32[5,24,128]{2,1,0:T(8,128)S(1)}, u32[]{:S(2)}, u32[]{:S(2)}) %collective-permute-start.26) | collective-permute-done | bytes 61472 | tf_op jit(solution)/shard_map/ppermute | solution.py:792
  135.2 3.5 %shard_map.156 = (f32[5,24,128]{2,1,0:T(8,128)S(1)}, f32[1,24,128]{2,1,0:T(8,128)S(1)}, f32[64,128]{1,0:T(8,128)}) custom-call(f32[10]{0:T(128)S(1)} %convert_element_type.4.flag.refs_1_, f32[5,24,128]{2,1,0:T(8,128)S(1)} %get-tuple-element.53.refs_0_, f32[5,24,128]{2,1,0:T(8,128)S(1)} %get-tuple-element.58.refs_1_, ...), custom_call_target="tpu_custom_call" | custom-call | flops 805306368 | bytes 4194304 | tf_op jit(solution)/shard_map/pallas_call | solution.py:758
  142.2 4.3 %collective-permute-done.31.refs_5_ = f32[1,24,128]{2,1,0:T(8,128)S(1)} collective-permute-done((f32[1,24,128]{2,1,0:T(8,128)S(1)}, f32[1,24,128]{2,1,0:T(8,128)S(1)}, u32[]{:S(2)}, u32[]{:S(2)}) %collective-permute-start.31) | collective-permute-done | bytes 12320 | tf_op jit(solution)/shard_map/ppermute | solution.py:791
  146.4 7.2 %shard_map.157 = (f32[4096,128]{1,0:T(8,128)}, f32[64,128]{1,0:T(8,128)}) custom-call(f32[48]{0:T(128)S(1)} %copy-done.12, f32[10]{0:T(128)S(1)} %convert_element_type.4.flag.refs_1_, s32[2]{0:T(128)S(1)} %copy-done.13, f32[5,24,128]{2,1,0:T(8,128)S(1)} %collective-permute-done.29.refs_3_, f32[5,24,128]{2,1,0:T(8,128)S(1)} %collective-permute-done.30.refs_4_, ...), custom_call_target="tpu_custom_call" | custom-call | flops 314572800 | bytes 12582912 | tf_op jit(solution)/shard_map/pallas_call | solution.py:512
  (108 shorter events, 43.4 us)
Async XLA Ops:
  2.3 51.8 %collective-permute-start.2 = (f32[4,1040,128]{2,1,0:T(8,128)S(1)}, f32[4,1040,128]{2,1,0:T(8,128)}, u32[]{:S(2)}, u32[]{:S(2)}) collective-permute-start(f32[4,1040,128]{2,1,0:T(8,128)S(1)} %pad_maximum_fusion.po.tpo.refs_8_.refs_15_.refs_14_.refs_21_), channel_id=1, source_target_pairs={{0,1},{1,2},{2,3},{4,5},{5,6},{6,7},{8,9},{9,10},{10,11},{12,13},{... | collective-permute-start | bytes 6389768 | tf_op jit(solution)/shard_map/ppermute | solution.py:777
  8.8 51.2 %collective-permute-start.3 = (f32[4,1040,128]{2,1,0:T(8,128)S(1)}, f32[4,1040,128]{2,1,0:T(8,128)}, u32[]{:S(2)}, u32[]{:S(2)}) collective-permute-start(f32[4,1040,128]{2,1,0:T(8,128)S(1)} %pad_maximum_fusion.po.tpo.refs_8_.refs_15_.refs_14_.refs_21_), channel_id=1, source_target_pairs={{1,0},{2,1},{3,2},{5,4},{6,5},{7,6},{9,8},{10,9},{11,10},{13,12},{... | collective-permute-start | bytes 6389768 | tf_op jit(solution)/shard_map/ppermute | solution.py:777
  13.1 8.2 %collective-permute-start = (f32[4,272,128]{2,1,0:T(8,128)}, f32[4,272,128]{2,1,0:T(8,128)S(1)}, u32[]{:S(2)}, u32[]{:S(2)}) collective-permute-start(f32[4,272,128]{2,1,0:T(8,128)} %get-tuple-element.36), channel_id=1, source_target_pairs={{0,4},{4,0},{8,12},{12,8},{1,5},{5,1},{9,13},{13,9},{2,6},{6,2},{1... | collective-permute-start | bytes 1671176 | tf_op jit(solution)/shard_map/ppermute | solution.py:791
  13.1 8.2 %collective-permute-start.1 = (f32[4,272,128]{2,1,0:T(8,128)}, f32[4,272,128]{2,1,0:T(8,128)S(1)}, u32[]{:S(2)}, u32[]{:S(2)}) collective-permute-start(f32[4,272,128]{2,1,0:T(8,128)} %get-tuple-element.36), channel_id=1, source_target_pairs={{4,8},{8,4},{5,9},{9,5},{6,10},{10,6},{7,11},{11,7},{20,24},{24,20... | collective-permute-start | bytes 1671176 | tf_op jit(solution)/shard_map/ppermute | solution.py:859
  30.2 36.7 %all-to-all-start = ((f32[16,24,128]{2,1,0:T(8,128)}), f32[16,24,128]{2,1,0:T(8,128)}, u32[]{:S(2)}, u32[]{:S(2)}) async-start(f32[16,24,128]{2,1,0:T(8,128)} %copy-done.6), calls=%async_computation | async-start | bytes 393216 | tf_op jit(solution)/shard_map/all_to_all | solution.py:902
  65.3 44.2 %collective-permute-start.20 = (f32[8,272,128]{2,1,0:T(8,128)}, f32[8,272,128]{2,1,0:T(8,128)S(1)}, u32[]{:S(2)}, u32[]{:S(2)}) collective-permute-start(f32[8,272,128]{2,1,0:T(8,128)} %get-tuple-element.57), channel_id=1, source_target_pairs={{0,4},{4,0},{8,12},{12,8},{1,5},{5,1},{9,13},{13,9},{2,6},{6,2},{1... | collective-permute-start | bytes 3342344 | tf_op jit(solution)/shard_map/ppermute | solution.py:791
  65.3 44.2 %collective-permute-start.21 = (f32[8,272,128]{2,1,0:T(8,128)}, f32[8,272,128]{2,1,0:T(8,128)}, u32[]{:S(2)}, u32[]{:S(2)}) collective-permute-start(f32[8,272,128]{2,1,0:T(8,128)} %get-tuple-element.57), channel_id=1, source_target_pairs={{4,8},{8,4},{5,9},{9,5},{6,10},{10,6},{7,11},{11,7},{20,24},{24,20... | collective-permute-start | bytes 3342344 | tf_op jit(solution)/shard_map/ppermute | solution.py:859
  67.0 13.9 %collective-permute-start.4 = (f32[5,16,128]{2,1,0:T(8,128)}, f32[5,16,128]{2,1,0:T(8,128)S(1)}, u32[]{:S(2)}, u32[]{:S(2)}) collective-permute-start(f32[5,16,128]{2,1,0:T(8,128)} %get-tuple-element.44.refs_0_), channel_id=1, source_target_pairs={{0,16},{1,17},{2,18},{3,19},{16,0},{17,1},{18,2},{19,3},{4,20},{5,... | collective-permute-start | bytes 122888 | tf_op jit(solution)/shard_map/ppermute | solution.py:792
  68.5 13.1 %collective-permute-start.5 = (f32[5,16,128]{2,1,0:T(8,128)}, f32[5,16,128]{2,1,0:T(8,128)S(1)}, u32[]{:S(2)}, u32[]{:S(2)}) collective-permute-start(f32[5,16,128]{2,1,0:T(8,128)} %get-tuple-element.45), channel_id=1, source_target_pairs={{0,1},{1,0},{2,3},{3,2},{4,5},{5,4},{6,7},{7,6},{8,9},{9,8},{10,11... | collective-permute-start | bytes 122888 | tf_op jit(solution)/shard_map/ppermute | solution.py:791
  79.5 6.1 %collective-permute-start.6 = (f32[5,16,128]{2,1,0:T(8,128)}, f32[5,16,128]{2,1,0:T(8,128)S(1)}, u32[]{:S(2)}, u32[]{:S(2)}) collective-permute-start(f32[5,16,128]{2,1,0:T(8,128)} %get-tuple-element.45), channel_id=1, source_target_pairs={{0,17},{1,16},{2,19},{3,18},{16,1},{17,0},{18,3},{19,2},{4,21},{5,... | collective-permute-start | bytes 122888 | tf_op jit(solution)/shard_map/ppermute | solution.py:792
  80.9 6.0 %collective-permute-start.7 = (f32[5,16,128]{2,1,0:T(8,128)}, f32[5,16,128]{2,1,0:T(8,128)S(1)}, u32[]{:S(2)}, u32[]{:S(2)}) collective-permute-start(f32[5,16,128]{2,1,0:T(8,128)} %get-tuple-element.46), channel_id=1, source_target_pairs={{0,3},{1,2},{2,1},{3,0},{4,7},{5,6},{6,5},{7,4},{8,11},{9,10},{10,... | collective-permute-start | bytes 122888 | tf_op jit(solution)/shard_map/ppermute | solution.py:791
  81.6 6.9 %collective-permute-start.8 = (f32[5,16,128]{2,1,0:T(8,128)}, f32[5,16,128]{2,1,0:T(8,128)S(1)}, u32[]{:S(2)}, u32[]{:S(2)}) collective-permute-start(f32[5,16,128]{2,1,0:T(8,128)} %get-tuple-element.46), channel_id=1, source_target_pairs={{0,19},{1,18},{2,17},{3,16},{16,3},{17,2},{18,1},{19,0},{4,23},{5,... | collective-permute-start | bytes 122888 | tf_op jit(solution)/shard_map/ppermute | solution.py:792
  85.7 17.2 %collective-permute-start.18 = (f32[4,272,128]{2,1,0:T(8,128)}, f32[4,272,128]{2,1,0:T(8,128)S(1)}, u32[]{:S(2)}, u32[]{:S(2)}) collective-permute-start(f32[4,272,128]{2,1,0:T(8,128)} %copy-done.14), channel_id=1, source_target_pairs={{0,4},{4,0},{8,12},{12,8},{1,5},{5,1},{9,13},{13,9},{2,6},{6,2},{1... | collective-permute-start | bytes 1671176 | tf_op jit(solution)/shard_map/ppermute | solution.py:791
  86.9 17.5 %collective-permute-start.19 = (f32[4,272,128]{2,1,0:T(8,128)}, f32[4,272,128]{2,1,0:T(8,128)S(1)}, u32[]{:S(2)}, u32[]{:S(2)}) collective-permute-start(f32[4,272,128]{2,1,0:T(8,128)} %copy-done.14), channel_id=1, source_target_pairs={{4,8},{8,4},{5,9},{9,5},{6,10},{10,6},{7,11},{11,7},{20,24},{24,20... | collective-permute-start | bytes 1671176 | tf_op jit(solution)/shard_map/ppermute | solution.py:859
  102.8 6.7 %collective-permute-start.15 = (f32[5,24,128]{2,1,0:T(8,128)S(1)}, f32[5,24,128]{2,1,0:T(8,128)S(1)}, u32[]{:S(2)}, u32[]{:S(2)}) collective-permute-start(f32[5,24,128]{2,1,0:T(8,128)S(1)} %get-tuple-element.54.refs_6_.refs_10_), channel_id=1, source_target_pairs={{0,1},{1,0},{2,3},{3,2},{4,5},{5,4},{6,7},{7,6},{8,9},{9,8},{10,11... | collective-permute-start | bytes 184328 | tf_op jit(solution)/shard_map/ppermute | solution.py:791
  102.9 6.6 %collective-permute-start.16 = (f32[5,24,128]{2,1,0:T(8,128)S(1)}, f32[5,24,128]{2,1,0:T(8,128)S(1)}, u32[]{:S(2)}, u32[]{:S(2)}) collective-permute-start(f32[5,24,128]{2,1,0:T(8,128)S(1)} %get-tuple-element.54.refs_6_.refs_10_), channel_id=1, source_target_pairs={{0,3},{1,2},{2,1},{3,0},{4,7},{5,6},{6,5},{7,4},{8,11},{9,10},{10,... | collective-permute-start | bytes 184328 | tf_op jit(solution)/shard_map/ppermute | solution.py:791
  118.2 7.5 %collective-permute-start.27 = (f32[1,24,128]{2,1,0:T(8,128)S(1)}, f32[1,24,128]{2,1,0:T(8,128)S(1)}, u32[]{:S(2)}, u32[]{:S(2)}) collective-permute-start(f32[1,24,128]{2,1,0:T(8,128)S(1)} %get-tuple-element.61), channel_id=1, source_target_pairs={{0,2},{1,3},{2,0},{3,1},{4,6},{5,7},{6,4},{7,5},{8,10},{9,11},{10,... | collective-permute-start | bytes 36872 | tf_op jit(solution)/shard_map/ppermute | solution.py:791
  119.7 7.8 %collective-permute-start.28 = (f32[1,24,128]{2,1,0:T(8,128)S(1)}, f32[1,24,128]{2,1,0:T(8,128)S(1)}, u32[]{:S(2)}, u32[]{:S(2)}) collective-permute-start(f32[1,24,128]{2,1,0:T(8,128)S(1)} %get-tuple-element.61), channel_id=1, source_target_pairs={{0,18},{1,19},{2,16},{3,17},{16,2},{17,3},{18,0},{19,1},{4,22},{5,... | collective-permute-start | bytes 36872 | tf_op jit(solution)/shard_map/ppermute | solution.py:792
  122.2 7.2 %collective-permute-start.23 = (f32[5,24,128]{2,1,0:T(8,128)S(1)}, f32[5,24,128]{2,1,0:T(8,128)S(1)}, u32[]{:S(2)}, u32[]{:S(2)}) collective-permute-start(f32[5,24,128]{2,1,0:T(8,128)S(1)} %get-tuple-element.59), channel_id=1, source_target_pairs={{0,1},{1,0},{2,3},{3,2},{4,5},{5,4},{6,7},{7,6},{8,9},{9,8},{10,11... | collective-permute-start | bytes 184328 | tf_op jit(solution)/shard_map/ppermute | solution.py:791
  122.6 6.8 %collective-permute-start.24 = (f32[5,24,128]{2,1,0:T(8,128)S(1)}, f32[5,24,128]{2,1,0:T(8,128)S(1)}, u32[]{:S(2)}, u32[]{:S(2)}) collective-permute-start(f32[5,24,128]{2,1,0:T(8,128)S(1)} %get-tuple-element.59), channel_id=1, source_target_pairs={{0,17},{1,16},{2,19},{3,18},{16,1},{17,0},{18,3},{19,2},{4,21},{5,... | collective-permute-start | bytes 184328 | tf_op jit(solution)/shard_map/ppermute | solution.py:792
  125.7 6.5 %collective-permute-start.25 = (f32[5,24,128]{2,1,0:T(8,128)S(1)}, f32[5,24,128]{2,1,0:T(8,128)S(1)}, u32[]{:S(2)}, u32[]{:S(2)}) collective-permute-start(f32[5,24,128]{2,1,0:T(8,128)S(1)} %get-tuple-element.60), channel_id=1, source_target_pairs={{0,3},{1,2},{2,1},{3,0},{4,7},{5,6},{6,5},{7,4},{8,11},{9,10},{10,... | collective-permute-start | bytes 184328 | tf_op jit(solution)/shard_map/ppermute | solution.py:791
  127.6 7.6 %collective-permute-start.26 = (f32[5,24,128]{2,1,0:T(8,128)S(1)}, f32[5,24,128]{2,1,0:T(8,128)S(1)}, u32[]{:S(2)}, u32[]{:S(2)}) collective-permute-start(f32[5,24,128]{2,1,0:T(8,128)S(1)} %get-tuple-element.60), channel_id=1, source_target_pairs={{0,19},{1,18},{2,17},{3,16},{16,3},{17,2},{18,1},{19,0},{4,23},{5,... | collective-permute-start | bytes 184328 | tf_op jit(solution)/shard_map/ppermute | solution.py:792
  138.7 7.8 %collective-permute-start.29 = (f32[5,24,128]{2,1,0:T(8,128)S(1)}, f32[5,24,128]{2,1,0:T(8,128)S(1)}, u32[]{:S(2)}, u32[]{:S(2)}) collective-permute-start(f32[5,24,128]{2,1,0:T(8,128)S(1)} %get-tuple-element.62.refs_6_), channel_id=1, source_target_pairs={{0,1},{1,0},{2,3},{3,2},{4,5},{5,4},{6,7},{7,6},{8,9},{9,8},{10,11... | collective-permute-start | bytes 184328 | tf_op jit(solution)/shard_map/ppermute | solution.py:791
  138.7 7.8 %collective-permute-start.30 = (f32[5,24,128]{2,1,0:T(8,128)S(1)}, f32[5,24,128]{2,1,0:T(8,128)S(1)}, u32[]{:S(2)}, u32[]{:S(2)}) collective-permute-start(f32[5,24,128]{2,1,0:T(8,128)S(1)} %get-tuple-element.62.refs_6_), channel_id=1, source_target_pairs={{0,3},{1,2},{2,1},{3,0},{4,7},{5,6},{6,5},{7,4},{8,11},{9,10},{10,... | collective-permute-start | bytes 184328 | tf_op jit(solution)/shard_map/ppermute | solution.py:791
  (31 other events, 186.4 us)
